TPU v7x, 128 devices: a whole 4x4x4 slice. The times are simulated.
128 devices in a mesh: tensor: 8 (over y_hi, x), context: 16 (over z, y_lo, core).
Axes of the slice: x: 4, y: 4 (y_hi: 2, y_lo: 2; y = y_hi * 2 + y_lo), z: 4, core: 2. Of those that a mesh axis runs over, the one named last changes fastest.
Arguments:
- tokens: bfloat16 [16, 1024, 4096], P('context', 'tensor'), may hold values from -6 to 6
- norm_gain: float32 [4096], replicated, may hold values from 0.25 to 1.75
- q_weight: bfloat16 [4096, 2048], P(None, 'tensor')
- k_weight: bfloat16 [4096, 1024], P(None, 'tensor')
- v_weight: bfloat16 [4096, 1024], P(None, 'tensor'), may hold values from -0.75 to 0.75
- o_weight: bfloat16 [2048, 4096], P('tensor'), may hold values from -0.125 to 0.125
- doc_lengths: int32 [16], replicated, may hold values from 1 to 4096, 16384 in all
- span_order: int32 [32], replicated, may hold values from 0 to 31, each once
Outputs:
- layer_out: bfloat16 [16, 1024, 4096], P('context', 'tensor')
Inputs may be any that keep to these rules, and one draw needn't show every extreme that they name: `doc_lengths`: documents fill the sequence in order; the longest has exactly 4096 tokens. `span_order`: each value appears once.
All inputs are finite; a program needn't handle non-finite values.
Results may differ from a plain program's by a relative error of at most 0.019.
Values may be sent and summed in bfloat16 or wider, within the bound.
A program may use at most 320 MiB of HBM per device.

v0:
```python
import math

import jax
import jax.numpy as jnp
from jax import lax
from jax.sharding import PartitionSpec as P

HEAD_DIM = 128


rope_theta = 500000.0
epsilon = 1e-05
masked_score = -1e30


def positions(rows, span_order, span_rows):
    slot_ids = jnp.arange(span_order.shape[0], dtype=jnp.int32)
    matches = (rows // span_rows)[:, None] == slot_ids[None, :]
    picked = jnp.sum(jnp.where(matches, span_order[None, :], 0), axis=1)
    return picked * span_rows + rows % span_rows


def documents(places, doc_lengths):
    doc_ends = jnp.cumsum(doc_lengths)
    return jnp.sum((doc_ends[None, :] <= places[:, None]).astype(jnp.int32), axis=1)


def rotary(values, places):
    head_dim = values.shape[-1]
    half_dim = head_dim // 2
    frequency = rope_theta ** (-(2.0 / head_dim) * jnp.arange(half_dim, dtype=jnp.float32))
    angles = places.astype(jnp.float32)[:, None] * frequency[None, :]
    cosine = jnp.cos(angles)[:, None, :]
    sine_part = jnp.sin(angles)[:, None, :]
    first_half = values[..., :half_dim]
    second = values[..., half_dim:]
    return jnp.concatenate(
        [first_half * cosine - second * sine_part, second * cosine + first_half * sine_part],
        axis=-1,
    )


def per_device(tokens, norm_gain, q_weight, k_weight, v_weight, o_weight, doc_lengths, span_order):
    local_rows = tokens.shape[1]
    tok_dev = local_rows * lax.axis_size("tensor")
    model_width = tokens.shape[2]
    head_dim = HEAD_DIM
    q_cols = q_weight.shape[1]
    kv_cols = k_weight.shape[1]
    q_heads = q_cols // head_dim
    kv_local = kv_cols // head_dim
    group_size = q_heads // kv_local
    span_rows = tok_dev // 2
    base_row = lax.axis_index("context") * tok_dev
    score_scale = 1.0 / math.sqrt(head_dim)
    rows_float = tokens.astype(jnp.float32)
    normed = (
        rows_float
        * lax.rsqrt(jnp.mean(rows_float * rows_float, axis=-1, keepdims=True) + epsilon)
        * norm_gain
    ).astype(jnp.bfloat16)
    portion = lax.all_gather(normed, "tensor", axis=1, tiled=True)
    row_count = portion.shape[1]
    flat_rows = portion.reshape(row_count, model_width)
    places = positions(base_row + jnp.arange(row_count, dtype=jnp.int32), span_order, span_rows)
    query_rows = jnp.dot(flat_rows, q_weight, preferred_element_type=jnp.float32).reshape(
        row_count, q_heads, head_dim
    )
    key_rows = jnp.dot(flat_rows, k_weight, preferred_element_type=jnp.float32).reshape(
        row_count, kv_local, head_dim
    )
    value_rows = jnp.dot(flat_rows, v_weight, preferred_element_type=jnp.float32).astype(
        jnp.bfloat16
    )
    query_rows = rotary(query_rows, places).reshape(row_count, q_cols).astype(jnp.bfloat16)
    key_rows = rotary(key_rows, places).reshape(row_count, kv_cols).astype(jnp.bfloat16)
    projected = jnp.concatenate([query_rows, key_rows, value_rows], axis=1)[None][0]
    query_places = positions(base_row + jnp.arange(tok_dev, dtype=jnp.int32), span_order, span_rows)
    query_docs = documents(query_places, doc_lengths)
    queries = projected[:, :q_cols].reshape(tok_dev, kv_local, group_size, head_dim)
    kv_pair = jnp.stack([projected[:, q_cols : q_cols + kv_cols], projected[:, q_cols + kv_cols :]])

    def attend(running, portion, offset):
        row_count = portion.shape[1]
        key_places = positions(
            offset + jnp.arange(row_count, dtype=jnp.int32), span_order, span_rows
        )
        key_docs = documents(key_places, doc_lengths)
        visible = (key_places[None, :] <= query_places[:, None]) & (
            key_docs[None, :] == query_docs[:, None]
        )
        running_max, row_sum, weighted = running
        key_rows = portion[0].reshape(row_count, kv_local, head_dim)
        value_rows = portion[1].reshape(row_count, kv_local, head_dim)
        scores = (
            jnp.einsum("qkgd,skd->kgqs", queries, key_rows, preferred_element_type=jnp.float32)
            * score_scale
        )
        limited = jnp.where(visible, scores, masked_score)
        new_max = jnp.maximum(running_max, jnp.max(limited, axis=-1))
        factor = jnp.exp(running_max - new_max)
        weights = jnp.where(visible, jnp.exp(scores - new_max[..., None]), 0.0)
        row_sum = row_sum * factor + jnp.sum(weights, axis=-1)
        weighted = weighted * factor.transpose(2, 0, 1)[..., None] + jnp.einsum(
            "kgqs,skd->qkgd",
            weights.astype(jnp.bfloat16),
            value_rows,
            preferred_element_type=jnp.float32,
        )
        return (new_max, row_sum, weighted)

    initial = (
        jnp.full((kv_local, group_size, tok_dev), masked_score, jnp.float32),
        jnp.zeros((kv_local, group_size, tok_dev), jnp.float32),
        jnp.zeros((tok_dev, kv_local, group_size, head_dim), jnp.float32),
    )
    gathered = lax.all_gather(kv_pair, "context", axis=1, tiled=True)

    def visit_block(block_index, carried):
        offset = block_index * tok_dev
        portion = lax.dynamic_slice_in_dim(gathered, offset, tok_dev, 1)
        return attend(carried, portion, offset)

    running_max, row_sum, weighted = lax.fori_loop(
        0, lax.axis_size("context"), visit_block, initial
    )
    attended = (
        (weighted / row_sum.transpose(2, 0, 1)[..., None])
        .reshape(tok_dev, q_cols)
        .astype(jnp.bfloat16)
    )
    mixed_rows = lax.psum_scatter(
        jnp.dot(attended, o_weight, preferred_element_type=jnp.float32).astype(jnp.bfloat16),
        "tensor",
        scatter_dimension=0,
        tiled=True,
    )
    return mixed_rows.reshape(tokens.shape)


def solution(mesh):
    in_specs = (
        P("context", "tensor", None),
        P(),
        P(None, "tensor"),
        P(None, "tensor"),
        P(None, "tensor"),
        P("tensor", None),
        P(),
        P(),
    )
    out_specs = P("context", "tensor", None)
    return jax.shard_map(
        per_device, mesh=mesh, in_specs=in_specs, out_specs=out_specs, check_vma=False
    )
```

profile of v0, /device:TPU:8, one launch (start us, length us, event | category | flops | bytes accessed | tf_op | source)
XLA Modules:
  0.0 583.9 jit_solution(13166002887668406212)
XLA Ops:
  11.7 109.5 %all-gather.3.cloned.1.call-done = bf16[1,1024,4096]{2,1,0:T(8,128)(2,1)} async-done(((bf16[1,128,4096]{2,1,0:T(8,128)(2,1)}), bf16[1,1024,4096]{2,1,0:T(8,128)(2,1)}) %all-gather.3.cloned.1.call-update) | async-done | bytes 8388624 | tf_op jit(solution)/shard_map/all_gather | solution.py:62
  121.2 6.7 %fusion.37 = f32[1024,1,128]{0,2,1:T(8,128)S(1)} fusion(bf16[4096,128]{1,0:T(8,128)(2,1)} %param.13, bf16[1,1024,4096]{2,1,0:T(8,128)(2,1)} %all-gather.3.cloned.1.call-done), kind=kOutput, calls=%fused_computation.56 | convolution fusion | flops 1073741824 | bytes 9961472 | tf_op jit(solution)/shard_map/dot_general | solution.py:69
  138.5 6.7 %fusion.28 = f32[1024,2,128]{0,2,1:T(8,128)S(1)} fusion(bf16[2,128,4096]{2,1,0:T(8,128)(2,1)} %bitcast.129, bf16[1,1024,4096]{2,1,0:T(8,128)(2,1)} %all-gather.3.cloned.1.call-done), kind=kOutput, calls=%fused_computation.44 | convolution fusion | flops 2147483648 | bytes 11534336 | tf_op jit(solution)/shard_map/dot_general | solution.py:66
  146.4 37.5 %all-gather.5.cloned.1.call-done = bf16[2,16384,128]{1,2,0:T(8,128)(2,1)} async-done(((bf16[2,1024,128]{1,2,0:T(8,128)(2,1)}), bf16[2,16384,128]{1,2,0:T(8,128)(2,1)}) %all-gather.5.cloned.1.call-update) | async-done | bytes 8388624 | tf_op jit(solution)/shard_map/all_gather | solution.py:117
  183.9 270.9 %while.20 = (s32[]{:T(128)}, f32[1,2,1024]{2,1,0:T(2,128)S(1)}, f32[1,2,1024]{2,1,0:T(2,128)S(1)}, f32[1024,1,2,128]{0,3,2,1:T(8,128)}, s32[32]{0:T(128)S(1)}, /...) while((s32[]{:T(128)}, f32[1,2,1024]{2,1,0:T(2,128)S(1)}, ...), condition=%wide.region_9.10_spmd.clone, body=%wide.region_4.9_spmd.clone.sunk | while | flops 1100931072 | bytes 66236864 | solution.py:124
  191.6 7.0 %fusion.80 = f32[1024,1,2,128]{0,3,2,1:T(8,128)} fusion(f32[1024,1024,2]{1,0,2:T(8,128)} %get-tuple-element.407, f32[2,1024]{1,0:T(2,128)S(1)} %bitcast.126, pred[1024,1024]{0,1:T(8,128)(4,1)S(1)} %compare_and_fusion.2, f32[1024,1,2,128]{0,3,2,1:T(8,128)} %get-tuple-element.427, f32[1024,2]{0,1:T(2,128)S(1)} %get-tuple-element.408, ...), kind=kOutput, calls=%fused_computation.12.clone.1 | convolution fusion | flops 546045952 | bytes 11812873 | tf_op jit(solution)/shard_map/while/body/eval_jaxpr/kgqs,skd->qkgd/dot_general | solution.py:104
  202.0 6.3 %fusion.77 = (f32[2,1024]{1,0:T(2,128)S(1)}, f32[1024,1024,2]{1,0,2:T(8,128)}) fusion(pred[1024,1024]{0,1:T(8,128)(4,1)S(1)} %compare_and_fusion.2, bf16[1024,1,2,128]{3,0,2,1:T(8,128)(2,1)} %get-tuple-element.448, bf16[2,16384,128]{1,2,0:T(8,128)(2,1)} %get-tuple-element.447, s32[]{:T(128)S(6)} %select_n.164), kind=kOutput, calls=%fused_computation.2.clone.1 | convolution fusion | flops 543160320 | bytes 10231812 | tf_op jit(solution)/shard_map/while/body/eval_jaxpr/qkgd,skd->kgqs/dot_general | solution.py:96
  208.3 7.2 %fusion.80 = f32[1024,1,2,128]{0,3,2,1:T(8,128)} fusion(f32[1024,1024,2]{1,0,2:T(8,128)} %get-tuple-element.407, f32[2,1024]{1,0:T(2,128)S(1)} %bitcast.126, pred[1024,1024]{0,1:T(8,128)(4,1)S(1)} %compare_and_fusion.2, f32[1024,1,2,128]{0,3,2,1:T(8,128)} %get-tuple-element.427, f32[1024,2]{0,1:T(2,128)S(1)} %get-tuple-element.408, ...), kind=kOutput, calls=%fused_computation.12.clone.1 | convolution fusion | flops 546045952 | bytes 11812873 | tf_op jit(solution)/shard_map/while/body/eval_jaxpr/kgqs,skd->qkgd/dot_general | solution.py:104
  225.3 7.2 %fusion.80 = f32[1024,1,2,128]{0,3,2,1:T(8,128)} fusion(f32[1024,1024,2]{1,0,2:T(8,128)} %get-tuple-element.407, f32[2,1024]{1,0:T(2,128)S(1)} %bitcast.126, pred[1024,1024]{0,1:T(8,128)(4,1)S(1)} %compare_and_fusion.2, f32[1024,1,2,128]{0,3,2,1:T(8,128)} %get-tuple-element.427, f32[1024,2]{0,1:T(2,128)S(1)} %get-tuple-element.408, ...), kind=kOutput, calls=%fused_computation.12.clone.1 | convolution fusion | flops 546045952 | bytes 11812873 | tf_op jit(solution)/shard_map/while/body/eval_jaxpr/kgqs,skd->qkgd/dot_general | solution.py:104
  235.9 6.3 %fusion.77 = (f32[2,1024]{1,0:T(2,128)S(1)}, f32[1024,1024,2]{1,0,2:T(8,128)}) fusion(pred[1024,1024]{0,1:T(8,128)(4,1)S(1)} %compare_and_fusion.2, bf16[1024,1,2,128]{3,0,2,1:T(8,128)(2,1)} %get-tuple-element.448, bf16[2,16384,128]{1,2,0:T(8,128)(2,1)} %get-tuple-element.447, s32[]{:T(128)S(6)} %select_n.164), kind=kOutput, calls=%fused_computation.2.clone.1 | convolution fusion | flops 543160320 | bytes 10231812 | tf_op jit(solution)/shard_map/while/body/eval_jaxpr/qkgd,skd->kgqs/dot_general | solution.py:96
  242.2 7.2 %fusion.80 = f32[1024,1,2,128]{0,3,2,1:T(8,128)} fusion(f32[1024,1024,2]{1,0,2:T(8,128)} %get-tuple-element.407, f32[2,1024]{1,0:T(2,128)S(1)} %bitcast.126, pred[1024,1024]{0,1:T(8,128)(4,1)S(1)} %compare_and_fusion.2, f32[1024,1,2,128]{0,3,2,1:T(8,128)} %get-tuple-element.427, f32[1024,2]{0,1:T(2,128)S(1)} %get-tuple-element.408, ...), kind=kOutput, calls=%fused_computation.12.clone.1 | convolution fusion | flops 546045952 | bytes 11812873 | tf_op jit(solution)/shard_map/while/body/eval_jaxpr/kgqs,skd->qkgd/dot_general | solution.py:104
  259.2 7.2 %fusion.80 = f32[1024,1,2,128]{0,3,2,1:T(8,128)} fusion(f32[1024,1024,2]{1,0,2:T(8,128)} %get-tuple-element.407, f32[2,1024]{1,0:T(2,128)S(1)} %bitcast.126, pred[1024,1024]{0,1:T(8,128)(4,1)S(1)} %compare_and_fusion.2, f32[1024,1,2,128]{0,3,2,1:T(8,128)} %get-tuple-element.427, f32[1024,2]{0,1:T(2,128)S(1)} %get-tuple-element.408, ...), kind=kOutput, calls=%fused_computation.12.clone.1 | convolution fusion | flops 546045952 | bytes 11812873 | tf_op jit(solution)/shard_map/while/body/eval_jaxpr/kgqs,skd->qkgd/dot_general | solution.py:104
  276.1 7.2 %fusion.80 = f32[1024,1,2,128]{0,3,2,1:T(8,128)} fusion(f32[1024,1024,2]{1,0,2:T(8,128)} %get-tuple-element.407, f32[2,1024]{1,0:T(2,128)S(1)} %bitcast.126, pred[1024,1024]{0,1:T(8,128)(4,1)S(1)} %compare_and_fusion.2, f32[1024,1,2,128]{0,3,2,1:T(8,128)} %get-tuple-element.427, f32[1024,2]{0,1:T(2,128)S(1)} %get-tuple-element.408, ...), kind=kOutput, calls=%fused_computation.12.clone.1 | convolution fusion | flops 546045952 | bytes 11812873 | tf_op jit(solution)/shard_map/while/body/eval_jaxpr/kgqs,skd->qkgd/dot_general | solution.py:104
  293.1 7.2 %fusion.80 = f32[1024,1,2,128]{0,3,2,1:T(8,128)} fusion(f32[1024,1024,2]{1,0,2:T(8,128)} %get-tuple-element.407, f32[2,1024]{1,0:T(2,128)S(1)} %bitcast.126, pred[1024,1024]{0,1:T(8,128)(4,1)S(1)} %compare_and_fusion.2, f32[1024,1,2,128]{0,3,2,1:T(8,128)} %get-tuple-element.427, f32[1024,2]{0,1:T(2,128)S(1)} %get-tuple-element.408, ...), kind=kOutput, calls=%fused_computation.12.clone.1 | convolution fusion | flops 546045952 | bytes 11812873 | tf_op jit(solution)/shard_map/while/body/eval_jaxpr/kgqs,skd->qkgd/dot_general | solution.py:104
  310.0 7.2 %fusion.80 = f32[1024,1,2,128]{0,3,2,1:T(8,128)} fusion(f32[1024,1024,2]{1,0,2:T(8,128)} %get-tuple-element.407, f32[2,1024]{1,0:T(2,128)S(1)} %bitcast.126, pred[1024,1024]{0,1:T(8,128)(4,1)S(1)} %compare_and_fusion.2, f32[1024,1,2,128]{0,3,2,1:T(8,128)} %get-tuple-element.427, f32[1024,2]{0,1:T(2,128)S(1)} %get-tuple-element.408, ...), kind=kOutput, calls=%fused_computation.12.clone.1 | convolution fusion | flops 546045952 | bytes 11812873 | tf_op jit(solution)/shard_map/while/body/eval_jaxpr/kgqs,skd->qkgd/dot_general | solution.py:104
  327.0 7.2 %fusion.80 = f32[1024,1,2,128]{0,3,2,1:T(8,128)} fusion(f32[1024,1024,2]{1,0,2:T(8,128)} %get-tuple-element.407, f32[2,1024]{1,0:T(2,128)S(1)} %bitcast.126, pred[1024,1024]{0,1:T(8,128)(4,1)S(1)} %compare_and_fusion.2, f32[1024,1,2,128]{0,3,2,1:T(8,128)} %get-tuple-element.427, f32[1024,2]{0,1:T(2,128)S(1)} %get-tuple-element.408, ...), kind=kOutput, calls=%fused_computation.12.clone.1 | convolution fusion | flops 546045952 | bytes 11812873 | tf_op jit(solution)/shard_map/while/body/eval_jaxpr/kgqs,skd->qkgd/dot_general | solution.py:104
  343.9 7.2 %fusion.80 = f32[1024,1,2,128]{0,3,2,1:T(8,128)} fusion(f32[1024,1024,2]{1,0,2:T(8,128)} %get-tuple-element.407, f32[2,1024]{1,0:T(2,128)S(1)} %bitcast.126, pred[1024,1024]{0,1:T(8,128)(4,1)S(1)} %compare_and_fusion.2, f32[1024,1,2,128]{0,3,2,1:T(8,128)} %get-tuple-element.427, f32[1024,2]{0,1:T(2,128)S(1)} %get-tuple-element.408, ...), kind=kOutput, calls=%fused_computation.12.clone.1 | convolution fusion | flops 546045952 | bytes 11812873 | tf_op jit(solution)/shard_map/while/body/eval_jaxpr/kgqs,skd->qkgd/dot_general | solution.py:104
  360.9 7.2 %fusion.80 = f32[1024,1,2,128]{0,3,2,1:T(8,128)} fusion(f32[1024,1024,2]{1,0,2:T(8,128)} %get-tuple-element.407, f32[2,1024]{1,0:T(2,128)S(1)} %bitcast.126, pred[1024,1024]{0,1:T(8,128)(4,1)S(1)} %compare_and_fusion.2, f32[1024,1,2,128]{0,3,2,1:T(8,128)} %get-tuple-element.427, f32[1024,2]{0,1:T(2,128)S(1)} %get-tuple-element.408, ...), kind=kOutput, calls=%fused_computation.12.clone.1 | convolution fusion | flops 546045952 | bytes 11812873 | tf_op jit(solution)/shard_map/while/body/eval_jaxpr/kgqs,skd->qkgd/dot_general | solution.py:104
  377.8 7.2 %fusion.80 = f32[1024,1,2,128]{0,3,2,1:T(8,128)} fusion(f32[1024,1024,2]{1,0,2:T(8,128)} %get-tuple-element.407, f32[2,1024]{1,0:T(2,128)S(1)} %bitcast.126, pred[1024,1024]{0,1:T(8,128)(4,1)S(1)} %compare_and_fusion.2, f32[1024,1,2,128]{0,3,2,1:T(8,128)} %get-tuple-element.427, f32[1024,2]{0,1:T(2,128)S(1)} %get-tuple-element.408, ...), kind=kOutput, calls=%fused_computation.12.clone.1 | convolution fusion | flops 546045952 | bytes 11812873 | tf_op jit(solution)/shard_map/while/body/eval_jaxpr/kgqs,skd->qkgd/dot_general | solution.py:104
  394.8 7.2 %fusion.80 = f32[1024,1,2,128]{0,3,2,1:T(8,128)} fusion(f32[1024,1024,2]{1,0,2:T(8,128)} %get-tuple-element.407, f32[2,1024]{1,0:T(2,128)S(1)} %bitcast.126, pred[1024,1024]{0,1:T(8,128)(4,1)S(1)} %compare_and_fusion.2, f32[1024,1,2,128]{0,3,2,1:T(8,128)} %get-tuple-element.427, f32[1024,2]{0,1:T(2,128)S(1)} %get-tuple-element.408, ...), kind=kOutput, calls=%fused_computation.12.clone.1 | convolution fusion | flops 546045952 | bytes 11812873 | tf_op jit(solution)/shard_map/while/body/eval_jaxpr/kgqs,skd->qkgd/dot_general | solution.py:104
  411.7 7.2 %fusion.80 = f32[1024,1,2,128]{0,3,2,1:T(8,128)} fusion(f32[1024,1024,2]{1,0,2:T(8,128)} %get-tuple-element.407, f32[2,1024]{1,0:T(2,128)S(1)} %bitcast.126, pred[1024,1024]{0,1:T(8,128)(4,1)S(1)} %compare_and_fusion.2, f32[1024,1,2,128]{0,3,2,1:T(8,128)} %get-tuple-element.427, f32[1024,2]{0,1:T(2,128)S(1)} %get-tuple-element.408, ...), kind=kOutput, calls=%fused_computation.12.clone.1 | convolution fusion | flops 546045952 | bytes 11812873 | tf_op jit(solution)/shard_map/while/body/eval_jaxpr/kgqs,skd->qkgd/dot_general | solution.py:104
  428.7 7.2 %fusion.80 = f32[1024,1,2,128]{0,3,2,1:T(8,128)} fusion(f32[1024,1024,2]{1,0,2:T(8,128)} %get-tuple-element.407, f32[2,1024]{1,0:T(2,128)S(1)} %bitcast.126, pred[1024,1024]{0,1:T(8,128)(4,1)S(1)} %compare_and_fusion.2, f32[1024,1,2,128]{0,3,2,1:T(8,128)} %get-tuple-element.427, f32[1024,2]{0,1:T(2,128)S(1)} %get-tuple-element.408, ...), kind=kOutput, calls=%fused_computation.12.clone.1 | convolution fusion | flops 546045952 | bytes 11812873 | tf_op jit(solution)/shard_map/while/body/eval_jaxpr/kgqs,skd->qkgd/dot_general | solution.py:104
  445.6 7.2 %fusion.80 = f32[1024,1,2,128]{0,3,2,1:T(8,128)} fusion(f32[1024,1024,2]{1,0,2:T(8,128)} %get-tuple-element.407, f32[2,1024]{1,0:T(2,128)S(1)} %bitcast.126, pred[1024,1024]{0,1:T(8,128)(4,1)S(1)} %compare_and_fusion.2, f32[1024,1,2,128]{0,3,2,1:T(8,128)} %get-tuple-element.427, f32[1024,2]{0,1:T(2,128)S(1)} %get-tuple-element.408, ...), kind=kOutput, calls=%fused_computation.12.clone.1 | convolution fusion | flops 546045952 | bytes 11812873 | tf_op jit(solution)/shard_map/while/body/eval_jaxpr/kgqs,skd->qkgd/dot_general | solution.py:104
  461.8 115.6 %reduce-scatter.2.cloned.1.call-done = bf16[128,4096]{1,0:T(8,128)(2,1)} async-done(((bf16[1024,4096]{1,0:T(8,128)(2,1)}), bf16[128,4096]{1,0:T(8,128)(2,1)}) %reduce-scatter.2.cloned.1.call-update) | async-done | bytes 1048592 | tf_op jit(solution)/shard_map/reduce_scatter | solution.py:132
  (229 shorter events, 166.1 us)
Async XLA Ops:
  6.5 449.6 %copy-start = (bf16[256,4096]{1,0:T(8,128)(2,1)S(1)}, bf16[256,4096]{1,0:T(8,128)(2,1)}, u32[]{:S(2)}) copy-start(bf16[256,4096]{1,0:T(8,128)(2,1)} %param.15) | copy-start | bytes 6291460
  6.5 114.6 %all-gather.3.cloned.1.call-start = ((), (), s32[]{:S(2)}) async-start(), calls=%async_computation.1 | async-start | bytes 9437184 | tf_op jit(solution)/shard_map/all_gather | solution.py:62
  10.7 118.3 %copy-start.3 = (bf16[4096,128]{1,0:T(8,128)(2,1)S(1)}, bf16[4096,128]{1,0:T(8,128)(2,1)}, u32[]{:S(2)}) copy-start(bf16[4096,128]{1,0:T(8,128)(2,1)} %param.14) | copy-start | bytes 3145732
  10.8 173.1 %all-gather.5.cloned.1.call-start = ((), (), s32[]{:S(2)}) async-start(), calls=%async_computation.2 | async-start | bytes 8912896 | tf_op jit(solution)/shard_map/all_gather | solution.py:117
  121.2 7.9 %copy-start.2 = (bf16[1,1024,4096]{2,1,0:T(8,128)(2,1)S(1)}, bf16[1,1024,4096]{2,1,0:T(8,128)(2,1)}, u32[]{:S(2)}) copy-start(bf16[1,1024,4096]{2,1,0:T(8,128)(2,1)} %all-gather.3.cloned.1.call-done) | copy-start | bytes 25165828
  129.1 8.1 %copy-start.5 = (s32[16]{0:T(128)S(1)}, s32[16]{0:T(128)}, u32[]{:S(2)}) copy-start(s32[16]{0:T(128)} %param.16) | copy-start | bytes 196
  132.8 444.5 %reduce-scatter.2.cloned.1.call-start = ((), (), s32[]{:S(2)}) async-start(), calls=%async_computation.3 | async-start | bytes 9437184 | tf_op jit(solution)/shard_map/reduce_scatter | solution.py:132
  138.5 45.4 %copy-start.4 = (s32[32]{0:T(128)S(1)}, s32[32]{0:T(128)}, u32[]{:S(2)}) copy-start(s32[32]{0:T(128)} %param.17) | copy-start | bytes 388
  191.6 7.0 %copy-start.1 = (f32[1024,1024,2]{1,0,2:T(8,128)S(1)}, f32[1024,1024,2]{1,0,2:T(8,128)}, u32[]{:S(2)}) copy-start(f32[1024,1024,2]{1,0,2:T(8,128)} %get-tuple-element.407) | copy-start | bytes 25165828 | tf_op jit(solution)/shard_map/while
  208.3 7.2 %copy-start.1 = (f32[1024,1024,2]{1,0,2:T(8,128)S(1)}, f32[1024,1024,2]{1,0,2:T(8,128)}, u32[]{:S(2)}) copy-start(f32[1024,1024,2]{1,0,2:T(8,128)} %get-tuple-element.407) | copy-start | bytes 25165828 | tf_op jit(solution)/shard_map/while
  225.3 7.2 %copy-start.1 = (f32[1024,1024,2]{1,0,2:T(8,128)S(1)}, f32[1024,1024,2]{1,0,2:T(8,128)}, u32[]{:S(2)}) copy-start(f32[1024,1024,2]{1,0,2:T(8,128)} %get-tuple-element.407) | copy-start | bytes 25165828 | tf_op jit(solution)/shard_map/while
  242.2 7.2 %copy-start.1 = (f32[1024,1024,2]{1,0,2:T(8,128)S(1)}, f32[1024,1024,2]{1,0,2:T(8,128)}, u32[]{:S(2)}) copy-start(f32[1024,1024,2]{1,0,2:T(8,128)} %get-tuple-element.407) | copy-start | bytes 25165828 | tf_op jit(solution)/shard_map/while
  259.2 7.2 %copy-start.1 = (f32[1024,1024,2]{1,0,2:T(8,128)S(1)}, f32[1024,1024,2]{1,0,2:T(8,128)}, u32[]{:S(2)}) copy-start(f32[1024,1024,2]{1,0,2:T(8,128)} %get-tuple-element.407) | copy-start | bytes 25165828 | tf_op jit(solution)/shard_map/while
  276.1 7.2 %copy-start.1 = (f32[1024,1024,2]{1,0,2:T(8,128)S(1)}, f32[1024,1024,2]{1,0,2:T(8,128)}, u32[]{:S(2)}) copy-start(f32[1024,1024,2]{1,0,2:T(8,128)} %get-tuple-element.407) | copy-start | bytes 25165828 | tf_op jit(solution)/shard_map/while
  293.1 7.2 %copy-start.1 = (f32[1024,1024,2]{1,0,2:T(8,128)S(1)}, f32[1024,1024,2]{1,0,2:T(8,128)}, u32[]{:S(2)}) copy-start(f32[1024,1024,2]{1,0,2:T(8,128)} %get-tuple-element.407) | copy-start | bytes 25165828 | tf_op jit(solution)/shard_map/while
  310.0 7.2 %copy-start.1 = (f32[1024,1024,2]{1,0,2:T(8,128)S(1)}, f32[1024,1024,2]{1,0,2:T(8,128)}, u32[]{:S(2)}) copy-start(f32[1024,1024,2]{1,0,2:T(8,128)} %get-tuple-element.407) | copy-start | bytes 25165828 | tf_op jit(solution)/shard_map/while
  327.0 7.2 %copy-start.1 = (f32[1024,1024,2]{1,0,2:T(8,128)S(1)}, f32[1024,1024,2]{1,0,2:T(8,128)}, u32[]{:S(2)}) copy-start(f32[1024,1024,2]{1,0,2:T(8,128)} %get-tuple-element.407) | copy-start | bytes 25165828 | tf_op jit(solution)/shard_map/while
  343.9 7.2 %copy-start.1 = (f32[1024,1024,2]{1,0,2:T(8,128)S(1)}, f32[1024,1024,2]{1,0,2:T(8,128)}, u32[]{:S(2)}) copy-start(f32[1024,1024,2]{1,0,2:T(8,128)} %get-tuple-element.407) | copy-start | bytes 25165828 | tf_op jit(solution)/shard_map/while
  360.9 7.2 %copy-start.1 = (f32[1024,1024,2]{1,0,2:T(8,128)S(1)}, f32[1024,1024,2]{1,0,2:T(8,128)}, u32[]{:S(2)}) copy-start(f32[1024,1024,2]{1,0,2:T(8,128)} %get-tuple-element.407) | copy-start | bytes 25165828 | tf_op jit(solution)/shard_map/while
  377.8 7.2 %copy-start.1 = (f32[1024,1024,2]{1,0,2:T(8,128)S(1)}, f32[1024,1024,2]{1,0,2:T(8,128)}, u32[]{:S(2)}) copy-start(f32[1024,1024,2]{1,0,2:T(8,128)} %get-tuple-element.407) | copy-start | bytes 25165828 | tf_op jit(solution)/shard_map/while
  394.8 7.2 %copy-start.1 = (f32[1024,1024,2]{1,0,2:T(8,128)S(1)}, f32[1024,1024,2]{1,0,2:T(8,128)}, u32[]{:S(2)}) copy-start(f32[1024,1024,2]{1,0,2:T(8,128)} %get-tuple-element.407) | copy-start | bytes 25165828 | tf_op jit(solution)/shard_map/while
  411.7 7.2 %copy-start.1 = (f32[1024,1024,2]{1,0,2:T(8,128)S(1)}, f32[1024,1024,2]{1,0,2:T(8,128)}, u32[]{:S(2)}) copy-start(f32[1024,1024,2]{1,0,2:T(8,128)} %get-tuple-element.407) | copy-start | bytes 25165828 | tf_op jit(solution)/shard_map/while
  428.7 7.2 %copy-start.1 = (f32[1024,1024,2]{1,0,2:T(8,128)S(1)}, f32[1024,1024,2]{1,0,2:T(8,128)}, u32[]{:S(2)}) copy-start(f32[1024,1024,2]{1,0,2:T(8,128)} %get-tuple-element.407) | copy-start | bytes 25165828 | tf_op jit(solution)/shard_map/while
  445.6 7.2 %copy-start.1 = (f32[1024,1024,2]{1,0,2:T(8,128)S(1)}, f32[1024,1024,2]{1,0,2:T(8,128)}, u32[]{:S(2)}) copy-start(f32[1024,1024,2]{1,0,2:T(8,128)} %get-tuple-element.407) | copy-start | bytes 25165828 | tf_op jit(solution)/shard_map/while
Sparse Core Ops, SparseCore 0:
  10.9 110.2 all-gather.2
  132.9 50.9 all-gather.4
  461.9 115.3 reduce-scatter.1
where the time goes:
time: 586 us; the launch traced here: 584 us
  waiting for transfers between devices  263 us (45%)
  matrix products  237 us (40%)
  other arithmetic  64.2 us (11%)
  between operations  13.3 us (2%)
    reduce_scatter x1, waiting for transfers between devices, per_device(): lax.psum_scatter(jnp.dot(attended, o_weight, preferred_element_type=jnp.f...  116 us
    dot_general x16, matrix products, attend(): jnp.einsum('kgqs,skd->qkgd', weights.astype(jnp.bfloat16), value_rows, pr...  115 us
    all_gather x1, waiting for transfers between devices, per_device(): portion = lax.all_gather(normed, 'tensor', axis=1, tiled=True)  109 us
    dot_general x16, matrix products, attend(): jnp.einsum('qkgd,skd->kgqs', queries, key_rows, preferred_element_type=jn...  100 us
    all_gather x1, waiting for transfers between devices, per_device(): gathered = lax.all_gather(kv_pair, 'context', axis=1, tiled=True)  37.5 us
    reduce_sum x16, other arithmetic, attend(): row_sum = row_sum * factor + jnp.sum(weights, axis=-1)  31.5 us
    and x16, other arithmetic, attend(): (key_places[None, :] <= query_places[:, None]) & (key_docs[None, :] == qu...  19.1 us
  transfers between devices with their start and end apart: 3, of which 3 were waited for; matrix products, arithmetic and copies ran while one was open for 2% of the time, Pallas kernels for 0%

commit v1 on v0

v1 whole, which is shorter than its diff:
```python
import functools
import math

import jax
import jax.numpy as jnp
from jax import lax
from jax.experimental import pallas as pl
from jax.experimental.pallas import tpu as pltpu
from jax.sharding import PartitionSpec as P

HEAD_DIM = 128
SPAN = 512
KEY_SLOTS = 9

rope_theta = 500000.0
epsilon = 1e-05
masked_score = -1e30


def positions(rows, span_order, span_rows):
    slot_ids = jnp.arange(span_order.shape[0], dtype=jnp.int32)
    matches = (rows // span_rows)[:, None] == slot_ids[None, :]
    picked = jnp.sum(jnp.where(matches, span_order[None, :], 0), axis=1)
    return picked * span_rows + rows % span_rows


def rotary(values, places):
    head_dim = values.shape[-1]
    half_dim = head_dim // 2
    frequency = rope_theta ** (-(2.0 / head_dim) * jnp.arange(half_dim, dtype=jnp.float32))
    angles = places.astype(jnp.float32)[:, None] * frequency[None, :]
    cosine = jnp.cos(angles)[:, None, :]
    sine_part = jnp.sin(angles)[:, None, :]
    first_half = values[..., :half_dim]
    second = values[..., half_dim:]
    return jnp.concatenate(
        [first_half * cosine - second * sine_part, second * cosine + first_half * sine_part],
        axis=-1,
    )


def attention_kernel(heads, scale, tbl_ref, seq_ref, cnt_ref, q_ref, qpos_ref, qstart_ref,
                     k_ref, v_ref, o_ref, m_sc, l_sc, acc_sc):
    i = pl.program_id(0)
    j = pl.program_id(1)

    @pl.when(j == 0)
    def _():
        m_sc[...] = jnp.full_like(m_sc, masked_score)
        l_sc[...] = jnp.zeros_like(l_sc)
        acc_sc[...] = jnp.zeros_like(acc_sc)

    @pl.when(j < cnt_ref[i])
    def _():
        k = k_ref[...]
        v = v_ref[...]
        span = k.shape[0]
        kpos = seq_ref[i, j] * span + lax.broadcasted_iota(jnp.int32, (1, span), 1)
        visible = (kpos <= qpos_ref[...]) & (kpos >= qstart_ref[...])
        for h in range(heads):
            q = q_ref[:, h * HEAD_DIM:(h + 1) * HEAD_DIM]
            s = lax.dot_general(q, k, (((1,), (1,)), ((), ())),
                                preferred_element_type=jnp.float32) * scale
            m_old = m_sc[h]
            m_new = jnp.maximum(
                m_old, jnp.max(jnp.where(visible, s, masked_score), axis=-1, keepdims=True))
            p = jnp.where(visible, jnp.exp(s - m_new), 0.0)
            alpha = jnp.exp(m_old - m_new)
            l_sc[h] = alpha * l_sc[h] + jnp.sum(p, axis=-1, keepdims=True)
            acc_sc[h] = alpha * acc_sc[h] + jnp.dot(
                p.astype(jnp.bfloat16), v, preferred_element_type=jnp.float32)
            m_sc[h] = m_new

    @pl.when(j == pl.num_programs(1) - 1)
    def _():
        for h in range(heads):
            o_ref[:, h * HEAD_DIM:(h + 1) * HEAD_DIM] = (acc_sc[h] / l_sc[h]).astype(o_ref.dtype)


def span_attention(tbl, seq, cnt, queries, qpos, qstart, keys, values):
    rows, q_cols = queries.shape
    heads = q_cols // HEAD_DIM
    n_q = rows // SPAN
    kernel = functools.partial(attention_kernel, heads, 1.0 / math.sqrt(HEAD_DIM))
    steps = n_q * KEY_SLOTS
    cost = pl.CostEstimate(
        flops=4 * steps * heads * SPAN * SPAN * HEAD_DIM,
        transcendentals=steps * heads * SPAN * SPAN,
        bytes_accessed=steps * 2 * SPAN * HEAD_DIM * 2 + 2 * rows * q_cols * 2,
    )
    return pl.pallas_call(
        kernel,
        out_shape=jax.ShapeDtypeStruct((rows, q_cols), jnp.bfloat16),
        grid_spec=pltpu.PrefetchScalarGridSpec(
            num_scalar_prefetch=3,
            grid=(n_q, KEY_SLOTS),
            in_specs=[
                pl.BlockSpec((SPAN, q_cols), lambda i, j, t, s, c: (i, 0)),
                pl.BlockSpec((SPAN, 1), lambda i, j, t, s, c: (i, 0)),
                pl.BlockSpec((SPAN, 1), lambda i, j, t, s, c: (i, 0)),
                pl.BlockSpec((SPAN, HEAD_DIM), lambda i, j, t, s, c: (t[i, j], 0)),
                pl.BlockSpec((SPAN, HEAD_DIM), lambda i, j, t, s, c: (t[i, j], 0)),
            ],
            out_specs=pl.BlockSpec((SPAN, q_cols), lambda i, j, t, s, c: (i, 0)),
            scratch_shapes=[
                pltpu.VMEM((heads, SPAN, 1), jnp.float32),
                pltpu.VMEM((heads, SPAN, 1), jnp.float32),
                pltpu.VMEM((heads, SPAN, HEAD_DIM), jnp.float32),
            ],
        ),
        compiler_params=pltpu.CompilerParams(dimension_semantics=("arbitrary", "arbitrary")),
        cost_estimate=cost,
    )(tbl, seq, cnt, queries, qpos, qstart, keys, values)


def key_tables(span_order, doc_ends, query_spans):
    n_spans = span_order.shape[0]
    span_ids = jnp.arange(n_spans, dtype=jnp.int32)
    inverse = jnp.sum(
        jnp.where(span_order[None, :] == span_ids[:, None], span_ids[None, :], 0), axis=1)
    first_doc = jnp.sum((doc_ends[None, :] <= (span_ids * SPAN)[:, None]).astype(jnp.int32), axis=1)
    last_doc = jnp.sum(
        (doc_ends[None, :] <= (span_ids * SPAN + SPAN - 1)[:, None]).astype(jnp.int32), axis=1)
    sq = jnp.sum(jnp.where(query_spans[:, None] == span_ids[None, :], span_order[None, :], 0), axis=1)
    q_first = jnp.sum(jnp.where(sq[:, None] == span_ids[None, :], first_doc[None, :], 0), axis=1)
    back = jnp.arange(KEY_SLOTS, dtype=jnp.int32) - (KEY_SLOTS - 1)
    cand = sq[:, None] + back[None, :]
    cand_last = jnp.sum(
        jnp.where(cand[:, :, None] == span_ids[None, None, :], last_doc[None, None, :], 0), axis=2)
    valid = (cand >= 0) & (cand_last >= q_first[:, None])
    count = jnp.sum(valid.astype(jnp.int32), axis=1)
    slot = jnp.arange(KEY_SLOTS, dtype=jnp.int32)
    seq = jnp.minimum(sq[:, None] - count[:, None] + 1 + slot[None, :], sq[:, None])
    tbl = jnp.sum(jnp.where(seq[:, :, None] == span_ids[None, None, :], inverse[None, None, :], 0),
                  axis=2)
    return tbl.astype(jnp.int32), seq.astype(jnp.int32), count.astype(jnp.int32)


def per_device(tokens, norm_gain, q_weight, k_weight, v_weight, o_weight, doc_lengths, span_order):
    local_rows = tokens.shape[1]
    tok_dev = local_rows * lax.axis_size("tensor")
    model_width = tokens.shape[2]
    head_dim = HEAD_DIM
    q_cols = q_weight.shape[1]
    kv_cols = k_weight.shape[1]
    q_heads = q_cols // head_dim
    kv_local = kv_cols // head_dim
    span_rows = tok_dev // 2
    base_row = lax.axis_index("context") * tok_dev
    rows_float = tokens.astype(jnp.float32)
    normed = (
        rows_float
        * lax.rsqrt(jnp.mean(rows_float * rows_float, axis=-1, keepdims=True) + epsilon)
        * norm_gain
    ).astype(jnp.bfloat16)
    portion = lax.all_gather(normed, "tensor", axis=1, tiled=True)
    row_count = portion.shape[1]
    flat_rows = portion.reshape(row_count, model_width)
    places = positions(base_row + jnp.arange(row_count, dtype=jnp.int32), span_order, span_rows)
    query_rows = jnp.dot(flat_rows, q_weight, preferred_element_type=jnp.float32).reshape(
        row_count, q_heads, head_dim
    )
    key_rows = jnp.dot(flat_rows, k_weight, preferred_element_type=jnp.float32).reshape(
        row_count, kv_local, head_dim
    )
    value_rows = jnp.dot(flat_rows, v_weight, preferred_element_type=jnp.float32).astype(
        jnp.bfloat16
    )
    query_rows = rotary(query_rows, places).reshape(row_count, q_cols).astype(jnp.bfloat16)
    key_rows = rotary(key_rows, places).reshape(row_count, kv_cols).astype(jnp.bfloat16)
    kv_pair = jnp.stack([key_rows, value_rows])
    gathered = lax.all_gather(kv_pair, "context", axis=1, tiled=True)

    doc_ends = jnp.cumsum(doc_lengths)
    query_start = jnp.max(
        jnp.where(doc_ends[None, :] <= places[:, None], doc_ends[None, :], 0), axis=1)
    query_spans = lax.axis_index("context") * 2 + jnp.arange(2, dtype=jnp.int32)
    tbl, seq, cnt = key_tables(span_order, doc_ends, query_spans)
    attended = span_attention(
        tbl, seq, cnt, query_rows,
        places.astype(jnp.int32)[:, None], query_start.astype(jnp.int32)[:, None],
        gathered[0], gathered[1],
    )
    mixed_rows = lax.psum_scatter(
        jnp.dot(attended, o_weight, preferred_element_type=jnp.float32).astype(jnp.bfloat16),
        "tensor",
        scatter_dimension=0,
        tiled=True,
    )
    return mixed_rows.reshape(tokens.shape)


def solution(mesh):
    in_specs = (
        P("context", "tensor", None),
        P(),
        P(None, "tensor"),
        P(None, "tensor"),
        P(None, "tensor"),
        P("tensor", None),
        P(),
        P(),
    )
    out_specs = P("context", "tensor", None)
    return jax.shard_map(
        per_device, mesh=mesh, in_specs=in_specs, out_specs=out_specs, check_vma=False
    )
```

time: 586 us -> 351 us (0.60)
  matrix products: 237 us -> 21.5 us
  other arithmetic: 64.2 us -> 11.8 us
  Pallas kernels: 0 us -> 22.2 us
  local copies, waits for them, and re-layouts: 5.24 us -> 13.2 us
    dot_general x32 -> x0, matrix products: 215 us -> none  [the longest x16 115 us: attend(): jnp.einsum('kgqs,skd->qkgd', weights.astype(jnp.bfloat16), value_rows, pr...]
    reduce_sum x33 -> x7, other arithmetic: 32.9 us -> 1.39 us  [the longest x1 0.32 us: key_tables(): jnp.sum(jnp.where(seq[:, :, None] == span_ids[None, None, :], inverse[Non...]
    pallas_call x0 -> x1, Pallas kernels: none -> 22.2 us  [span_attention(): pl.pallas_call(kernel, out_shape=jax.ShapeDtypeStruct((rows, q_cols), jnp...]
    and x16 -> x0, other arithmetic: 19.1 us -> none  [attend(): (key_places[None, :] <= query_places[:, None]) & (key_docs[None, :] == qu...]
    reduce_scatter x1, waiting for transfers between devices: 116 us -> 124 us  [per_device(): lax.psum_scatter(jnp.dot(attended, o_weight, preferred_element_type=jnp.f...]
  transfers between devices with their start and end apart: 3 -> 3, of which waited for: 3 -> 3; matrix products, arithmetic and copies ran while one was open for 2% -> 5% of each run, Pallas kernels for 0% -> 0%
where the time goes in v1:
time: 351 us; the launch traced here: 349 us
  waiting for transfers between devices  267 us (76%)
  Pallas kernels  22.2 us (6%)
  matrix products  21.5 us (6%)
  between operations  13.3 us (4%)
  local copies, waits for them, and re-layouts  13.2 us (4%)
  other arithmetic  11.8 us (3%)
    reduce_scatter x1, waiting for transfers between devices, per_device(): lax.psum_scatter(jnp.dot(attended, o_weight, preferred_element_type=jnp.f...  124 us
    all_gather x1, waiting for transfers between devices, per_device(): portion = lax.all_gather(normed, 'tensor', axis=1, tiled=True)  110 us
    all_gather x1, waiting for transfers between devices, per_device(): gathered = lax.all_gather(kv_pair, 'context', axis=1, tiled=True)  32.9 us
    pallas_call x1, Pallas kernels, span_attention(): pl.pallas_call(kernel, out_shape=jax.ShapeDtypeStruct((rows, q_cols), jnp...  22.2 us
  transfers between devices with their start and end apart: 3, of which 3 were waited for; matrix products, arithmetic and copies ran while one was open for 5% of the time, Pallas kernels for 0%

profile of v1, /device:TPU:8, one launch (start us, length us, event | category | flops | bytes accessed | tf_op | source)
XLA Modules:
  0.0 349.0 jit_solution(8208729810666434161)
XLA Ops:
  6.5 1.7 fusion.6
  8.2 2.5 fusion.8
  11.0 110.2 %all-gather.3.cloned.1.call-done = bf16[1,1024,4096]{2,1,0:T(8,128)(2,1)} async-done(((bf16[1,128,4096]{2,1,0:T(8,128)(2,1)}), bf16[1,1024,4096]{2,1,0:T(8,128)(2,1)}) %all-gather.3.cloned.1.call-update) | async-done | bytes 8388624 | tf_op jit(solution)/shard_map/all_gather | solution.py:156
  121.2 6.1 %fusion.9 = f32[1024,1,128]{2,0,1:T(8,128)S(1)} fusion(bf16[4096,128]{1,0:T(8,128)(2,1)} %param.11, bf16[1,1024,4096]{2,1,0:T(8,128)(2,1)} %all-gather.3.cloned.1.call-done), kind=kOutput, calls=%fused_computation.14 | convolution fusion | flops 1073741824 | bytes 9961472 | tf_op jit(solution)/shard_map/dot_general | solution.py:163
  127.3 2.4 fusion.23
  129.9 2.3 fusion.15
  132.2 0.8 pad_maximum_fusion.1
  133.1 0.2 reduce-scatter.2.cloned.1.call-start
  133.3 4.1 %copy.41 = bf16[256,4096]{1,0:T(8,128)(2,1)} copy(bf16[256,4096]{0,1:T(8,128)(2,1)} %bitcast.36) | data formatting | bytes 4194304 | tf_op jit(solution)/shard_map/dot_general | solution.py:160
  138.1 0.3 fusion.31
  138.7 0.2 fusion.41.cnt_ref
  139.2 0.3 fusion.32
  139.5 0.7 copy.38.tbl_ref
  140.2 0.2 copy.35
  140.5 1.1 copy.39.qstart_ref
  141.6 1.0 multiply_cosine_fusion.1
  142.6 1.0 fusion.27.qpos_ref
  143.6 6.5 %fusion = f32[1024,2,128]{0,2,1:T(8,128)S(1)} fusion(bf16[2,128,4096]{2,1,0:T(8,128)(2,1)} %bitcast.37, bf16[1,1024,4096]{2,1,0:T(8,128)(2,1)} %all-gather.3.cloned.1.call-done), kind=kOutput, calls=%fused_computation | convolution fusion | flops 2147483648 | bytes 11534336 | tf_op jit(solution)/shard_map/dot_general | solution.py:160
  150.3 1.0 copy.42.q_ref
  151.3 32.9 %all-gather.5.cloned.1.call-done = bf16[2,16384,128]{2,1,0:T(8,128)(2,1)} async-done(((bf16[2,1024,128]{2,1,0:T(8,128)(2,1)}), bf16[2,16384,128]{2,1,0:T(8,128)(2,1)}) %all-gather.5.cloned.1.call-update) | async-done | bytes 8388624 | tf_op jit(solution)/shard_map/all_gather | solution.py:172
  184.3 5.7 %slice_bitcast_fusion = (bf16[16384,128]{1,0:T(8,128)(2,1)}, bf16[16384,128]{1,0:T(8,128)(2,1)}) fusion(bf16[2,16384,128]{2,1,0:T(8,128)(2,1)} %all-gather.5.cloned.1.call-done), kind=kLoop, calls=%fused_computation.7 | loop fusion | bytes 16777216 | tf_op jit(solution)/shard_map/squeeze | solution.py:182
  190.0 22.2 %shard_map.82 = bf16[1024,256]{1,0:T(8,128)(2,1)} custom-call(s32[2,9]{1,0:T(2,128)} %copy.38.tbl_ref, s32[2,9]{1,0:T(2,128)} %copy-done.1, s32[2]{0:T(128)} %copy-done.4, bf16[1024,256]{1,0:T(8,128)(2,1)} %copy.42.q_ref, s32[1024,1]{1,0:T(8,128)} %fusion.27.qpos_ref, s32[1024,1]{1,0:T(8,128)} %copy.39.qstart_ref, ...), custom_call_target="tpu_custom_call" | custom-call | flops 4831838208 | bytes 5767168 | tf_op jit(solution)/shard_map/pallas_call | solution.py:91
  212.2 6.6 %convolution_convert_fusion = bf16[1024,4096]{1,0:T(8,128)(2,1)} fusion(bf16[1024,256]{1,0:T(8,128)(2,1)} %shard_map.82, bf16[256,4096]{1,0:T(8,128)(2,1)S(1)} %copy-done), kind=kOutput, calls=%fused_computation.6 | convolution fusion | flops 2151677952 | bytes 11010048 | tf_op jit(solution)/shard_map/dot_general | solution.py:185
  218.8 123.7 %reduce-scatter.2.cloned.1.call-done = bf16[128,4096]{1,0:T(8,128)(2,1)} async-done(((bf16[1024,4096]{1,0:T(8,128)(2,1)}), bf16[128,4096]{1,0:T(8,128)(2,1)}) %reduce-scatter.2.cloned.1.call-update) | async-done | bytes 1048592 | tf_op jit(solution)/shard_map/reduce_scatter | solution.py:184
  (44 shorter events, 2.0 us)
Async XLA Ops:
  6.5 205.7 %copy-start = (bf16[256,4096]{1,0:T(8,128)(2,1)S(1)}, bf16[256,4096]{1,0:T(8,128)(2,1)}, u32[]{:S(2)}) copy-start(bf16[256,4096]{1,0:T(8,128)(2,1)} %param.13) | copy-start | bytes 6291460
  6.5 4.3 %copy-start.3 = (s32[32]{0:T(128)S(1)}, s32[32]{0:T(128)}, u32[]{:S(2)}) copy-start(s32[32]{0:T(128)} %param.15) | copy-start | bytes 388
  6.5 114.6 %all-gather.3.cloned.1.call-start = ((), (), s32[]{:S(2)}) async-start(), calls=%async_computation.1 | async-start | bytes 9437184 | tf_op jit(solution)/shard_map/all_gather | solution.py:156
  10.8 173.5 %all-gather.5.cloned.1.call-start = ((), (), s32[]{:S(2)}) async-start(), calls=%async_computation.2 | async-start | bytes 8912896 | tf_op jit(solution)/shard_map/all_gather | solution.py:172
  121.2 8.7 %copy-start.5 = (bf16[1,1024,4096]{2,1,0:T(8,128)(2,1)S(1)}, bf16[1,1024,4096]{2,1,0:T(8,128)(2,1)}, u32[]{:S(2)}) copy-start(bf16[1,1024,4096]{2,1,0:T(8,128)(2,1)} %all-gather.3.cloned.1.call-done) | copy-start | bytes 25165828
  121.2 8.7 %copy-start.6 = (bf16[4096,128]{1,0:T(8,128)(2,1)S(1)}, bf16[4096,128]{1,0:T(8,128)(2,1)}, u32[]{:S(2)}) copy-start(bf16[4096,128]{1,0:T(8,128)(2,1)} %param.12) | copy-start | bytes 3145732
  132.2 5.6 %copy-start.2 = (s32[16]{0:T(128)S(1)}, s32[16]{0:T(128)}, u32[]{:S(2)}) copy-start(s32[16]{0:T(128)} %param.14) | copy-start | bytes 196
  133.1 209.4 %reduce-scatter.2.cloned.1.call-start = ((), (), s32[]{:S(2)}) async-start(), calls=%async_computation.3 | async-start | bytes 9437184 | tf_op jit(solution)/shard_map/reduce_scatter | solution.py:184
  138.9 11.2 %copy-start.4 = (s32[2]{0:T(128)}, s32[2]{0:T(128)S(1)}, u32[]{:S(2)}) copy-start(s32[2]{0:T(128)S(1)} %fusion.41.cnt_ref) | copy-start | bytes 28
  139.0 11.1 %copy-start.1 = (s32[2,9]{1,0:T(2,128)}, s32[2,9]{1,0:T(2,128)S(1)}, u32[]{:S(2)}) copy-start(s32[2,9]{1,0:T(2,128)S(1)} %add_minimum_fusion.seq_ref) | copy-start | bytes 220
Sparse Core Ops, SparseCore 0:
  10.9 110.2 all-gather.2
  133.2 51.0 all-gather.4
  219.0 123.5 reduce-scatter.1

commit v2 on v1

--- a/solution.py
+++ b/solution.py
@@ -77,7 +77,7 @@
             o_ref[:, h * HEAD_DIM:(h + 1) * HEAD_DIM] = (acc_sc[h] / l_sc[h]).astype(o_ref.dtype)
 
 
-def span_attention(tbl, seq, cnt, queries, qpos, qstart, keys, values):
+def span_attention(tbl, seq, cnt, queries, qpos, qstart, kv):
     rows, q_cols = queries.shape
     heads = q_cols // HEAD_DIM
     n_q = rows // SPAN
@@ -98,8 +98,8 @@
                 pl.BlockSpec((SPAN, q_cols), lambda i, j, t, s, c: (i, 0)),
                 pl.BlockSpec((SPAN, 1), lambda i, j, t, s, c: (i, 0)),
                 pl.BlockSpec((SPAN, 1), lambda i, j, t, s, c: (i, 0)),
-                pl.BlockSpec((SPAN, HEAD_DIM), lambda i, j, t, s, c: (t[i, j], 0)),
-                pl.BlockSpec((SPAN, HEAD_DIM), lambda i, j, t, s, c: (t[i, j], 0)),
+                pl.BlockSpec((None, SPAN, HEAD_DIM), lambda i, j, t, s, c: (0, t[i, j], 0)),
+                pl.BlockSpec((None, SPAN, HEAD_DIM), lambda i, j, t, s, c: (1, t[i, j], 0)),
             ],
             out_specs=pl.BlockSpec((SPAN, q_cols), lambda i, j, t, s, c: (i, 0)),
             scratch_shapes=[
@@ -110,7 +110,7 @@
         ),
         compiler_params=pltpu.CompilerParams(dimension_semantics=("arbitrary", "arbitrary")),
         cost_estimate=cost,
-    )(tbl, seq, cnt, queries, qpos, qstart, keys, values)
+    )(tbl, seq, cnt, queries, qpos, qstart, kv, kv)
 
 
 def key_tables(span_order, doc_ends, query_spans):
@@ -138,7 +138,7 @@
 
 def per_device(tokens, norm_gain, q_weight, k_weight, v_weight, o_weight, doc_lengths, span_order):
     local_rows = tokens.shape[1]
-    tok_dev = local_rows * lax.axis_size("tensor")
+    tok_dev = local_rows * lax.axis_size(TENSOR)
     model_width = tokens.shape[2]
     head_dim = HEAD_DIM
     q_cols = q_weight.shape[1]
@@ -146,14 +146,14 @@
     q_heads = q_cols // head_dim
     kv_local = kv_cols // head_dim
     span_rows = tok_dev // 2
-    base_row = lax.axis_index("context") * tok_dev
+    base_row = lax.axis_index(CONTEXT) * tok_dev
     rows_float = tokens.astype(jnp.float32)
     normed = (
         rows_float
         * lax.rsqrt(jnp.mean(rows_float * rows_float, axis=-1, keepdims=True) + epsilon)
         * norm_gain
     ).astype(jnp.bfloat16)
-    portion = lax.all_gather(normed, "tensor", axis=1, tiled=True)
+    portion = lax.all_gather(normed, TENSOR, axis=1, tiled=True)
     row_count = portion.shape[1]
     flat_rows = portion.reshape(row_count, model_width)
     places = positions(base_row + jnp.arange(row_count, dtype=jnp.int32), span_order, span_rows)
@@ -169,39 +169,51 @@
     query_rows = rotary(query_rows, places).reshape(row_count, q_cols).astype(jnp.bfloat16)
     key_rows = rotary(key_rows, places).reshape(row_count, kv_cols).astype(jnp.bfloat16)
     kv_pair = jnp.stack([key_rows, value_rows])
-    gathered = lax.all_gather(kv_pair, "context", axis=1, tiled=True)
+    gathered = lax.all_gather(kv_pair, CONTEXT, axis=1, tiled=True)
 
     doc_ends = jnp.cumsum(doc_lengths)
     query_start = jnp.max(
         jnp.where(doc_ends[None, :] <= places[:, None], doc_ends[None, :], 0), axis=1)
-    query_spans = lax.axis_index("context") * 2 + jnp.arange(2, dtype=jnp.int32)
+    query_spans = lax.axis_index(CONTEXT) * 2 + jnp.arange(2, dtype=jnp.int32)
     tbl, seq, cnt = key_tables(span_order, doc_ends, query_spans)
     attended = span_attention(
         tbl, seq, cnt, query_rows,
         places.astype(jnp.int32)[:, None], query_start.astype(jnp.int32)[:, None],
-        gathered[0], gathered[1],
-    )
-    mixed_rows = lax.psum_scatter(
-        jnp.dot(attended, o_weight, preferred_element_type=jnp.float32).astype(jnp.bfloat16),
-        "tensor",
-        scatter_dimension=0,
-        tiled=True,
-    )
+        gathered,
+    )
+    partner_o = lax.ppermute(o_weight, ("yh", "ylo"), [(0, 3), (3, 0), (1, 2), (2, 1)])
+    plane = lax.axis_index("yh")
+    half = row_count // 2
+    own_rows = lax.dynamic_slice_in_dim(attended, plane * half, half, 0)
+    other_rows = lax.dynamic_slice_in_dim(attended, (1 - plane) * half, half, 0)
+    partner_rows = lax.ppermute(other_rows, "yh", [(0, 1), (1, 0)])
+    mixed = jnp.dot(
+        jnp.concatenate([own_rows, partner_rows], axis=1),
+        jnp.concatenate([o_weight, partner_o], axis=0),
+        preferred_element_type=jnp.float32,
+    ).astype(jnp.bfloat16)
+    mixed_rows = lax.psum_scatter(mixed, "x", scatter_dimension=0, tiled=True)
     return mixed_rows.reshape(tokens.shape)
 
 
+TENSOR = ("yh", "x")
+CONTEXT = ("z", "ylo", "core")
+
+
 def solution(mesh):
+    devices = mesh.devices.reshape(2, mesh.devices.shape[0] // 2, -1, 2, 2)
+    split_mesh = jax.sharding.Mesh(devices, ("yh", "x", "z", "ylo", "core"))
     in_specs = (
-        P("context", "tensor", None),
+        P(CONTEXT, TENSOR, None),
         P(),
-        P(None, "tensor"),
-        P(None, "tensor"),
-        P(None, "tensor"),
-        P("tensor", None),
+        P(None, TENSOR),
+        P(None, TENSOR),
+        P(None, TENSOR),
+        P(TENSOR, None),
         P(),
         P(),
     )
-    out_specs = P("context", "tensor", None)
+    out_specs = P(CONTEXT, TENSOR, None)
     return jax.shard_map(
-        per_device, mesh=mesh, in_specs=in_specs, out_specs=out_specs, check_vma=False
-    )
+        per_device, mesh=split_mesh, in_specs=in_specs, out_specs=out_specs, check_vma=False
+    )

time: 351 us -> 291 us (0.83)
  waiting for transfers between devices: 267 us -> 201 us
  Pallas kernels: 22.2 us -> 33.3 us
  local copies, waits for them, and re-layouts: 13.2 us -> 7.28 us
    reduce_scatter x1, waiting for transfers between devices: 124 us -> 50.5 us  [per_device(): mixed_rows = lax.psum_scatter(mixed, 'x', scatter_dimension=0, tiled=True)]
    pallas_call x1, Pallas kernels: 22.2 us -> 33.3 us  [span_attention(): pl.pallas_call(kernel, out_shape=jax.ShapeDtypeStruct((rows, q_cols), jnp...]
    ppermute x0 -> x2, waiting for transfers between devices: none -> 5.79 us  [the longest x1 5.79 us: per_device(): partner_rows = lax.ppermute(other_rows, 'yh', [(0, 1), (1, 0)])]
    squeeze x1 -> x0, local copies, waits for them, and re-layouts: 5.71 us -> none  [per_device(): gathered[1]]
  transfers between devices with their start and end apart: 3 -> 5, of which waited for: 3 -> 4; matrix products, arithmetic and copies ran while one was open for 5% -> 6% of each run, Pallas kernels for 0% -> 12%
where the time goes in v2:
time: 291 us; the launch traced here: 289 us
  waiting for transfers between devices  201 us (69%)
  Pallas kernels  33.3 us (11%)
  matrix products  20.5 us (7%)
  between operations  13.3 us (5%)
  other arithmetic  11.7 us (4%)
  local copies, waits for them, and re-layouts  7.28 us (3%)
    all_gather x1, waiting for transfers between devices, per_device(): portion = lax.all_gather(normed, TENSOR, axis=1, tiled=True)  110 us
    reduce_scatter x1, waiting for transfers between devices, per_device(): mixed_rows = lax.psum_scatter(mixed, 'x', scatter_dimension=0, tiled=True)  50.5 us
    all_gather x1, waiting for transfers between devices, per_device(): gathered = lax.all_gather(kv_pair, CONTEXT, axis=1, tiled=True)  34 us
    pallas_call x1, Pallas kernels, span_attention(): pl.pallas_call(kernel, out_shape=jax.ShapeDtypeStruct((rows, q_cols), jnp...  33.3 us
    dot_general x1, matrix products, per_device(): jnp.dot(flat_rows, q_weight, preferred_element_type=jnp.float32)  6.41 us
    dot_general x1, matrix products, per_device(): jnp.dot(jnp.concatenate([own_rows, partner_rows], axis=1), jnp.concatenat...  5.9 us
    dot_general x1, matrix products, per_device(): jnp.dot(flat_rows, k_weight, preferred_element_type=jnp.float32)  5.85 us
  transfers between devices with their start and end apart: 5, of which 4 were waited for; matrix products, arithmetic and copies ran while one was open for 6% of the time, Pallas kernels for 12%

profile of v2, /device:TPU:8, one launch (start us, length us, event | category | flops | bytes accessed | tf_op | source)
XLA Modules:
  0.0 289.3 jit_solution(1383756307426927836)
XLA Ops:
  6.5 1.6 fusion.9
  8.2 2.5 fusion.11
  10.9 110.2 %all-gather.3.cloned.1.call-done = bf16[1,1024,4096]{2,1,0:T(8,128)(2,1)} async-done(((bf16[1,128,4096]{2,1,0:T(8,128)(2,1)}), bf16[1,1024,4096]{2,1,0:T(8,128)(2,1)}) %all-gather.3.cloned.1.call-update) | async-done | bytes 8388624 | tf_op jit(solution)/shard_map/all_gather | solution.py:156
  121.1 5.9 %fusion.12 = f32[1024,1,128]{2,0,1:T(8,128)S(1)} fusion(bf16[4096,128]{1,0:T(8,128)(2,1)S(1)} %copy-done, bf16[1,1024,4096]{2,1,0:T(8,128)(2,1)} %all-gather.3.cloned.1.call-done), kind=kOutput, calls=%fused_computation.15 | convolution fusion | flops 1073741824 | bytes 9961472 | tf_op jit(solution)/shard_map/dot_general | solution.py:163
  127.0 2.4 fusion.26
  129.6 2.3 fusion.18
  131.9 0.8 pad_maximum_fusion.1
  132.9 0.3 collective-permute-start.1
  133.2 3.0 %copy.41 = bf16[256,4096]{1,0:T(8,128)(2,1)} copy(bf16[256,4096]{0,1:T(8,128)(2,1)S(1)} %bitcast.30) | data formatting | bytes 4194304 | tf_op jit(solution)/shard_map/dot_general | solution.py:160
  136.8 0.3 fusion.37
  137.9 0.3 fusion.38
  138.2 0.6 copy.38.tbl_ref
  139.2 1.0 copy.39.qstart_ref
  140.2 1.0 multiply_cosine_fusion.1
  141.2 1.1 fusion.30.qpos_ref
  142.2 6.4 %fusion = f32[1024,2,128]{0,2,1:T(8,128)S(1)} fusion(bf16[2,128,4096]{2,1,0:T(8,128)(2,1)} %bitcast.31, bf16[1,1024,4096]{2,1,0:T(8,128)(2,1)} %all-gather.3.cloned.1.call-done), kind=kOutput, calls=%fused_computation | convolution fusion | flops 2147483648 | bytes 11534336 | tf_op jit(solution)/shard_map/dot_general | solution.py:160
  148.9 1.0 copy.42.q_ref
  149.9 34.0 %all-gather.5.cloned.1.call-done.k_ref.v_ref = bf16[2,16384,128]{2,1,0:T(8,128)(2,1)} async-done(((bf16[2,1024,128]{2,1,0:T(8,128)(2,1)}), bf16[2,16384,128]{2,1,0:T(8,128)(2,1)}) %all-gather.5.cloned.1.call-update) | async-done | bytes 8388624 | tf_op jit(solution)/shard_map/all_gather | solution.py:172
  183.9 33.3 %shard_map.82 = bf16[1024,256]{1,0:T(8,128)(2,1)} custom-call(s32[2,9]{1,0:T(2,128)} %copy.38.tbl_ref, s32[2,9]{1,0:T(2,128)} %copy-done.2, s32[2]{0:T(128)} %copy-done.3, bf16[1024,256]{1,0:T(8,128)(2,1)} %copy.42.q_ref, s32[1024,1]{1,0:T(8,128)} %fusion.30.qpos_ref, s32[1024,1]{1,0:T(8,128)} %copy.39.qstart_ref, ...), custom_call_target="tpu_custom_call" | custom-call | flops 4831838208 | bytes 5767168 | tf_op jit(solution)/shard_map/pallas_call | solution.py:91
  217.3 1.1 constant_dynamic-slice_fusion.1
  218.3 2.2 collective-permute-start
  220.5 5.8 %collective-permute-done = bf16[512,256]{1,0:T(8,128)(2,1)S(1)} collective-permute-done((bf16[512,256]{1,0:T(8,128)(2,1)S(1)}, bf16[512,256]{1,0:T(8,128)(2,1)S(1)}, u32[]{:S(2)}, u32[]{:S(2)}) %collective-permute-start) | collective-permute-done | bytes 262176 | tf_op jit(solution)/shard_map/ppermute | solution.py:189
  226.3 5.9 %convolution_convert_fusion = bf16[512,4096]{1,0:T(8,128)(2,1)} fusion(bf16[256,4096]{1,0:T(8,128)(2,1)} %collective-permute-done.1, bf16[256,4096]{1,0:T(8,128)(2,1)S(1)} %copy-done.7, bf16[512,256]{1,0:T(8,128)(2,1)S(1)} %collective-permute-done, bf16[512,256]{1,0:T(8,128)(2,1)S(1)} %get-tuple-element.13), kind=kOutput, calls=%fused_computation.6 | convolution fusion | flops 2159017984 | bytes 8912896 | tf_op jit(solution)/shard_map/dot_general | solution.py:190
  232.2 50.5 %reduce-scatter.2.cloned.1.call-done = bf16[128,4096]{1,0:T(8,128)(2,1)} async-done(((bf16[512,4096]{1,0:T(8,128)(2,1)}), bf16[128,4096]{1,0:T(8,128)(2,1)}) %reduce-scatter.2.cloned.1.call-update) | async-done | bytes 1048592 | tf_op jit(solution)/shard_map/reduce_scatter | solution.py:195
  (52 shorter events, 2.4 us)
Async XLA Ops:
  6.5 114.6 %copy-start = (bf16[4096,128]{1,0:T(8,128)(2,1)S(1)}, bf16[4096,128]{1,0:T(8,128)(2,1)}, u32[]{:S(2)}) copy-start(bf16[4096,128]{1,0:T(8,128)(2,1)} %param.11) | copy-start | bytes 3145732
  6.5 4.3 %copy-start.5 = (s32[32]{0:T(128)S(1)}, s32[32]{0:T(128)}, u32[]{:S(2)}) copy-start(s32[32]{0:T(128)} %param.15) | copy-start | bytes 388
  6.5 114.6 %all-gather.3.cloned.1.call-start = ((), (), s32[]{:S(2)}) async-start(), calls=%async_computation.1 | async-start | bytes 9437184 | tf_op jit(solution)/shard_map/all_gather | solution.py:156
  10.7 173.2 %all-gather.5.cloned.1.call-start = ((), (), s32[]{:S(2)}) async-start(), calls=%async_computation.2 | async-start | bytes 8912896 | tf_op jit(solution)/shard_map/all_gather | solution.py:172
  121.1 8.4 %copy-start.6 = (bf16[1,1024,4096]{2,1,0:T(8,128)(2,1)S(1)}, bf16[1,1024,4096]{2,1,0:T(8,128)(2,1)}, u32[]{:S(2)}) copy-start(bf16[1,1024,4096]{2,1,0:T(8,128)(2,1)} %all-gather.3.cloned.1.call-done) | copy-start | bytes 25165828
  121.1 8.5 %copy-start.8 = (bf16[4096,128]{1,0:T(8,128)(2,1)S(1)}, bf16[4096,128]{1,0:T(8,128)(2,1)}, u32[]{:S(2)}) copy-start(bf16[4096,128]{1,0:T(8,128)(2,1)} %param.12) | copy-start | bytes 3145732
  129.6 3.6 %copy-start.1 = (bf16[4096,256]{1,0:T(8,128)(2,1)S(1)}, bf16[4096,256]{1,0:T(8,128)(2,1)}, u32[]{:S(2)}) copy-start(bf16[4096,256]{1,0:T(8,128)(2,1)} %param.10) | copy-start | bytes 6291460
  131.9 4.5 %copy-start.4 = (s32[16]{0:T(128)S(1)}, s32[16]{0:T(128)}, u32[]{:S(2)}) copy-start(s32[16]{0:T(128)} %param.14) | copy-start | bytes 196
  132.8 149.9 %reduce-scatter.2.cloned.1.call-start = ((), (), s32[]{:S(2)}) async-start(), calls=%async_computation.3 | async-start | bytes 5242880 | tf_op jit(solution)/shard_map/reduce_scatter | solution.py:195
  132.9 87.6 %collective-permute-start.1 = (bf16[256,4096]{1,0:T(8,128)(2,1)}, bf16[256,4096]{1,0:T(8,128)(2,1)}, u32[]{:S(2)}, u32[]{:S(2)}) collective-permute-start(bf16[256,4096]{1,0:T(8,128)(2,1)} %param.13), channel_id=1, source_target_pairs={{0,66},{66,0},{2,64},{64,2},{1,67},{67,1},{3,65},{65,3},{4,70},{70... | collective-permute-start | bytes 6291464 | tf_op jit(solution)/shard_map/ppermute | solution.py:184
  137.6 11.1 %copy-start.3 = (s32[2]{0:T(128)}, s32[2]{0:T(128)S(1)}, u32[]{:S(2)}) copy-start(s32[2]{0:T(128)S(1)} %fusion.47.cnt_ref) | copy-start | bytes 28
  137.7 11.0 %copy-start.2 = (s32[2,9]{1,0:T(2,128)}, s32[2,9]{1,0:T(2,128)S(1)}, u32[]{:S(2)}) copy-start(s32[2,9]{1,0:T(2,128)S(1)} %add_minimum_fusion.seq_ref) | copy-start | bytes 220
  149.9 76.4 %copy-start.7 = (bf16[256,4096]{1,0:T(8,128)(2,1)S(1)}, bf16[256,4096]{1,0:T(8,128)(2,1)}, u32[]{:S(2)}) copy-start(bf16[256,4096]{1,0:T(8,128)(2,1)} %param.13) | copy-start | bytes 6291460
  218.3 8.0 %collective-permute-start = (bf16[512,256]{1,0:T(8,128)(2,1)S(1)}, bf16[512,256]{1,0:T(8,128)(2,1)S(1)}, u32[]{:S(2)}, u32[]{:S(2)}) collective-permute-start(bf16[512,256]{1,0:T(8,128)(2,1)S(1)} %get-tuple-element.14), channel_id=1, source_target_pairs={{0,64},{64,0},{1,65},{65,1},{2,66},{66,2},{3,67},{67,3},{4,68},{68... | collective-permute-start | bytes 786440 | tf_op jit(solution)/shard_map/ppermute | solution.py:189
Sparse Core Ops, SparseCore 0:
  10.8 110.2 all-gather.2
  132.9 50.9 all-gather.4
  232.3 50.3 reduce-scatter.1

commit v3 on v2

--- a/solution.py
+++ b/solution.py
@@ -153,23 +153,38 @@
         * lax.rsqrt(jnp.mean(rows_float * rows_float, axis=-1, keepdims=True) + epsilon)
         * norm_gain
     ).astype(jnp.bfloat16)
-    portion = lax.all_gather(normed, TENSOR, axis=1, tiled=True)
-    row_count = portion.shape[1]
-    flat_rows = portion.reshape(row_count, model_width)
-    places = positions(base_row + jnp.arange(row_count, dtype=jnp.int32), span_order, span_rows)
-    query_rows = jnp.dot(flat_rows, q_weight, preferred_element_type=jnp.float32).reshape(
-        row_count, q_heads, head_dim
-    )
-    key_rows = jnp.dot(flat_rows, k_weight, preferred_element_type=jnp.float32).reshape(
-        row_count, kv_local, head_dim
-    )
-    value_rows = jnp.dot(flat_rows, v_weight, preferred_element_type=jnp.float32).astype(
-        jnp.bfloat16
-    )
-    query_rows = rotary(query_rows, places).reshape(row_count, q_cols).astype(jnp.bfloat16)
-    key_rows = rotary(key_rows, places).reshape(row_count, kv_cols).astype(jnp.bfloat16)
-    kv_pair = jnp.stack([key_rows, value_rows])
+    plane = lax.axis_index("yh")
+    core = lax.axis_index("core")
+    weights = jnp.concatenate([q_weight, k_weight, v_weight], axis=1)
+    half_in = weights.shape[0] // 2
+    sent_half = lax.dynamic_slice_in_dim(weights, core * half_in, half_in, 0)
+    partner_half = lax.ppermute(sent_half, ("yh", "ylo"), NEIGHBOUR)
+    partner_weights = lax.all_gather(partner_half, "core", axis=0, tiled=True)
+    plane_rows = lax.all_gather(normed, "x", axis=1, tiled=True)
+    half = plane_rows.shape[1]
+    flat_rows = plane_rows.reshape(half, model_width)
+    all_places = positions(base_row + jnp.arange(tok_dev, dtype=jnp.int32), span_order, span_rows)
+    places = lax.dynamic_slice_in_dim(all_places, plane * half, half, 0)
+
+    def project(w):
+        out = jnp.dot(flat_rows, w, preferred_element_type=jnp.float32)
+        q = rotary(out[:, :q_cols].reshape(half, q_heads, head_dim), places)
+        k = rotary(out[:, q_cols:q_cols + kv_cols].reshape(half, kv_local, head_dim), places)
+        return jnp.concatenate(
+            [q.reshape(half, q_cols), k.reshape(half, kv_cols), out[:, q_cols + kv_cols:]], axis=1
+        ).astype(jnp.bfloat16)
+
+    own = project(weights)
+    for_partner = project(partner_weights)
+    received = lax.ppermute(for_partner, "yh", [(0, 1), (1, 0)])
+    first = jnp.where(plane == 0, own, received)
+    second = jnp.where(plane == 0, received, own)
+    projected = jnp.concatenate([first, second], axis=0)
+    query_rows = projected[:, :q_cols]
+    kv_pair = jnp.stack([projected[:, q_cols:q_cols + kv_cols], projected[:, q_cols + kv_cols:]])
     gathered = lax.all_gather(kv_pair, CONTEXT, axis=1, tiled=True)
+    places = all_places
+    row_count = tok_dev
 
     doc_ends = jnp.cumsum(doc_lengths)
     query_start = jnp.max(
@@ -181,8 +196,10 @@
         places.astype(jnp.int32)[:, None], query_start.astype(jnp.int32)[:, None],
         gathered,
     )
-    partner_o = lax.ppermute(o_weight, ("yh", "ylo"), [(0, 3), (3, 0), (1, 2), (2, 1)])
-    plane = lax.axis_index("yh")
+    o_half = o_weight.shape[0] // 2
+    o_sent = lax.dynamic_slice_in_dim(o_weight, core * o_half, o_half, 0)
+    partner_o = lax.all_gather(
+        lax.ppermute(o_sent, ("yh", "ylo"), NEIGHBOUR), "core", axis=0, tiled=True)
     half = row_count // 2
     own_rows = lax.dynamic_slice_in_dim(attended, plane * half, half, 0)
     other_rows = lax.dynamic_slice_in_dim(attended, (1 - plane) * half, half, 0)
@@ -197,6 +214,7 @@
 
 
 TENSOR = ("yh", "x")
+NEIGHBOUR = [(0, 3), (3, 0), (1, 2), (2, 1)]
 CONTEXT = ("z", "ylo", "core")
 
 

time: 291 us -> 323 us (1.11)
  waiting for transfers between devices: 201 us -> 227 us
  local copies, waits for them, and re-layouts: 7.28 us -> 16.7 us
  matrix products: 20.5 us -> 14.2 us
  starting transfers between devices: 2.52 us -> 8.03 us
    ppermute x1 -> x3, waiting for transfers between devices: 0.01 us -> 79.8 us  [the longest x1 45.8 us: per_device(): partner_half = lax.ppermute(sent_half, ('yh', 'ylo'), NEIGHBOUR)]
    all_gather x1 -> x3, waiting for transfers between devices: 110 us -> 68.1 us  [the longest x1 51.2 us: per_device(): plane_rows = lax.all_gather(normed, 'x', axis=1, tiled=True)]
    all_gather x1, waiting for transfers between devices: 34 us -> 21.4 us  [per_device(): gathered = lax.all_gather(kv_pair, CONTEXT, axis=1, tiled=True)]
    unnamed x18 -> x46, local copies, waits for them, and re-layouts: 0.04 us -> 9.09 us
    dot_general x3 -> x2, matrix products: 14.6 us -> 8.34 us  [project(): out = jnp.dot(flat_rows, w, preferred_element_type=jnp.float32)]
    ppermute x1 -> x3, starting transfers between devices: 0.27 us -> 5.59 us  [the longest x1 2.37 us: per_device(): received = lax.ppermute(for_partner, 'yh', [(0, 1), (1, 0)])]
  transfers between devices with their start and end apart: 5 -> 9, of which waited for: 4 -> 8; matrix products, arithmetic and copies ran while one was open for 6% -> 4% of each run, Pallas kernels for 12% -> 10%
where the time goes in v3:
time: 323 us; the launch traced here: 322 us
  waiting for transfers between devices  227 us (70%)
  Pallas kernels  30.7 us (10%)
  local copies, waits for them, and re-layouts  16.7 us (5%)
  matrix products  14.2 us (4%)
  between operations  13.6 us (4%)
  other arithmetic  11.7 us (4%)
  starting transfers between devices  8.03 us (2%)
    reduce_scatter x1, waiting for transfers between devices, per_device(): mixed_rows = lax.psum_scatter(mixed, 'x', scatter_dimension=0, tiled=True)  51.8 us
    all_gather x1, waiting for transfers between devices, per_device(): plane_rows = lax.all_gather(normed, 'x', axis=1, tiled=True)  51.2 us
    ppermute x1, waiting for transfers between devices, per_device(): partner_half = lax.ppermute(sent_half, ('yh', 'ylo'), NEIGHBOUR)  45.8 us
    pallas_call x1, Pallas kernels, span_attention(): pl.pallas_call(kernel, out_shape=jax.ShapeDtypeStruct((rows, q_cols), jnp...  30.7 us
    all_gather x1, waiting for transfers between devices, per_device(): gathered = lax.all_gather(kv_pair, CONTEXT, axis=1, tiled=True)  21.4 us
    ppermute x1, waiting for transfers between devices, per_device(): lax.ppermute(o_sent, ('yh', 'ylo'), NEIGHBOUR)  21.2 us
    all_gather x1, waiting for transfers between devices, per_device(): partner_weights = lax.all_gather(partner_half, 'core', axis=0, tiled=True)  16.9 us
    ppermute x1, waiting for transfers between devices, per_device(): received = lax.ppermute(for_partner, 'yh', [(0, 1), (1, 0)])  12.7 us
  transfers between devices with their start and end apart: 9, of which 8 were waited for; matrix products, arithmetic and copies ran while one was open for 4% of the time, Pallas kernels for 10%

profile of v3, /device:TPU:8, one launch (start us, length us, event | category | flops | bytes accessed | tf_op | source)
XLA Modules:
  0.0 321.8 jit_solution(4454122952196643168)
XLA Ops:
  6.5 3.3 %constant_dynamic-update-slice_fusion.2 = bf16[4096,512]{1,0:T(8,128)(2,1)} fusion(bf16[4096,256]{1,0:T(8,128)(2,1)} %param.10), kind=kLoop, calls=%fused_computation.79 | loop fusion | bytes 4194304
  12.0 1.7 constant_dynamic-slice_fusion.2
  13.8 1.7 collective-permute-start
  15.5 45.8 %collective-permute-done = bf16[2048,512]{1,0:T(8,128)(2,1)S(1)} collective-permute-done((bf16[2048,512]{1,0:T(8,128)(2,1)S(1)}, bf16[2048,512]{1,0:T(8,128)(2,1)S(1)}, u32[]{:S(2)}, u32[]{:S(2)}) %collective-permute-start) | collective-permute-done | bytes 2097184 | tf_op jit(solution)/shard_map/ppermute | solution.py:161
  61.2 1.3 copy-done.2
  63.0 1.3 fusion.9
  65.6 16.9 %all-gather.7.cloned.1.call-done = bf16[4096,512]{1,0:T(8,128)(2,1)} async-done(((bf16[2048,512]{1,0:T(8,128)(2,1)}), bf16[4096,512]{1,0:T(8,128)(2,1)}) %all-gather.7.cloned.1.call-update) | async-done | bytes 4194320 | tf_op jit(solution)/shard_map/all_gather | solution.py:162
  82.5 51.2 %all-gather.5.cloned.1.call-done = bf16[1,512,4096]{2,1,0:T(8,128)(2,1)} async-done(((bf16[1,128,4096]{2,1,0:T(8,128)(2,1)}), bf16[1,512,4096]{2,1,0:T(8,128)(2,1)}) %all-gather.5.cloned.1.call-update) | async-done | bytes 4194320 | tf_op jit(solution)/shard_map/all_gather | solution.py:163
  133.7 6.0 %fusion.3 = f32[512,512]{0,1:T(8,128)S(1)} fusion(bf16[4096,512]{1,0:T(8,128)(2,1)} %all-gather.7.cloned.1.call-done, bf16[1,512,4096]{2,1,0:T(8,128)(2,1)} %all-gather.5.cloned.1.call-done), kind=kOutput, calls=%fused_computation.4 | convolution fusion | flops 2147483648 | bytes 9437184 | tf_op jit(solution)/shard_map/dot_general | solution.py:170
  139.8 2.4 fusion.5
  144.1 1.1 subtract_convert_fusion.1
  145.3 1.4 pad_maximum_fusion.4
  147.2 1.3 fusion.28
  148.6 2.4 collective-permute-start.1
  151.4 12.7 %collective-permute-done.1 = bf16[512,512]{1,0:T(8,128)(2,1)S(1)} collective-permute-done((bf16[512,512]{1,0:T(8,128)(2,1)S(1)}, bf16[512,512]{1,0:T(8,128)(2,1)S(1)}, u32[]{:S(2)}, u32[]{:S(2)}) %collective-permute-start.1) | collective-permute-done | bytes 524320 | tf_op jit(solution)/shard_map/ppermute | solution.py:179
  165.3 1.3 constant_dynamic-slice_fusion.3
  166.6 1.6 collective-permute-start.3
  169.5 21.2 %collective-permute-done.3 = bf16[128,4096]{1,0:T(8,128)(2,1)S(1)} collective-permute-done((bf16[128,4096]{1,0:T(8,128)(2,1)S(1)}, bf16[128,4096]{1,0:T(8,128)(2,1)S(1)}, u32[]{:S(2)}, u32[]{:S(2)}) %collective-permute-start.3) | collective-permute-done | bytes 1048608 | tf_op jit(solution)/shard_map/ppermute | solution.py:202
  196.4 21.4 %all-gather.9.cloned.1.call-done.k_ref.v_ref = bf16[2,16384,128]{2,1,0:T(8,128)(2,1)} async-done(((bf16[2,1024,128]{2,1,0:T(8,128)(2,1)}), bf16[2,16384,128]{2,1,0:T(8,128)(2,1)}) %all-gather.9.cloned.1.call-update) | async-done | bytes 8388624 | tf_op jit(solution)/shard_map/all_gather | solution.py:185
  217.9 30.7 %shard_map.82 = bf16[1024,256]{1,0:T(8,128)(2,1)} custom-call(s32[2,9]{1,0:T(2,128)} %copy.58.tbl_ref, s32[2,9]{1,0:T(2,128)} %copy-done.11, s32[2]{0:T(128)} %copy-done.12, bf16[1024,256]{1,0:T(8,128)(2,1)} %fusion.12.q_ref, s32[1024,1]{1,0:T(8,128)} %fusion.11.qpos_ref, s32[1024,1]{1,0:T(8,128)} %copy.59.qstart_ref, ...), custom_call_target="tpu_custom_call" | custom-call | flops 4831838208 | bytes 5767168 | tf_op jit(solution)/shard_map/pallas_call | solution.py:91
  249.6 2.3 collective-permute-start.2
  251.9 5.7 %collective-permute-done.2 = bf16[512,256]{1,0:T(8,128)(2,1)S(1)} collective-permute-done((bf16[512,256]{1,0:T(8,128)(2,1)S(1)}, bf16[512,256]{1,0:T(8,128)(2,1)S(1)}, u32[]{:S(2)}, u32[]{:S(2)}) %collective-permute-start.2) | collective-permute-done | bytes 262176 | tf_op jit(solution)/shard_map/ppermute | solution.py:206
  257.6 5.9 %convolution_convert_fusion = bf16[512,4096]{1,0:T(8,128)(2,1)} fusion(bf16[256,4096]{1,0:T(8,128)(2,1)} %all-gather.11.cloned.1.call-done, bf16[256,4096]{1,0:T(8,128)(2,1)S(1)} %copy-done.9, bf16[512,256]{1,0:T(8,128)(2,1)S(1)} %collective-permute-done.2, bf16[512,256]{1,0:T(8,128)(2,1)S(1)} %get-tuple-element.15), kind=kOutput, calls=%fused_computation | convolution fusion | flops 2159017984 | bytes 8912896 | tf_op jit(solution)/shard_map/dot_general | solution.py:207
  263.5 51.8 %reduce-scatter.2.cloned.1.call-done = bf16[128,4096]{1,0:T(8,128)(2,1)} async-done(((bf16[512,4096]{1,0:T(8,128)(2,1)}), bf16[128,4096]{1,0:T(8,128)(2,1)}) %reduce-scatter.2.cloned.1.call-update) | async-done | bytes 1048592 | tf_op jit(solution)/shard_map/reduce_scatter | solution.py:212
  (106 shorter events, 15.9 us)
Async XLA Ops:
  6.5 3.3 %copy-start.3 = (bf16[4096,128]{1,0:T(8,128)(2,1)S(1)}, bf16[4096,128]{1,0:T(8,128)(2,1)}, u32[]{:S(2)}) copy-start(bf16[4096,128]{1,0:T(8,128)(2,1)} %param.11) | copy-start | bytes 3145732
  6.5 4.4 %copy-start.4 = (bf16[4096,128]{1,0:T(8,128)(2,1)S(1)}, bf16[4096,128]{1,0:T(8,128)(2,1)}, u32[]{:S(2)}) copy-start(bf16[4096,128]{1,0:T(8,128)(2,1)} %param.12) | copy-start | bytes 3145732
  6.5 76.0 %all-gather.7.cloned.1.call-start = ((), (), s32[]{:S(2)}) async-start(), calls=%async_computation.2 | async-start | bytes 6291456 | tf_op jit(solution)/shard_map/all_gather | solution.py:162
  10.9 51.7 %copy-start = (bf16[1,128,4096]{2,1,0:T(8,128)(2,1)S(1)}, bf16[1,128,4096]{2,1,0:T(8,128)(2,1)}, u32[]{:S(2)}) copy-start(bf16[1,128,4096]{2,1,0:T(8,128)(2,1)} %param.8) | copy-start | bytes 3145732
  12.0 50.9 %copy-start.10 = (f32[4096]{0:T(1024)S(1)}, f32[4096]{0:T(1024)}, u32[]{:S(2)}) copy-start(f32[4096]{0:T(1024)} %param.9) | copy-start | bytes 49156
  13.8 50.6 %copy-start.14 = (s32[32]{0:T(128)S(1)}, s32[32]{0:T(128)}, u32[]{:S(2)}) copy-start(s32[32]{0:T(128)} %param.15) | copy-start | bytes 388
  13.8 47.4 %collective-permute-start = (bf16[2048,512]{1,0:T(8,128)(2,1)S(1)}, bf16[2048,512]{1,0:T(8,128)(2,1)S(1)}, u32[]{:S(2)}, u32[]{:S(2)}) collective-permute-start(bf16[2048,512]{1,0:T(8,128)(2,1)S(1)} %constant_dynamic-slice_fusion.2), channel_id=1, source_target_pairs={{0,66},{66,0},{2,64},{64,2},{1,67},{67,1},{3,65},{65,3},{4,70},{70... | collective-permute-start | bytes 6291464 | tf_op jit(solution)/shard_map/ppermute | solution.py:161
  62.6 71.1 %all-gather.5.cloned.1.call-start = ((), (), s32[]{:S(2)}) async-start(), calls=%async_computation.1 | async-start | bytes 5242880 | tf_op jit(solution)/shard_map/all_gather | solution.py:163
  64.3 153.6 %all-gather.9.cloned.1.call-start = ((), (), s32[]{:S(2)}) async-start(), calls=%async_computation.3 | async-start | bytes 8912896 | tf_op jit(solution)/shard_map/all_gather | solution.py:185
  133.7 6.0 %copy-start.1 = (bf16[4096,512]{1,0:T(8,128)(2,1)S(1)}, bf16[4096,512]{1,0:T(8,128)(2,1)}, u32[]{:S(2)}) copy-start(bf16[4096,512]{1,0:T(8,128)(2,1)} %constant_dynamic-update-slice_fusion) | copy-start | bytes 12582916
  133.7 6.0 %copy-start.16 = (bf16[1,512,4096]{2,1,0:T(8,128)(2,1)S(1)}, bf16[1,512,4096]{2,1,0:T(8,128)(2,1)}, u32[]{:S(2)}) copy-start(bf16[1,512,4096]{2,1,0:T(8,128)(2,1)} %all-gather.5.cloned.1.call-done) | copy-start | bytes 12582916
  143.6 3.2 slice-start
  143.6 3.3 %slice-start.1 = ((f32[512,512]{0,1:T(8,128)}), f32[512,128]{0,1:T(8,128)S(1)}, s32[]{:S(2)}) async-start(f32[512,512]{0,1:T(8,128)} %copy-done.7), calls=%async_computation.7 | async-start | bytes 524288 | tf_op jit(solution)/shard_map/slice | solution.py:172
  145.3 5.7 %copy-start.8 = (f32[512,512]{0,1:T(8,128)S(1)}, f32[512,512]{0,1:T(8,128)}, u32[]{:S(2)}) copy-start(f32[512,512]{0,1:T(8,128)} %copy-done.7) | copy-start | bytes 3145732
  148.6 15.4 %collective-permute-start.1 = (bf16[512,512]{1,0:T(8,128)(2,1)S(1)}, bf16[512,512]{1,0:T(8,128)(2,1)S(1)}, u32[]{:S(2)}, u32[]{:S(2)}) collective-permute-start(bf16[512,512]{1,0:T(8,128)(2,1)S(1)} %pad_maximum_fusion.1), channel_id=1, source_target_pairs={{0,64},{64,0},{1,65},{65,1},{2,66},{66,2},{3,67},{67,3},{4,68},{68... | collective-permute-start | bytes 1572872 | tf_op jit(solution)/shard_map/ppermute | solution.py:179
  151.0 17.1 %copy-start.15 = (s32[32]{0:T(128)S(1)}, s32[32]{0:T(128)}, u32[]{:S(2)}) copy-start(s32[32]{0:T(128)} %param.15) | copy-start | bytes 388
  151.1 17.5 %copy-start.13 = (s32[16]{0:T(128)S(1)}, s32[16]{0:T(128)}, u32[]{:S(2)}) copy-start(s32[16]{0:T(128)} %param.14) | copy-start | bytes 196
  165.3 86.6 %all-gather.11.cloned.1.call-start = ((), (), s32[]{:S(2)}) async-start(), calls=%async_computation.4 | async-start | bytes 3145728 | tf_op jit(solution)/shard_map/all_gather | solution.py:201
  166.6 24.1 %collective-permute-start.3 = (bf16[128,4096]{1,0:T(8,128)(2,1)S(1)}, bf16[128,4096]{1,0:T(8,128)(2,1)S(1)}, u32[]{:S(2)}, u32[]{:S(2)}) collective-permute-start(bf16[128,4096]{1,0:T(8,128)(2,1)S(1)} %constant_dynamic-slice_fusion.3), channel_id=1, source_target_pairs={{0,66},{66,0},{2,64},{64,2},{1,67},{67,1},{3,65},{65,3},{4,70},{70... | collective-permute-start | bytes 3145736 | tf_op jit(solution)/shard_map/ppermute | solution.py:202
  191.7 123.5 %reduce-scatter.2.cloned.1.call-start = ((), (), s32[]{:S(2)}) async-start(), calls=%async_computation.5 | async-start | bytes 5242880 | tf_op jit(solution)/shard_map/reduce_scatter | solution.py:212
  192.0 25.9 %copy-start.12 = (s32[2]{0:T(128)}, s32[2]{0:T(128)S(1)}, u32[]{:S(2)}) copy-start(s32[2]{0:T(128)S(1)} %fusion.48.cnt_ref) | copy-start | bytes 28
  192.0 25.8 %copy-start.11 = (s32[2,9]{1,0:T(2,128)}, s32[2,9]{1,0:T(2,128)S(1)}, u32[]{:S(2)}) copy-start(s32[2,9]{1,0:T(2,128)S(1)} %add_minimum_fusion.seq_ref) | copy-start | bytes 220
  196.4 61.1 %copy-start.9 = (bf16[256,4096]{1,0:T(8,128)(2,1)S(1)}, bf16[256,4096]{1,0:T(8,128)(2,1)}, u32[]{:S(2)}) copy-start(bf16[256,4096]{1,0:T(8,128)(2,1)} %param.13) | copy-start | bytes 6291460
  249.6 8.0 %collective-permute-start.2 = (bf16[512,256]{1,0:T(8,128)(2,1)S(1)}, bf16[512,256]{1,0:T(8,128)(2,1)S(1)}, u32[]{:S(2)}, u32[]{:S(2)}) collective-permute-start(bf16[512,256]{1,0:T(8,128)(2,1)S(1)} %get-tuple-element.16), channel_id=1, source_target_pairs={{0,64},{64,0},{1,65},{65,1},{2,66},{66,2},{3,67},{67,3},{4,68},{68... | collective-permute-start | bytes 786440 | tf_op jit(solution)/shard_map/ppermute | solution.py:206
  (4 other events, 5.8 us)
Sparse Core Ops, SparseCore 0:
  62.7 19.7 all-gather.6
  84.2 49.4 all-gather.4
  165.4 52.4 all-gather.8
  219.4 14.3 all-gather.10
  263.6 51.5 reduce-scatter.1

commit v4 on v3

--- a/solution.py
+++ b/solution.py
@@ -158,24 +158,31 @@
     weights = jnp.concatenate([q_weight, k_weight, v_weight], axis=1)
     half_in = weights.shape[0] // 2
     sent_half = lax.dynamic_slice_in_dim(weights, core * half_in, half_in, 0)
+    plane_rows = lax.all_gather(normed, "x", axis=1, tiled=True)
     partner_half = lax.ppermute(sent_half, ("yh", "ylo"), NEIGHBOUR)
-    partner_weights = lax.all_gather(partner_half, "core", axis=0, tiled=True)
-    plane_rows = lax.all_gather(normed, "x", axis=1, tiled=True)
+    plane_rows, partner_half = lax.optimization_barrier((plane_rows, partner_half))
+    other_half = lax.ppermute(partner_half, "core", [(0, 1), (1, 0)])
     half = plane_rows.shape[1]
     flat_rows = plane_rows.reshape(half, model_width)
     all_places = positions(base_row + jnp.arange(tok_dev, dtype=jnp.int32), span_order, span_rows)
     places = lax.dynamic_slice_in_dim(all_places, plane * half, half, 0)
-
-    def project(w):
-        out = jnp.dot(flat_rows, w, preferred_element_type=jnp.float32)
+    rows_mine = lax.dynamic_slice_in_dim(flat_rows, core * half_in, half_in, 1)
+    rows_other = lax.dynamic_slice_in_dim(flat_rows, (1 - core) * half_in, half_in, 1)
+
+    def finish(out):
         q = rotary(out[:, :q_cols].reshape(half, q_heads, head_dim), places)
         k = rotary(out[:, q_cols:q_cols + kv_cols].reshape(half, kv_local, head_dim), places)
         return jnp.concatenate(
             [q.reshape(half, q_cols), k.reshape(half, kv_cols), out[:, q_cols + kv_cols:]], axis=1
         ).astype(jnp.bfloat16)
 
+    def project(w):
+        return finish(jnp.dot(flat_rows, w, preferred_element_type=jnp.float32))
+
     own = project(weights)
-    for_partner = project(partner_weights)
+    for_partner = finish(
+        jnp.dot(rows_mine, partner_half, preferred_element_type=jnp.float32)
+        + jnp.dot(rows_other, other_half, preferred_element_type=jnp.float32))
     received = lax.ppermute(for_partner, "yh", [(0, 1), (1, 0)])
     first = jnp.where(plane == 0, own, received)
     second = jnp.where(plane == 0, received, own)
@@ -196,10 +203,7 @@
         places.astype(jnp.int32)[:, None], query_start.astype(jnp.int32)[:, None],
         gathered,
     )
-    o_half = o_weight.shape[0] // 2
-    o_sent = lax.dynamic_slice_in_dim(o_weight, core * o_half, o_half, 0)
-    partner_o = lax.all_gather(
-        lax.ppermute(o_sent, ("yh", "ylo"), NEIGHBOUR), "core", axis=0, tiled=True)
+    partner_o = lax.ppermute(o_weight, ("yh", "ylo"), NEIGHBOUR)
     half = row_count // 2
     own_rows = lax.dynamic_slice_in_dim(attended, plane * half, half, 0)
     other_rows = lax.dynamic_slice_in_dim(attended, (1 - plane) * half, half, 0)

time: 323 us -> 267 us (0.83)
  waiting for transfers between devices: 227 us -> 181 us
  Pallas kernels: 30.7 us -> 19.5 us
  local copies, waits for them, and re-layouts: 16.7 us -> 9.92 us
  matrix products: 14.2 us -> 18.2 us
    all_gather x1, waiting for transfers between devices: 51.2 us -> 0.01 us  [per_device(): plane_rows = lax.all_gather(normed, 'x', axis=1, tiled=True)]
    all_gather x1, waiting for transfers between devices: 21.4 us -> 47.8 us  [per_device(): gathered = lax.all_gather(kv_pair, CONTEXT, axis=1, tiled=True)]
    ppermute x1 -> x2, waiting for transfers between devices: 21.2 us -> 0.01 us  [the longest x1 0.01 us: per_device(): other_half = lax.ppermute(partner_half, 'core', [(0, 1), (1, 0)])]
    reduce_scatter x1, waiting for transfers between devices: 51.8 us -> 70.3 us  [per_device(): mixed_rows = lax.psum_scatter(mixed, 'x', scatter_dimension=0, tiled=True)]
    all_gather x2 -> x0, waiting for transfers between devices: 16.9 us -> none  [the longest x1 16.9 us: per_device(): partner_weights = lax.all_gather(partner_half, 'core', axis=0, tiled=True)]
    pallas_call x1, Pallas kernels: 30.7 us -> 19.5 us  [span_attention(): pl.pallas_call(kernel, out_shape=jax.ShapeDtypeStruct((rows, q_cols), jnp...]
    unnamed x46 -> x30, local copies, waits for them, and re-layouts: 9.09 us -> 4.73 us
    dot_general x2 -> x3, matrix products: 8.34 us -> 12.3 us  [the longest x1 5.83 us: project(): return finish(jnp.dot(flat_rows, w, preferred_element_type=jnp.float32))]
  transfers between devices with their start and end apart: 9 -> 8, of which waited for: 8 -> 5; matrix products, arithmetic and copies ran while one was open for 4% -> 6% of each run, Pallas kernels for 10% -> 7%
where the time goes in v4:
time: 267 us; the launch traced here: 266 us
  waiting for transfers between devices  181 us (68%)
  Pallas kernels  19.5 us (7%)
  matrix products  18.2 us (7%)
  other arithmetic  14.5 us (5%)
  between operations  13.5 us (5%)
  local copies, waits for them, and re-layouts  9.92 us (4%)
  starting transfers between devices  9.1 us (3%)
    reduce_scatter x1, waiting for transfers between devices, per_device(): mixed_rows = lax.psum_scatter(mixed, 'x', scatter_dimension=0, tiled=True)  70.3 us
    all_gather x1, waiting for transfers between devices, per_device(): gathered = lax.all_gather(kv_pair, CONTEXT, axis=1, tiled=True)  47.8 us
    ppermute x1, waiting for transfers between devices, per_device(): partner_half = lax.ppermute(sent_half, ('yh', 'ylo'), NEIGHBOUR)  45.9 us
    pallas_call x1, Pallas kernels, span_attention(): pl.pallas_call(kernel, out_shape=jax.ShapeDtypeStruct((rows, q_cols), jnp...  19.5 us
    ppermute x1, waiting for transfers between devices, per_device(): received = lax.ppermute(for_partner, 'yh', [(0, 1), (1, 0)])  11.3 us
    dot_general x1, matrix products, per_device(): jnp.dot(jnp.concatenate([own_rows, partner_rows], axis=1), jnp.concatenat...  5.89 us
    dot_general x1, matrix products, project(): return finish(jnp.dot(flat_rows, w, preferred_element_type=jnp.float32))  5.83 us
    ppermute x1, waiting for transfers between devices, per_device(): partner_rows = lax.ppermute(other_rows, 'yh', [(0, 1), (1, 0)])  5.76 us
  transfers between devices with their start and end apart: 8, of which 5 were waited for; matrix products, arithmetic and copies ran while one was open for 6% of the time, Pallas kernels for 7%

profile of v4, /device:TPU:8, one launch (start us, length us, event | category | flops | bytes accessed | tf_op | source)
XLA Modules:
  0.0 265.9 jit_solution(12526297699838640460)
XLA Ops:
  6.5 1.7 fusion.5
  8.2 2.5 fusion.7
  12.3 2.0 copy-done
  14.4 1.7 collective-permute-start
  16.1 45.9 %collective-permute-done = bf16[2048,512]{1,0:T(8,128)(2,1)} collective-permute-done((bf16[2048,512]{1,0:T(8,128)(2,1)S(1)}, bf16[2048,512]{1,0:T(8,128)(2,1)}, u32[]{:S(2)}, u32[]{:S(2)}) %collective-permute-start) | collective-permute-done | bytes 2097184 | tf_op jit(solution)/shard_map/ppermute | solution.py:162
  62.2 1.0 multiply_cosine_fusion.1
  63.2 5.8 %fusion.3 = f32[512,512]{0,1:T(8,128)S(1)} fusion(bf16[4096,512]{1,0:T(8,128)(2,1)} %copy-done, bf16[1,512,4096]{2,1,0:T(8,128)(2,1)} %all-gather.3.cloned.1.call-done), kind=kOutput, calls=%fused_computation.4 | convolution fusion | flops 2147483648 | bytes 9437184 | tf_op jit(solution)/shard_map/dot_general | solution.py:180
  70.6 3.6 %fusion.8 = f32[512,512]{1,0:T(8,128)S(1)} fusion(bf16[2048,512]{1,0:T(8,128)(2,1)} %collective-permute-done.1, bf16[1,512,4096]{2,1,0:T(8,128)(2,1)} %all-gather.3.cloned.1.call-done, s32[]{:T(128)S(6)} %select_n.89), kind=kOutput, calls=%fused_computation.11 | convolution fusion | flops 1073741824 | bytes 5242884 | tf_op jit(solution)/shard_map/dot_general | solution.py:185
  74.2 2.9 %fusion.14 = f32[512,512]{1,0:T(8,128)S(1)} fusion(f32[512,512]{1,0:T(8,128)S(1)} %fusion.8, bf16[2048,512]{1,0:T(8,128)(2,1)} %collective-permute-done, bf16[1,512,4096]{2,1,0:T(8,128)(2,1)S(1)} %copy-done.9, s32[]{:T(128)S(6)} %select_n.84), kind=kOutput, calls=%fused_computation.17 | convolution fusion | flops 1074003968 | bytes 6291460 | tf_op jit(solution)/shard_map/dot_general | solution.py:184
  77.5 1.3 subtract_convert_fusion.1
  78.8 1.4 pad_maximum_fusion.4
  80.3 1.3 fusion.35
  81.8 3.8 %collective-permute-start.2 = (bf16[512,512]{1,0:T(8,128)(2,1)S(1)}, bf16[512,512]{1,0:T(8,128)(2,1)S(1)}, u32[]{:S(2)}, u32[]{:S(2)}) collective-permute-start(bf16[512,512]{1,0:T(8,128)(2,1)S(1)} %pad_maximum_fusion.1), channel_id=1, source_target_pairs={{0,64},{64,0},{1,65},{65,1},{2,66},{66,2},{3,67},{67,3},{4,68},{68... | collective-permute-start | bytes 1572872 | tf_op jit(solution)/shard_map/ppermute | solution.py:186
  86.8 11.3 %collective-permute-done.2 = bf16[512,512]{1,0:T(8,128)(2,1)S(1)} collective-permute-done((bf16[512,512]{1,0:T(8,128)(2,1)S(1)}, bf16[512,512]{1,0:T(8,128)(2,1)S(1)}, u32[]{:S(2)}, u32[]{:S(2)}) %collective-permute-start.2) | collective-permute-done | bytes 524320 | tf_op jit(solution)/shard_map/ppermute | solution.py:186
  99.4 1.4 collective-permute-start.4
  103.9 1.0 copy.51.qstart_ref
  104.9 1.1 fusion.18.qpos_ref
  106.8 47.8 %all-gather.5.cloned.1.call-done.k_ref.v_ref = bf16[2,16384,128]{2,1,0:T(8,128)(2,1)} async-done(((bf16[2,1024,128]{2,1,0:T(8,128)(2,1)}), bf16[2,16384,128]{2,1,0:T(8,128)(2,1)}) %all-gather.5.cloned.1.call-update) | async-done | bytes 8388624 | tf_op jit(solution)/shard_map/all_gather | solution.py:192
  154.6 19.5 %shard_map.82 = bf16[1024,256]{1,0:T(8,128)(2,1)} custom-call(s32[2,9]{1,0:T(2,128)} %copy.50.tbl_ref, s32[2,9]{1,0:T(2,128)} %copy-done.5, s32[2]{0:T(128)} %copy-done.6, bf16[1024,256]{1,0:T(8,128)(2,1)} %fusion.19.q_ref, s32[1024,1]{1,0:T(8,128)} %fusion.18.qpos_ref, s32[1024,1]{1,0:T(8,128)} %copy.51.qstart_ref, ...), custom_call_target="tpu_custom_call" | custom-call | flops 4831838208 | bytes 5767168 | tf_op jit(solution)/shard_map/pallas_call | solution.py:91
  174.1 1.1 constant_dynamic-slice_fusion
  175.2 2.2 collective-permute-start.3
  177.4 5.8 %collective-permute-done.3 = bf16[512,256]{1,0:T(8,128)(2,1)S(1)} collective-permute-done((bf16[512,256]{1,0:T(8,128)(2,1)S(1)}, bf16[512,256]{1,0:T(8,128)(2,1)S(1)}, u32[]{:S(2)}, u32[]{:S(2)}) %collective-permute-start.3) | collective-permute-done | bytes 262176 | tf_op jit(solution)/shard_map/ppermute | solution.py:210
  183.1 5.9 %convolution_convert_fusion = bf16[512,4096]{1,0:T(8,128)(2,1)} fusion(bf16[256,4096]{1,0:T(8,128)(2,1)} %collective-permute-done.4, bf16[256,4096]{1,0:T(8,128)(2,1)S(1)} %copy-done.10, bf16[512,256]{1,0:T(8,128)(2,1)S(1)} %collective-permute-done.3, bf16[512,256]{1,0:T(8,128)(2,1)S(1)} %get-tuple-element.19), kind=kOutput, calls=%fused_computation | convolution fusion | flops 2159017984 | bytes 8912896 | tf_op jit(solution)/shard_map/dot_general | solution.py:211
  189.0 70.3 %reduce-scatter.2.cloned.1.call-done = bf16[128,4096]{1,0:T(8,128)(2,1)} async-done(((bf16[512,4096]{1,0:T(8,128)(2,1)}), bf16[128,4096]{1,0:T(8,128)(2,1)}) %reduce-scatter.2.cloned.1.call-update) | async-done | bytes 1048592 | tf_op jit(solution)/shard_map/reduce_scatter | solution.py:216
  (84 shorter events, 10.2 us)
Async XLA Ops:
  6.5 4.3 %copy-start.1 = (bf16[4096,256]{1,0:T(8,128)(2,1)S(1)}, bf16[4096,256]{1,0:T(8,128)(2,1)}, u32[]{:S(2)}) copy-start(bf16[4096,256]{1,0:T(8,128)(2,1)} %param.10) | copy-start | bytes 6291460
  6.5 4.5 %copy-start.2 = (bf16[4096,128]{1,0:T(8,128)(2,1)S(1)}, bf16[4096,128]{1,0:T(8,128)(2,1)}, u32[]{:S(2)}) copy-start(bf16[4096,128]{1,0:T(8,128)(2,1)} %param.11) | copy-start | bytes 3145732
  6.5 55.4 %all-gather.3.cloned.1.call-start = ((), (), s32[]{:S(2)}) async-start(), calls=%async_computation.1 | async-start | bytes 5242880 | tf_op jit(solution)/shard_map/all_gather | solution.py:161
  10.8 143.8 %all-gather.5.cloned.1.call-start = ((), (), s32[]{:S(2)}) async-start(), calls=%async_computation.2 | async-start | bytes 8912896 | tf_op jit(solution)/shard_map/all_gather | solution.py:192
  10.8 1.2 copy-start.3
  11.0 51.0 %copy-start.8 = (s32[32]{0:T(128)S(1)}, s32[32]{0:T(128)}, u32[]{:S(2)}) copy-start(s32[32]{0:T(128)} %param.15) | copy-start | bytes 388
  12.3 2.0 copy-start
  14.4 47.6 %collective-permute-start = (bf16[2048,512]{1,0:T(8,128)(2,1)S(1)}, bf16[2048,512]{1,0:T(8,128)(2,1)}, u32[]{:S(2)}, u32[]{:S(2)}) collective-permute-start(bf16[2048,512]{1,0:T(8,128)(2,1)S(1)} %constant_dynamic-slice_fusion.1), channel_id=1, source_target_pairs={{0,66},{66,0},{2,64},{64,2},{1,67},{67,1},{3,65},{65,3},{4,70},{70... | collective-permute-start | bytes 6291464 | tf_op jit(solution)/shard_map/ppermute | solution.py:162
  62.0 8.6 %collective-permute-start.1 = (bf16[2048,512]{1,0:T(8,128)(2,1)}, bf16[2048,512]{1,0:T(8,128)(2,1)}, u32[]{:S(2)}, u32[]{:S(2)}) collective-permute-start(bf16[2048,512]{1,0:T(8,128)(2,1)} %collective-permute-done), channel_id=1, source_target_pairs={{0,1},{1,0},{2,3},{3,2},{4,5},{5,4},{6,7},{7,6},{8,9},{9,8},{10,11... | collective-permute-start | bytes 6291464 | tf_op jit(solution)/shard_map/ppermute | solution.py:164
  69.0 1.0 copy-start.4
  70.5 3.6 %copy-start.9 = (bf16[1,512,4096]{2,1,0:T(8,128)(2,1)S(1)}, bf16[1,512,4096]{2,1,0:T(8,128)(2,1)}, u32[]{:S(2)}) copy-start(bf16[1,512,4096]{2,1,0:T(8,128)(2,1)} %all-gather.3.cloned.1.call-done) | copy-start | bytes 12582916
  81.6 19.5 %copy-start.7 = (s32[16]{0:T(128)S(1)}, s32[16]{0:T(128)}, u32[]{:S(2)}) copy-start(s32[16]{0:T(128)} %param.14) | copy-start | bytes 196
  81.8 16.4 %collective-permute-start.2 = (bf16[512,512]{1,0:T(8,128)(2,1)S(1)}, bf16[512,512]{1,0:T(8,128)(2,1)S(1)}, u32[]{:S(2)}, u32[]{:S(2)}) collective-permute-start(bf16[512,512]{1,0:T(8,128)(2,1)S(1)} %pad_maximum_fusion.1), channel_id=1, source_target_pairs={{0,64},{64,0},{1,65},{65,1},{2,66},{66,2},{3,67},{67,3},{4,68},{68... | collective-permute-start | bytes 1572872 | tf_op jit(solution)/shard_map/ppermute | solution.py:186
  99.3 160.0 %reduce-scatter.2.cloned.1.call-start = ((), (), s32[]{:S(2)}) async-start(), calls=%async_computation.3 | async-start | bytes 5242880 | tf_op jit(solution)/shard_map/reduce_scatter | solution.py:216
  99.4 78.0 %collective-permute-start.4 = (bf16[256,4096]{1,0:T(8,128)(2,1)}, bf16[256,4096]{1,0:T(8,128)(2,1)}, u32[]{:S(2)}, u32[]{:S(2)}) collective-permute-start(bf16[256,4096]{1,0:T(8,128)(2,1)} %param.13), channel_id=1, source_target_pairs={{0,66},{66,0},{2,64},{64,2},{1,67},{67,1},{3,65},{65,3},{4,70},{70... | collective-permute-start | bytes 6291464 | tf_op jit(solution)/shard_map/ppermute | solution.py:206
  102.2 52.4 %copy-start.6 = (s32[2]{0:T(128)}, s32[2]{0:T(128)S(1)}, u32[]{:S(2)}) copy-start(s32[2]{0:T(128)S(1)} %fusion.57.cnt_ref) | copy-start | bytes 28
  102.3 52.3 %copy-start.5 = (s32[2,9]{1,0:T(2,128)}, s32[2,9]{1,0:T(2,128)S(1)}, u32[]{:S(2)}) copy-start(s32[2,9]{1,0:T(2,128)S(1)} %add_minimum_fusion.seq_ref) | copy-start | bytes 220
  106.8 76.3 %copy-start.10 = (bf16[256,4096]{1,0:T(8,128)(2,1)S(1)}, bf16[256,4096]{1,0:T(8,128)(2,1)}, u32[]{:S(2)}) copy-start(bf16[256,4096]{1,0:T(8,128)(2,1)} %param.13) | copy-start | bytes 6291460
  175.2 8.0 %collective-permute-start.3 = (bf16[512,256]{1,0:T(8,128)(2,1)S(1)}, bf16[512,256]{1,0:T(8,128)(2,1)S(1)}, u32[]{:S(2)}, u32[]{:S(2)}) collective-permute-start(bf16[512,256]{1,0:T(8,128)(2,1)S(1)} %get-tuple-element.20), channel_id=1, source_target_pairs={{0,64},{64,0},{1,65},{65,1},{2,66},{66,2},{3,67},{67,3},{4,68},{68... | collective-permute-start | bytes 786440 | tf_op jit(solution)/shard_map/ppermute | solution.py:210
Sparse Core Ops, SparseCore 0:
  10.9 50.5 all-gather.2
  99.4 55.1 all-gather.4
  189.2 70.1 reduce-scatter.1

commit v5 on v4

--- a/solution.py
+++ b/solution.py
@@ -113,7 +113,7 @@
     )(tbl, seq, cnt, queries, qpos, qstart, kv, kv)
 
 
-def key_tables(span_order, doc_ends, query_spans):
+def key_tables(span_order, doc_ends, query_spans, cores):
     n_spans = span_order.shape[0]
     span_ids = jnp.arange(n_spans, dtype=jnp.int32)
     inverse = jnp.sum(
@@ -131,8 +131,10 @@
     count = jnp.sum(valid.astype(jnp.int32), axis=1)
     slot = jnp.arange(KEY_SLOTS, dtype=jnp.int32)
     seq = jnp.minimum(sq[:, None] - count[:, None] + 1 + slot[None, :], sq[:, None])
-    tbl = jnp.sum(jnp.where(seq[:, :, None] == span_ids[None, None, :], inverse[None, None, :], 0),
-                  axis=2)
+    storage = jnp.sum(
+        jnp.where(seq[:, :, None] == span_ids[None, None, :], inverse[None, None, :], 0), axis=2)
+    block = storage // 2
+    tbl = ((block % cores) * (n_spans // 2 // cores) + block // cores) * 2 + storage % 2
     return tbl.astype(jnp.int32), seq.astype(jnp.int32), count.astype(jnp.int32)
 
 
@@ -179,17 +181,19 @@
     def project(w):
         return finish(jnp.dot(flat_rows, w, preferred_element_type=jnp.float32))
 
-    own = project(weights)
     for_partner = finish(
         jnp.dot(rows_mine, partner_half, preferred_element_type=jnp.float32)
         + jnp.dot(rows_other, other_half, preferred_element_type=jnp.float32))
     received = lax.ppermute(for_partner, "yh", [(0, 1), (1, 0)])
+    flat_rows, for_partner = lax.optimization_barrier((flat_rows, for_partner))
+    own = project(weights)
     first = jnp.where(plane == 0, own, received)
     second = jnp.where(plane == 0, received, own)
     projected = jnp.concatenate([first, second], axis=0)
     query_rows = projected[:, :q_cols]
     kv_pair = jnp.stack([projected[:, q_cols:q_cols + kv_cols], projected[:, q_cols + kv_cols:]])
-    gathered = lax.all_gather(kv_pair, CONTEXT, axis=1, tiled=True)
+    gathered = lax.all_gather(
+        lax.all_gather(kv_pair, ("z", "ylo"), axis=1, tiled=True), "core", axis=1, tiled=True)
     places = all_places
     row_count = tok_dev
 
@@ -197,7 +201,7 @@
     query_start = jnp.max(
         jnp.where(doc_ends[None, :] <= places[:, None], doc_ends[None, :], 0), axis=1)
     query_spans = lax.axis_index(CONTEXT) * 2 + jnp.arange(2, dtype=jnp.int32)
-    tbl, seq, cnt = key_tables(span_order, doc_ends, query_spans)
+    tbl, seq, cnt = key_tables(span_order, doc_ends, query_spans, lax.axis_size("core"))
     attended = span_attention(
         tbl, seq, cnt, query_rows,
         places.astype(jnp.int32)[:, None], query_start.astype(jnp.int32)[:, None],

time: 267 us -> 319 us (1.19)
  waiting for transfers between devices: 181 us -> 229 us
  Pallas kernels: 19.5 us -> 25 us
    all_gather x1 -> x2, waiting for transfers between devices: 47.8 us -> 110 us  [the longest x1 92.9 us: per_device(): lax.all_gather(kv_pair, ('z', 'ylo'), axis=1, tiled=True)]
    reduce_scatter x1, waiting for transfers between devices: 70.3 us -> 60.3 us  [per_device(): mixed_rows = lax.psum_scatter(mixed, 'x', scatter_dimension=0, tiled=True)]
    ppermute x1, waiting for transfers between devices: 11.3 us -> 4.28 us  [per_device(): received = lax.ppermute(for_partner, 'yh', [(0, 1), (1, 0)])]
    pallas_call x1, Pallas kernels: 19.5 us -> 25 us  [span_attention(): pl.pallas_call(kernel, out_shape=jax.ShapeDtypeStruct((rows, q_cols), jnp...]
  transfers between devices with their start and end apart: 8 -> 9, of which waited for: 5 -> 7; matrix products, arithmetic and copies ran while one was open for 6% -> 5% of each run, Pallas kernels for 7% -> 8%
where the time goes in v5:
time: 319 us; the launch traced here: 318 us
  waiting for transfers between devices  229 us (72%)
  Pallas kernels  25 us (8%)
  other arithmetic  17 us (5%)
  matrix products  15.9 us (5%)
  between operations  13.5 us (4%)
  starting transfers between devices  9.94 us (3%)
  local copies, waits for them, and re-layouts  7.64 us (2%)
    all_gather x1, waiting for transfers between devices, per_device(): lax.all_gather(kv_pair, ('z', 'ylo'), axis=1, tiled=True)  92.9 us
    reduce_scatter x1, waiting for transfers between devices, per_device(): mixed_rows = lax.psum_scatter(mixed, 'x', scatter_dimension=0, tiled=True)  60.3 us
    ppermute x1, waiting for transfers between devices, per_device(): partner_half = lax.ppermute(sent_half, ('yh', 'ylo'), NEIGHBOUR)  45.8 us
    pallas_call x1, Pallas kernels, span_attention(): pl.pallas_call(kernel, out_shape=jax.ShapeDtypeStruct((rows, q_cols), jnp...  25 us
    all_gather x1, waiting for transfers between devices, per_device(): lax.all_gather(lax.all_gather(kv_pair, ('z', 'ylo'), axis=1, tiled=True),...  16.7 us
    dot_general x1, matrix products, per_device(): jnp.dot(jnp.concatenate([own_rows, partner_rows], axis=1), jnp.concatenat...  6.55 us
  transfers between devices with their start and end apart: 9, of which 7 were waited for; matrix products, arithmetic and copies ran while one was open for 5% of the time, Pallas kernels for 8%

profile of v5, /device:TPU:8, one launch (start us, length us, event | category | flops | bytes accessed | tf_op | source)
XLA Modules:
  0.0 317.9 jit_solution(3584198243696089896)
XLA Ops:
  6.5 1.7 fusion.3
  8.2 2.5 fusion.5
  12.3 2.0 copy-done
  14.4 1.7 collective-permute-start
  16.1 45.8 %collective-permute-done = bf16[2048,512]{1,0:T(8,128)(2,1)S(1)} collective-permute-done((bf16[2048,512]{1,0:T(8,128)(2,1)S(1)}, bf16[2048,512]{1,0:T(8,128)(2,1)S(1)}, u32[]{:S(2)}, u32[]{:S(2)}) %collective-permute-start) | collective-permute-done | bytes 2097184 | tf_op jit(solution)/shard_map/ppermute | solution.py:164
  63.1 3.1 collective-permute-done.1
  66.2 3.5 %fusion.6 = f32[512,512]{1,0:T(8,128)S(1)} fusion(bf16[2048,512]{1,0:T(8,128)(2,1)} %collective-permute-done.1, bf16[1,512,4096]{2,1,0:T(8,128)(2,1)} %all-gather.4.cloned.1.call-done, s32[]{:T(128)S(6)} %select_n.107), kind=kOutput, calls=%fused_computation.9 | convolution fusion | flops 1073741824 | bytes 5242884 | tf_op jit(solution)/shard_map/dot_general | solution.py:186
  69.6 1.3 fusion.12
  72.9 1.2 fusion.33
  75.1 3.5 %collective-permute-start.2 = (bf16[512,512]{1,0:T(8,128)(2,1)}, bf16[512,512]{1,0:T(8,128)(2,1)S(1)}, u32[]{:S(2)}, u32[]{:S(2)}) collective-permute-start(bf16[512,512]{1,0:T(8,128)(2,1)} %pad_maximum_fusion), channel_id=1, source_target_pairs={{0,64},{64,0},{1,65},{65,1},{2,66},{66,2},{3,67},{67,3},{4,68},{68... | collective-permute-start | bytes 1572872 | tf_op jit(solution)/shard_map/ppermute | solution.py:187
  78.6 4.6 %fusion.61 = f32[512,512]{0,1:T(8,128)S(1)} fusion(bf16[512,4096]{1,0:T(8,128)(2,1)} %bitcast.46, bf16[4096,512]{1,0:T(8,128)(2,1)S(1)} %copy-done.1), kind=kOutput, calls=%fused_computation.137 | convolution fusion | flops 2147483648 | bytes 9437184 | tf_op jit(solution)/shard_map/dot_general | solution.py:182
  85.4 1.2 fusion.37
  86.8 4.3 %collective-permute-done.2 = bf16[512,512]{1,0:T(8,128)(2,1)S(1)} collective-permute-done((bf16[512,512]{1,0:T(8,128)(2,1)}, bf16[512,512]{1,0:T(8,128)(2,1)S(1)}, u32[]{:S(2)}, u32[]{:S(2)}) %collective-permute-start.2) | collective-permute-done | bytes 524320 | tf_op jit(solution)/shard_map/ppermute | solution.py:187
  92.3 92.9 %all-gather.6.cloned.1.call-done = bf16[2,8192,128]{2,1,0:T(8,128)(2,1)} async-done(((bf16[2,1024,128]{2,1,0:T(8,128)(2,1)}), bf16[2,8192,128]{2,1,0:T(8,128)(2,1)}) %all-gather.6.cloned.1.call-update) | async-done | bytes 4194320 | tf_op jit(solution)/shard_map/all_gather | solution.py:196
  185.3 2.5 collective-permute-start.4
  190.3 1.0 copy.57.qstart_ref
  191.9 1.1 fusion.16.qpos_ref
  193.8 16.7 %all-gather.8.cloned.1.call-done.k_ref.v_ref = bf16[2,16384,128]{2,1,0:T(8,128)(2,1)} async-done(((bf16[2,8192,128]{2,1,0:T(8,128)(2,1)}), bf16[2,16384,128]{2,1,0:T(8,128)(2,1)}) %all-gather.8.cloned.1.call-update) | async-done | bytes 8388624 | tf_op jit(solution)/shard_map/all_gather | solution.py:195
  210.5 25.0 %shard_map.82 = bf16[1024,256]{1,0:T(8,128)(2,1)} custom-call(s32[2,9]{1,0:T(2,128)} %fusion.58.tbl_ref, s32[2,9]{1,0:T(2,128)} %copy-done.5, s32[2]{0:T(128)} %copy-done.6, bf16[1024,256]{1,0:T(8,128)(2,1)} %fusion.17.q_ref, s32[1024,1]{1,0:T(8,128)} %fusion.16.qpos_ref, s32[1024,1]{1,0:T(8,128)} %copy.57.qstart_ref, ...), custom_call_target="tpu_custom_call" | custom-call | flops 4831838208 | bytes 5767168 | tf_op jit(solution)/shard_map/pallas_call | solution.py:91
  235.5 1.1 constant_dynamic-slice_fusion
  236.6 2.2 collective-permute-start.3
  238.8 5.8 %collective-permute-done.3 = bf16[512,256]{1,0:T(8,128)(2,1)S(1)} collective-permute-done((bf16[512,256]{1,0:T(8,128)(2,1)S(1)}, bf16[512,256]{1,0:T(8,128)(2,1)S(1)}, u32[]{:S(2)}, u32[]{:S(2)}) %collective-permute-start.3) | collective-permute-done | bytes 262176 | tf_op jit(solution)/shard_map/ppermute | solution.py:214
  244.6 6.5 %convolution_convert_fusion = bf16[512,4096]{1,0:T(8,128)(2,1)} fusion(bf16[256,4096]{1,0:T(8,128)(2,1)} %collective-permute-done.4, bf16[256,4096]{1,0:T(8,128)(2,1)} %param.13, bf16[512,256]{1,0:T(8,128)(2,1)S(1)} %collective-permute-done.3, bf16[512,256]{1,0:T(8,128)(2,1)S(1)} %get-tuple-element.21), kind=kOutput, calls=%fused_computation | convolution fusion | flops 2159017984 | bytes 8912896 | tf_op jit(solution)/shard_map/dot_general | solution.py:215
  251.1 60.3 %reduce-scatter.2.cloned.1.call-done = bf16[128,4096]{1,0:T(8,128)(2,1)} async-done(((bf16[512,4096]{1,0:T(8,128)(2,1)}), bf16[128,4096]{1,0:T(8,128)(2,1)}) %reduce-scatter.2.cloned.1.call-update) | async-done | bytes 1048592 | tf_op jit(solution)/shard_map/reduce_scatter | solution.py:220
  (89 shorter events, 13.1 us)
Async XLA Ops:
  6.5 4.3 %copy-start.2 = (bf16[4096,256]{1,0:T(8,128)(2,1)S(1)}, bf16[4096,256]{1,0:T(8,128)(2,1)}, u32[]{:S(2)}) copy-start(bf16[4096,256]{1,0:T(8,128)(2,1)} %param.10) | copy-start | bytes 6291460
  6.5 4.5 %copy-start.3 = (bf16[4096,128]{1,0:T(8,128)(2,1)S(1)}, bf16[4096,128]{1,0:T(8,128)(2,1)}, u32[]{:S(2)}) copy-start(bf16[4096,128]{1,0:T(8,128)(2,1)} %param.11) | copy-start | bytes 3145732
  6.5 55.3 %all-gather.4.cloned.1.call-start = ((), (), s32[]{:S(2)}) async-start(), calls=%async_computation.1 | async-start | bytes 5242880 | tf_op jit(solution)/shard_map/all_gather | solution.py:163
  10.8 174.4 %all-gather.6.cloned.1.call-start = ((), (), s32[]{:S(2)}) async-start(), calls=%async_computation.2 | async-start | bytes 4718592 | tf_op jit(solution)/shard_map/all_gather | solution.py:196
  10.8 1.2 copy-start.4
  11.0 50.9 %copy-start.8 = (s32[32]{0:T(128)S(1)}, s32[32]{0:T(128)}, u32[]{:S(2)}) copy-start(s32[32]{0:T(128)} %param.15) | copy-start | bytes 388
  12.3 2.0 copy-start
  14.4 47.4 %collective-permute-start = (bf16[2048,512]{1,0:T(8,128)(2,1)S(1)}, bf16[2048,512]{1,0:T(8,128)(2,1)S(1)}, u32[]{:S(2)}, u32[]{:S(2)}) collective-permute-start(bf16[2048,512]{1,0:T(8,128)(2,1)S(1)} %constant_dynamic-slice_fusion.1), channel_id=1, source_target_pairs={{0,66},{66,0},{2,64},{64,2},{1,67},{67,1},{3,65},{65,3},{4,70},{70... | collective-permute-start | bytes 6291464 | tf_op jit(solution)/shard_map/ppermute | solution.py:164
  61.9 4.3 %collective-permute-start.1 = (bf16[2048,512]{1,0:T(8,128)(2,1)S(1)}, bf16[2048,512]{1,0:T(8,128)(2,1)}, u32[]{:S(2)}, u32[]{:S(2)}) collective-permute-start(bf16[2048,512]{1,0:T(8,128)(2,1)S(1)} %collective-permute-done), channel_id=1, source_target_pairs={{0,1},{1,0},{2,3},{3,2},{4,5},{5,4},{6,7},{7,6},{8,9},{9,8},{10,11... | collective-permute-start | bytes 6291464 | tf_op jit(solution)/shard_map/ppermute | solution.py:166
  61.9 7.8 %copy-start.9 = (bf16[1,512,4096]{2,1,0:T(8,128)(2,1)S(1)}, bf16[1,512,4096]{2,1,0:T(8,128)(2,1)}, u32[]{:S(2)}) copy-start(bf16[1,512,4096]{2,1,0:T(8,128)(2,1)} %all-gather.4.cloned.1.call-done) | copy-start | bytes 12582916
  71.3 7.3 %copy-start.1 = (bf16[4096,512]{1,0:T(8,128)(2,1)S(1)}, bf16[4096,512]{1,0:T(8,128)(2,1)}, u32[]{:S(2)}) copy-start(bf16[4096,512]{1,0:T(8,128)(2,1)} %copy-done) | copy-start | bytes 12582916
  75.1 15.9 %collective-permute-start.2 = (bf16[512,512]{1,0:T(8,128)(2,1)}, bf16[512,512]{1,0:T(8,128)(2,1)S(1)}, u32[]{:S(2)}, u32[]{:S(2)}) collective-permute-start(bf16[512,512]{1,0:T(8,128)(2,1)} %pad_maximum_fusion), channel_id=1, source_target_pairs={{0,64},{64,0},{1,65},{65,1},{2,66},{66,2},{3,67},{67,3},{4,68},{68... | collective-permute-start | bytes 1572872 | tf_op jit(solution)/shard_map/ppermute | solution.py:187
  91.3 96.8 %copy-start.7 = (s32[16]{0:T(128)S(1)}, s32[16]{0:T(128)}, u32[]{:S(2)}) copy-start(s32[16]{0:T(128)} %param.14) | copy-start | bytes 196
  92.2 118.3 %all-gather.8.cloned.1.call-start = ((), (), s32[]{:S(2)}) async-start(), calls=%async_computation.3 | async-start | bytes 12582912 | tf_op jit(solution)/shard_map/all_gather | solution.py:195
  185.2 126.2 %reduce-scatter.2.cloned.1.call-start = ((), (), s32[]{:S(2)}) async-start(), calls=%async_computation.4 | async-start | bytes 5242880 | tf_op jit(solution)/shard_map/reduce_scatter | solution.py:220
  185.3 53.5 %collective-permute-start.4 = (bf16[256,4096]{1,0:T(8,128)(2,1)}, bf16[256,4096]{1,0:T(8,128)(2,1)}, u32[]{:S(2)}, u32[]{:S(2)}) collective-permute-start(bf16[256,4096]{1,0:T(8,128)(2,1)} %param.13), channel_id=1, source_target_pairs={{0,66},{66,0},{2,64},{64,2},{1,67},{67,1},{3,65},{65,3},{4,70},{70... | collective-permute-start | bytes 6291464 | tf_op jit(solution)/shard_map/ppermute | solution.py:210
  189.2 21.3 %copy-start.6 = (s32[2]{0:T(128)}, s32[2]{0:T(128)S(1)}, u32[]{:S(2)}) copy-start(s32[2]{0:T(128)S(1)} %fusion.55.cnt_ref) | copy-start | bytes 28
  189.3 21.2 %copy-start.5 = (s32[2,9]{1,0:T(2,128)}, s32[2,9]{1,0:T(2,128)S(1)}, u32[]{:S(2)}) copy-start(s32[2,9]{1,0:T(2,128)S(1)} %add_minimum_fusion.seq_ref) | copy-start | bytes 220
  236.6 8.0 %collective-permute-start.3 = (bf16[512,256]{1,0:T(8,128)(2,1)S(1)}, bf16[512,256]{1,0:T(8,128)(2,1)S(1)}, u32[]{:S(2)}, u32[]{:S(2)}) collective-permute-start(bf16[512,256]{1,0:T(8,128)(2,1)S(1)} %get-tuple-element.22), channel_id=1, source_target_pairs={{0,64},{64,0},{1,65},{65,1},{2,66},{66,2},{3,67},{67,3},{4,68},{68... | collective-permute-start | bytes 786440 | tf_op jit(solution)/shard_map/ppermute | solution.py:214
Sparse Core Ops, SparseCore 0:
  10.9 50.5 all-gather.3
  92.3 92.8 all-gather.5
  186.8 23.6 all-gather.7
  251.3 60.0 reduce-scatter.1

commit v6 on v4

--- a/solution.py
+++ b/solution.py
@@ -131,9 +131,31 @@
     count = jnp.sum(valid.astype(jnp.int32), axis=1)
     slot = jnp.arange(KEY_SLOTS, dtype=jnp.int32)
     seq = jnp.minimum(sq[:, None] - count[:, None] + 1 + slot[None, :], sq[:, None])
-    tbl = jnp.sum(jnp.where(seq[:, :, None] == span_ids[None, None, :], inverse[None, None, :], 0),
-                  axis=2)
-    return tbl.astype(jnp.int32), seq.astype(jnp.int32), count.astype(jnp.int32)
+    storage = jnp.sum(
+        jnp.where(seq[:, :, None] == span_ids[None, None, :], inverse[None, None, :], 0), axis=2)
+    return storage.astype(jnp.int32), seq.astype(jnp.int32), count.astype(jnp.int32)
+
+
+def shift_x(value, d, n):
+    return lax.ppermute(value, "x", [(i, (i + d) % n) for i in range(n)])
+
+
+def gather_x(chunk):
+    n = lax.axis_size("x")
+    me = lax.axis_index("x")
+    from_right = jnp.stack([chunk] + [shift_x(chunk, n - e, n) for e in range(1, n)])
+    order = (jnp.arange(n, dtype=jnp.int32) - me) % n
+    return jnp.take(from_right, order, axis=0).reshape(n * chunk.shape[0], *chunk.shape[1:])
+
+
+def reduce_scatter_x(value):
+    n = lax.axis_size("x")
+    me = lax.axis_index("x")
+    parts = value.reshape(n, value.shape[0] // n, *value.shape[1:])
+    total = jnp.take(parts, me, axis=0).astype(jnp.float32)
+    for d in range(1, n):
+        total = total + shift_x(jnp.take(parts, (me + d) % n, axis=0), d, n).astype(jnp.float32)
+    return total.astype(value.dtype)
 
 
 def per_device(tokens, norm_gain, q_weight, k_weight, v_weight, o_weight, doc_lengths, span_order):
@@ -158,7 +180,7 @@
     weights = jnp.concatenate([q_weight, k_weight, v_weight], axis=1)
     half_in = weights.shape[0] // 2
     sent_half = lax.dynamic_slice_in_dim(weights, core * half_in, half_in, 0)
-    plane_rows = lax.all_gather(normed, "x", axis=1, tiled=True)
+    plane_rows = gather_x(normed[0])[None]
     partner_half = lax.ppermute(sent_half, ("yh", "ylo"), NEIGHBOUR)
     plane_rows, partner_half = lax.optimization_barrier((plane_rows, partner_half))
     other_half = lax.ppermute(partner_half, "core", [(0, 1), (1, 0)])
@@ -179,11 +201,12 @@
     def project(w):
         return finish(jnp.dot(flat_rows, w, preferred_element_type=jnp.float32))
 
-    own = project(weights)
     for_partner = finish(
         jnp.dot(rows_mine, partner_half, preferred_element_type=jnp.float32)
         + jnp.dot(rows_other, other_half, preferred_element_type=jnp.float32))
     received = lax.ppermute(for_partner, "yh", [(0, 1), (1, 0)])
+    flat_rows, for_partner = lax.optimization_barrier((flat_rows, for_partner))
+    own = project(weights)
     first = jnp.where(plane == 0, own, received)
     second = jnp.where(plane == 0, received, own)
     projected = jnp.concatenate([first, second], axis=0)
@@ -213,7 +236,7 @@
         jnp.concatenate([o_weight, partner_o], axis=0),
         preferred_element_type=jnp.float32,
     ).astype(jnp.bfloat16)
-    mixed_rows = lax.psum_scatter(mixed, "x", scatter_dimension=0, tiled=True)
+    mixed_rows = reduce_scatter_x(mixed)
     return mixed_rows.reshape(tokens.shape)
 
 

time: 267 us -> 268 us (level)
  the two profiles are of different devices: /device:TPU:8 before, /device:TPU:96 now
where the time goes in v6:
time: 268 us
  waiting for transfers between devices  140 us (52%)
  Pallas kernels  30.5 us (11%)
  other arithmetic  29.1 us (11%)
  starting transfers between devices  21.8 us (8%)
  local copies, waits for them, and re-layouts  18.3 us (7%)
  matrix products  14.9 us (6%)
  between operations  13.8 us (5%)
    ppermute x6, waiting for transfers between devices, shift_x(): return lax.ppermute(value, 'x', [(i, (i + d) % n) for i in range(n)])  82.7 us
    all_gather x1, waiting for transfers between devices, per_device(): gathered = lax.all_gather(kv_pair, CONTEXT, axis=1, tiled=True)  42.2 us
    pallas_call x1, Pallas kernels, span_attention(): pl.pallas_call(kernel, out_shape=jax.ShapeDtypeStruct((rows, q_cols), jnp...  30.5 us
    ppermute x6, starting transfers between devices, shift_x(): return lax.ppermute(value, 'x', [(i, (i + d) % n) for i in range(n)])  9.58 us
    ppermute x1, waiting for transfers between devices, per_device(): partner_rows = lax.ppermute(other_rows, 'yh', [(0, 1), (1, 0)])  7.21 us
    unnamed x30, local copies, waits for them, and re-layouts  5.39 us
  transfers between devices with their start and end apart: 12, of which 8 were waited for; matrix products, arithmetic and copies ran while one was open for 14% of the time, Pallas kernels for 11%

profile of v6, /device:TPU:96, one launch (start us, length us, event | category | flops | bytes accessed | tf_op | source)
XLA Modules:
  0.0 267.9 jit_solution(16541171522421706287)
XLA Ops:
  8.2 2.5 fusion.67
  10.8 2.8 %collective-permute-start = (bf16[128,4096]{1,0:T(8,128)(2,1)}, bf16[128,4096]{1,0:T(8,128)(2,1)}, u32[]{:S(2)}, u32[]{:S(2)}) collective-permute-start(bf16[128,4096]{1,0:T(8,128)(2,1)} %fusion.67), channel_id=1, source_target_pairs={{0,48},{16,0},{32,16},{48,32},{1,49},{17,1},{33,17},{49,33},{2,50}... | collective-permute-start | bytes 3145736 | tf_op jit(solution)/shard_map/ppermute | solution.py:140
  21.9 3.1 %collective-permute-start.3 = (bf16[2048,512]{1,0:T(8,128)(2,1)S(1)}, bf16[2048,512]{1,0:T(8,128)(2,1)}, u32[]{:S(2)}, u32[]{:S(2)}) collective-permute-start(bf16[2048,512]{1,0:T(8,128)(2,1)S(1)} %constant_dynamic-slice_fusion.2), channel_id=1, source_target_pairs={{0,66},{66,0},{2,64},{64,2},{1,67},{67,1},{3,65},{65,3},{4,70},{70... | collective-permute-start | bytes 6291464 | tf_op jit(solution)/shard_map/ppermute | solution.py:184
  25.5 33.3 %collective-permute-done = bf16[128,4096]{1,0:T(8,128)(2,1)} collective-permute-done((bf16[128,4096]{1,0:T(8,128)(2,1)}, bf16[128,4096]{1,0:T(8,128)(2,1)}, u32[]{:S(2)}, u32[]{:S(2)}) %collective-permute-start) | collective-permute-done | bytes 1048608 | tf_op jit(solution)/shard_map/ppermute | solution.py:140
  58.8 3.7 %collective-permute-done.2 = bf16[128,4096]{1,0:T(8,128)(2,1)} collective-permute-done((bf16[128,4096]{1,0:T(8,128)(2,1)}, bf16[128,4096]{1,0:T(8,128)(2,1)}, u32[]{:S(2)}, u32[]{:S(2)}) %collective-permute-start.2) | collective-permute-done | bytes 1048608 | tf_op jit(solution)/shard_map/ppermute | solution.py:140
  62.4 3.6 %pad_maximum_fusion = bf16[4,128,4096]{2,1,0:T(8,128)(2,1)} fusion(bf16[1,128,4096]{2,1,0:T(8,128)(2,1)} %bitcast.5, bf16[1,128,4096]{2,1,0:T(8,128)(2,1)} %bitcast.4, bf16[1,128,4096]{2,1,0:T(8,128)(2,1)} %bitcast.3, bf16[1,128,4096]{2,1,0:T(8,128)(2,1)S(1)} %fusion.5), kind=kLoop, calls=%fused_computation.2 | loop fusion | flops 6291456 | bytes 8388608 | tf_op jit(solution)/shard_map/stack | solution.py:146
  66.0 5.0 %gather_fusion = bf16[4,128,4096]{2,1,0:T(8,128)(2,1)} fusion(bf16[4,128,4096]{2,1,0:T(8,128)(2,1)} %pad_maximum_fusion, s32[1024]{0:T(1024)S(1)} %pad_clamp_fusion), kind=kCustom, calls=%fused_computation | custom fusion | bytes 8388624 | tf_op jit(solution)/shard_map/jit(_take)/gather | solution.py:148
  71.0 4.6 %bitcast_select_fusion = bf16[1,512,4096]{2,1,0:T(8,128)(2,1)} fusion(pred[512]{0:T(512)(128)(4,1)S(1)} %broadcast_bitcast_fusion, bf16[1,512,4096]{2,1,0:T(8,128)(2,1)} %bitcast.59), kind=kLoop, calls=%fused_computation.6 | loop fusion | flops 2097152 | bytes 8389120 | tf_op jit(solution)/shard_map/jit(_take)/select_n | solution.py:148
  76.8 3.1 %collective-permute-done.4 = bf16[2048,512]{1,0:T(8,128)(2,1)S(1)} collective-permute-done((bf16[2048,512]{1,0:T(8,128)(2,1)}, bf16[2048,512]{1,0:T(8,128)(2,1)S(1)}, u32[]{:S(2)}, u32[]{:S(2)}) %collective-permute-start.4) | collective-permute-done | bytes 2097184 | tf_op jit(solution)/shard_map/ppermute | solution.py:186
  79.9 2.8 %fusion.6 = f32[512,512]{1,0:T(8,128)S(1)} fusion(bf16[2048,512]{1,0:T(8,128)(2,1)S(1)} %collective-permute-done.4, bf16[1,512,4096]{2,1,0:T(8,128)(2,1)} %bitcast_select_fusion, s32[]{:T(128)S(6)} %select_n.154), kind=kOutput, calls=%fused_computation.12 | convolution fusion | flops 1073741824 | bytes 5242884 | tf_op jit(solution)/shard_map/dot_general | solution.py:206
  82.8 2.9 %fusion.12 = f32[512,512]{1,0:T(8,128)S(1)} fusion(f32[512,512]{1,0:T(8,128)S(1)} %fusion.6, bf16[2048,512]{1,0:T(8,128)(2,1)} %collective-permute-done.3, bf16[1,512,4096]{2,1,0:T(8,128)(2,1)S(1)} %copy-done.1, s32[]{:T(128)S(6)} %select_n.153), kind=kOutput, calls=%fused_computation.19 | convolution fusion | flops 1074003968 | bytes 6291460 | tf_op jit(solution)/shard_map/dot_general | solution.py:205
  89.8 3.2 %collective-permute-start.5 = (bf16[512,512]{1,0:T(8,128)(2,1)}, bf16[512,512]{1,0:T(8,128)(2,1)S(1)}, u32[]{:S(2)}, u32[]{:S(2)}) collective-permute-start(bf16[512,512]{1,0:T(8,128)(2,1)} %pad_maximum_fusion.1), channel_id=1, source_target_pairs={{0,64},{64,0},{1,65},{65,1},{2,66},{66,2},{3,67},{67,3},{4,68},{68... | collective-permute-start | bytes 1572872 | tf_op jit(solution)/shard_map/ppermute | solution.py:207
  93.0 4.6 %fusion.62 = f32[512,512]{0,1:T(8,128)S(1)} fusion(bf16[512,4096]{1,0:T(8,128)(2,1)S(1)} %bitcast.60, bf16[4096,512]{1,0:T(8,128)(2,1)} %constant_dynamic-update-slice_fusion), kind=kOutput, calls=%fused_computation.146 | convolution fusion | flops 2147483648 | bytes 9437184 | tf_op jit(solution)/shard_map/dot_general | solution.py:202
  101.2 4.3 %collective-permute-done.5 = bf16[512,512]{1,0:T(8,128)(2,1)S(1)} collective-permute-done((bf16[512,512]{1,0:T(8,128)(2,1)}, bf16[512,512]{1,0:T(8,128)(2,1)S(1)}, u32[]{:S(2)}, u32[]{:S(2)}) %collective-permute-start.5) | collective-permute-done | bytes 524320 | tf_op jit(solution)/shard_map/ppermute | solution.py:207
  106.7 3.1 %collective-permute-start.7 = (bf16[256,4096]{1,0:T(8,128)(2,1)}, bf16[256,4096]{1,0:T(8,128)(2,1)}, u32[]{:S(2)}, u32[]{:S(2)}) collective-permute-start(bf16[256,4096]{1,0:T(8,128)(2,1)} %param.15), channel_id=1, source_target_pairs={{0,66},{66,0},{2,64},{64,2},{1,67},{67,1},{3,65},{65,3},{4,70},{70... | collective-permute-start | bytes 6291464 | tf_op jit(solution)/shard_map/ppermute | solution.py:229
  115.8 42.2 %all-gather.2.cloned.1.call-done.k_ref.v_ref = bf16[2,16384,128]{2,1,0:T(8,128)(2,1)} async-done(((bf16[2,1024,128]{2,1,0:T(8,128)(2,1)}), bf16[2,16384,128]{2,1,0:T(8,128)(2,1)}) %all-gather.2.cloned.1.call-update) | async-done | bytes 8388624 | tf_op jit(solution)/shard_map/all_gather | solution.py:215
  158.0 30.5 %shard_map.82 = bf16[1024,256]{1,0:T(8,128)(2,1)} custom-call(s32[2,9]{1,0:T(2,128)} %copy.50.tbl_ref, s32[2,9]{1,0:T(2,128)} %copy-done.7, s32[2]{0:T(128)} %copy-done.8, bf16[1024,256]{1,0:T(8,128)(2,1)} %fusion.18.q_ref, s32[1024,1]{1,0:T(8,128)} %fusion.17.qpos_ref, s32[1024,1]{1,0:T(8,128)} %copy.51.qstart_ref, ...), custom_call_target="tpu_custom_call" | custom-call | flops 4831838208 | bytes 5767168 | tf_op jit(solution)/shard_map/pallas_call | solution.py:91
  189.6 2.8 %collective-permute-start.6 = (bf16[512,256]{1,0:T(8,128)(2,1)S(1)}, bf16[512,256]{1,0:T(8,128)(2,1)S(1)}, u32[]{:S(2)}, u32[]{:S(2)}) collective-permute-start(bf16[512,256]{1,0:T(8,128)(2,1)S(1)} %get-tuple-element.37), channel_id=1, source_target_pairs={{0,64},{64,0},{1,65},{65,1},{2,66},{66,2},{3,67},{67,3},{4,68},{68... | collective-permute-start | bytes 786440 | tf_op jit(solution)/shard_map/ppermute | solution.py:233
  192.4 7.2 %collective-permute-done.6 = bf16[512,256]{1,0:T(8,128)(2,1)S(1)} collective-permute-done((bf16[512,256]{1,0:T(8,128)(2,1)S(1)}, bf16[512,256]{1,0:T(8,128)(2,1)S(1)}, u32[]{:S(2)}, u32[]{:S(2)}) %collective-permute-start.6) | collective-permute-done | bytes 262176 | tf_op jit(solution)/shard_map/ppermute | solution.py:233
  199.6 4.6 %convolution_convert_fusion = bf16[512,4096]{1,0:T(8,128)(2,1)S(1)} fusion(bf16[256,4096]{1,0:T(8,128)(2,1)} %collective-permute-done.7, bf16[256,4096]{1,0:T(8,128)(2,1)} %param.15, bf16[512,256]{1,0:T(8,128)(2,1)S(1)} %collective-permute-done.6, bf16[512,256]{1,0:T(8,128)(2,1)S(1)} %get-tuple-element.36), kind=kOutput, calls=%fused_computation.1 | convolution fusion | flops 2159017984 | bytes 8912896 | tf_op jit(solution)/shard_map/dot_general | solution.py:234
  206.4 2.8 %collective-permute-start.10 = (bf16[128,4096]{1,0:T(8,128)(2,1)S(1)}, bf16[128,4096]{1,0:T(8,128)(2,1)}, u32[]{:S(2)}, u32[]{:S(2)}) collective-permute-start(bf16[128,4096]{1,0:T(8,128)(2,1)S(1)} %get-tuple-element.26), channel_id=1, source_target_pairs={{0,48},{16,0},{32,16},{48,32},{1,49},{17,1},{33,17},{49,33},{2,50}... | collective-permute-start | bytes 3145736 | tf_op jit(solution)/shard_map/ppermute | solution.py:140
  211.5 42.3 %collective-permute-done.10 = bf16[128,4096]{1,0:T(8,128)(2,1)} collective-permute-done((bf16[128,4096]{1,0:T(8,128)(2,1)S(1)}, bf16[128,4096]{1,0:T(8,128)(2,1)}, u32[]{:S(2)}, u32[]{:S(2)}) %collective-permute-start.10) | collective-permute-done | bytes 1048608 | tf_op jit(solution)/shard_map/ppermute | solution.py:140
  253.8 3.5 %collective-permute-done.8 = bf16[128,4096]{1,0:T(8,128)(2,1)} collective-permute-done((bf16[128,4096]{1,0:T(8,128)(2,1)S(1)}, bf16[128,4096]{1,0:T(8,128)(2,1)}, u32[]{:S(2)}, u32[]{:S(2)}) %collective-permute-start.8) | collective-permute-done | bytes 1048608 | tf_op jit(solution)/shard_map/ppermute | solution.py:140
  257.3 3.8 %fusion.15 = bf16[1,128,4096]{2,1,0:T(8,128)(2,1)} fusion(bf16[128,4096]{1,0:T(8,128)(2,1)} %collective-permute-done.10, bf16[128,4096]{1,0:T(8,128)(2,1)} %collective-permute-done.9, bf16[128,4096]{1,0:T(8,128)(2,1)} %collective-permute-done.8, bf16[4,128,4096]{2,1,0:T(8,128)(2,1)} %bitcast.62, s32[]{:T(128)S(6)} %select_n.177, pred[]{:T(512)S(6)} %and.107), kind=kLoop, calls=%fused_computation.24 | loop fusion | flops 4718592 | bytes 5242885 | tf_op jit(solution)/shard_map/reshape | solution.py:240
  (103 shorter events, 32.0 us)
Async XLA Ops:
  6.5 8.7 %copy-start.4 = (bf16[4096,256]{1,0:T(8,128)(2,1)S(1)}, bf16[4096,256]{1,0:T(8,128)(2,1)}, u32[]{:S(2)}) copy-start(bf16[4096,256]{1,0:T(8,128)(2,1)} %param.12) | copy-start | bytes 6291460
  6.5 10.2 %copy-start.5 = (bf16[4096,128]{1,0:T(8,128)(2,1)S(1)}, bf16[4096,128]{1,0:T(8,128)(2,1)}, u32[]{:S(2)}) copy-start(bf16[4096,128]{1,0:T(8,128)(2,1)} %param.13) | copy-start | bytes 3145732
  6.5 151.4 %all-gather.2.cloned.1.call-start = ((), (), s32[]{:S(2)}) async-start(), calls=%async_computation | async-start | bytes 8912896 | tf_op jit(solution)/shard_map/all_gather | solution.py:215
  10.8 48.0 %collective-permute-start = (bf16[128,4096]{1,0:T(8,128)(2,1)}, bf16[128,4096]{1,0:T(8,128)(2,1)}, u32[]{:S(2)}, u32[]{:S(2)}) collective-permute-start(bf16[128,4096]{1,0:T(8,128)(2,1)} %fusion.67), channel_id=1, source_target_pairs={{0,48},{16,0},{32,16},{48,32},{1,49},{17,1},{33,17},{49,33},{2,50}... | collective-permute-start | bytes 3145736 | tf_op jit(solution)/shard_map/ppermute | solution.py:140
  13.5 45.2 %collective-permute-start.1 = (bf16[128,4096]{1,0:T(8,128)(2,1)}, bf16[128,4096]{1,0:T(8,128)(2,1)}, u32[]{:S(2)}, u32[]{:S(2)}) collective-permute-start(bf16[128,4096]{1,0:T(8,128)(2,1)} %fusion.67), channel_id=1, source_target_pairs={{0,32},{16,48},{32,0},{48,16},{1,33},{17,49},{33,1},{49,17},{2,34}... | collective-permute-start | bytes 3145736 | tf_op jit(solution)/shard_map/ppermute | solution.py:140
  14.3 48.1 %collective-permute-start.2 = (bf16[128,4096]{1,0:T(8,128)(2,1)}, bf16[128,4096]{1,0:T(8,128)(2,1)}, u32[]{:S(2)}, u32[]{:S(2)}) collective-permute-start(bf16[128,4096]{1,0:T(8,128)(2,1)} %fusion.67), channel_id=1, source_target_pairs={{0,16},{16,32},{32,48},{48,0},{1,17},{17,33},{33,49},{49,1},{2,18}... | collective-permute-start | bytes 3145736 | tf_op jit(solution)/shard_map/ppermute | solution.py:140
  16.7 8.3 %copy-start = (bf16[1,128,4096]{2,1,0:T(8,128)(2,1)S(1)}, bf16[1,128,4096]{2,1,0:T(8,128)(2,1)}, u32[]{:S(2)}) copy-start(bf16[1,128,4096]{2,1,0:T(8,128)(2,1)} %param.10) | copy-start | bytes 3145732
  16.7 8.3 %copy-start.6 = (f32[4096]{0:T(1024)S(1)}, f32[4096]{0:T(1024)}, u32[]{:S(2)}) copy-start(f32[4096]{0:T(1024)} %param.11) | copy-start | bytes 49156
  21.9 53.6 %collective-permute-start.3 = (bf16[2048,512]{1,0:T(8,128)(2,1)S(1)}, bf16[2048,512]{1,0:T(8,128)(2,1)}, u32[]{:S(2)}, u32[]{:S(2)}) collective-permute-start(bf16[2048,512]{1,0:T(8,128)(2,1)S(1)} %constant_dynamic-slice_fusion.2), channel_id=1, source_target_pairs={{0,66},{66,0},{2,64},{64,2},{1,67},{67,1},{3,65},{65,3},{4,70},{70... | collective-permute-start | bytes 6291464 | tf_op jit(solution)/shard_map/ppermute | solution.py:184
  71.0 4.6 %copy-start.10 = (s32[32]{0:T(128)S(1)}, s32[32]{0:T(128)}, u32[]{:S(2)}) copy-start(s32[32]{0:T(128)} %param.17) | copy-start | bytes 388
  75.6 4.4 %collective-permute-start.4 = (bf16[2048,512]{1,0:T(8,128)(2,1)}, bf16[2048,512]{1,0:T(8,128)(2,1)S(1)}, u32[]{:S(2)}, u32[]{:S(2)}) collective-permute-start(bf16[2048,512]{1,0:T(8,128)(2,1)} %collective-permute-done.3), channel_id=1, source_target_pairs={{0,1},{1,0},{2,3},{3,2},{4,5},{5,4},{6,7},{7,6},{8,9},{9,8},{10,11... | collective-permute-start | bytes 6291464 | tf_op jit(solution)/shard_map/ppermute | solution.py:186
  75.6 7.2 %copy-start.1 = (bf16[1,512,4096]{2,1,0:T(8,128)(2,1)S(1)}, bf16[1,512,4096]{2,1,0:T(8,128)(2,1)}, u32[]{:S(2)}) copy-start(bf16[1,512,4096]{2,1,0:T(8,128)(2,1)} %bitcast_select_fusion) | copy-start | bytes 12582916
  86.1 7.0 %copy-start.2 = (bf16[1,512,4096]{2,1,0:T(8,128)(2,1)S(1)}, bf16[1,512,4096]{2,1,0:T(8,128)(2,1)}, u32[]{:S(2)}) copy-start(bf16[1,512,4096]{2,1,0:T(8,128)(2,1)} %bitcast_select_fusion) | copy-start | bytes 12582916
  89.8 15.7 %collective-permute-start.5 = (bf16[512,512]{1,0:T(8,128)(2,1)}, bf16[512,512]{1,0:T(8,128)(2,1)S(1)}, u32[]{:S(2)}, u32[]{:S(2)}) collective-permute-start(bf16[512,512]{1,0:T(8,128)(2,1)} %pad_maximum_fusion.1), channel_id=1, source_target_pairs={{0,64},{64,0},{1,65},{65,1},{2,66},{66,2},{3,67},{67,3},{4,68},{68... | collective-permute-start | bytes 1572872 | tf_op jit(solution)/shard_map/ppermute | solution.py:207
  98.8 11.3 %copy-start.9 = (s32[16]{0:T(128)S(1)}, s32[16]{0:T(128)}, u32[]{:S(2)}) copy-start(s32[16]{0:T(128)} %param.16) | copy-start | bytes 196
  106.7 85.7 %collective-permute-start.7 = (bf16[256,4096]{1,0:T(8,128)(2,1)}, bf16[256,4096]{1,0:T(8,128)(2,1)}, u32[]{:S(2)}, u32[]{:S(2)}) collective-permute-start(bf16[256,4096]{1,0:T(8,128)(2,1)} %param.15), channel_id=1, source_target_pairs={{0,66},{66,0},{2,64},{64,2},{1,67},{67,1},{3,65},{65,3},{4,70},{70... | collective-permute-start | bytes 6291464 | tf_op jit(solution)/shard_map/ppermute | solution.py:229
  111.2 46.7 %copy-start.8 = (s32[2]{0:T(128)}, s32[2]{0:T(128)S(1)}, u32[]{:S(2)}) copy-start(s32[2]{0:T(128)S(1)} %fusion.56.cnt_ref) | copy-start | bytes 28
  111.3 46.6 %copy-start.7 = (s32[2,9]{1,0:T(2,128)}, s32[2,9]{1,0:T(2,128)S(1)}, u32[]{:S(2)}) copy-start(s32[2,9]{1,0:T(2,128)S(1)} %add_minimum_fusion.seq_ref) | copy-start | bytes 220
  189.6 10.0 %collective-permute-start.6 = (bf16[512,256]{1,0:T(8,128)(2,1)S(1)}, bf16[512,256]{1,0:T(8,128)(2,1)S(1)}, u32[]{:S(2)}, u32[]{:S(2)}) collective-permute-start(bf16[512,256]{1,0:T(8,128)(2,1)S(1)} %get-tuple-element.37), channel_id=1, source_target_pairs={{0,64},{64,0},{1,65},{65,1},{2,66},{66,2},{3,67},{67,3},{4,68},{68... | collective-permute-start | bytes 786440 | tf_op jit(solution)/shard_map/ppermute | solution.py:233
  204.2 1.9 copy-start.3
  206.4 47.4 %collective-permute-start.10 = (bf16[128,4096]{1,0:T(8,128)(2,1)S(1)}, bf16[128,4096]{1,0:T(8,128)(2,1)}, u32[]{:S(2)}, u32[]{:S(2)}) collective-permute-start(bf16[128,4096]{1,0:T(8,128)(2,1)S(1)} %get-tuple-element.26), channel_id=1, source_target_pairs={{0,48},{16,0},{32,16},{48,32},{1,49},{17,1},{33,17},{49,33},{2,50}... | collective-permute-start | bytes 3145736 | tf_op jit(solution)/shard_map/ppermute | solution.py:140
  209.2 48.1 %collective-permute-start.8 = (bf16[128,4096]{1,0:T(8,128)(2,1)S(1)}, bf16[128,4096]{1,0:T(8,128)(2,1)}, u32[]{:S(2)}, u32[]{:S(2)}) collective-permute-start(bf16[128,4096]{1,0:T(8,128)(2,1)S(1)} %get-tuple-element.25), channel_id=1, source_target_pairs={{0,16},{16,32},{32,48},{48,0},{1,17},{17,33},{33,49},{49,1},{2,18}... | collective-permute-start | bytes 3145736 | tf_op jit(solution)/shard_map/ppermute | solution.py:140
  209.2 48.1 %collective-permute-start.9 = (bf16[128,4096]{1,0:T(8,128)(2,1)S(1)}, bf16[128,4096]{1,0:T(8,128)(2,1)}, u32[]{:S(2)}, u32[]{:S(2)}) collective-permute-start(bf16[128,4096]{1,0:T(8,128)(2,1)S(1)} %get-tuple-element.27), channel_id=1, source_target_pairs={{0,32},{16,48},{32,0},{48,16},{1,33},{17,49},{33,1},{49,17},{2,34}... | collective-permute-start | bytes 3145736 | tf_op jit(solution)/shard_map/ppermute | solution.py:140
Sparse Core Ops, SparseCore 0:
  106.8 51.1 all-gather.1

commit v7 on v6

--- a/solution.py
+++ b/solution.py
@@ -178,18 +178,24 @@
     plane = lax.axis_index("yh")
     core = lax.axis_index("core")
     weights = jnp.concatenate([q_weight, k_weight, v_weight], axis=1)
-    half_in = weights.shape[0] // 2
-    sent_half = lax.dynamic_slice_in_dim(weights, core * half_in, half_in, 0)
-    plane_rows = gather_x(normed[0])[None]
-    partner_half = lax.ppermute(sent_half, ("yh", "ylo"), NEIGHBOUR)
-    plane_rows, partner_half = lax.optimization_barrier((plane_rows, partner_half))
-    other_half = lax.ppermute(partner_half, "core", [(0, 1), (1, 0)])
-    half = plane_rows.shape[1]
-    flat_rows = plane_rows.reshape(half, model_width)
+    part_cols = weights.shape[1] // 2
+    sent_part = jnp.where(core == 0, weights[:, :part_cols], weights[:, part_cols:])
+    n_x = lax.axis_size("x")
+    me_x = lax.axis_index("x")
+    chunk = normed[0]
+    chunks = [chunk] + [shift_x(chunk, n_x - e, n_x) for e in range(1, n_x)]
+    partner_part = lax.ppermute(sent_part, ("yh", "ylo"), NEIGHBOUR)
+    got = lax.optimization_barrier((chunks, partner_part))
+    chunks, partner_part = got
+    other_part = lax.ppermute(partner_part, "core", [(0, 1), (1, 0)])
+    half = n_x * chunk.shape[0]
     all_places = positions(base_row + jnp.arange(tok_dev, dtype=jnp.int32), span_order, span_rows)
     places = lax.dynamic_slice_in_dim(all_places, plane * half, half, 0)
-    rows_mine = lax.dynamic_slice_in_dim(flat_rows, core * half_in, half_in, 1)
-    rows_other = lax.dynamic_slice_in_dim(flat_rows, (1 - core) * half_in, half_in, 1)
+    order = (jnp.arange(n_x, dtype=jnp.int32) - me_x) % n_x
+
+    def in_order(parts):
+        stacked = jnp.stack(parts)
+        return jnp.take(stacked, order, axis=0).reshape(half, stacked.shape[-1])
 
     def finish(out):
         q = rotary(out[:, :q_cols].reshape(half, q_heads, head_dim), places)
@@ -198,15 +204,17 @@
             [q.reshape(half, q_cols), k.reshape(half, kv_cols), out[:, q_cols + kv_cols:]], axis=1
         ).astype(jnp.bfloat16)
 
-    def project(w):
-        return finish(jnp.dot(flat_rows, w, preferred_element_type=jnp.float32))
-
-    for_partner = finish(
-        jnp.dot(rows_mine, partner_half, preferred_element_type=jnp.float32)
-        + jnp.dot(rows_other, other_half, preferred_element_type=jnp.float32))
+    def project(rows_list, w):
+        return in_order([jnp.dot(r, w, preferred_element_type=jnp.float32) for r in rows_list])
+
+    got_part = project(chunks, partner_part)
+    swapped_part = project(chunks, other_part)
+    for_partner = finish(jnp.concatenate([
+        jnp.where(core == 0, got_part, swapped_part),
+        jnp.where(core == 0, swapped_part, got_part)], axis=1))
     received = lax.ppermute(for_partner, "yh", [(0, 1), (1, 0)])
-    flat_rows, for_partner = lax.optimization_barrier((flat_rows, for_partner))
-    own = project(weights)
+    chunks, for_partner = lax.optimization_barrier((chunks, for_partner))
+    own = finish(project(chunks, weights))
     first = jnp.where(plane == 0, own, received)
     second = jnp.where(plane == 0, received, own)
     projected = jnp.concatenate([first, second], axis=0)

time: 268 us -> 282 us (1.052)
  the two profiles are of different devices: /device:TPU:96 before, /device:TPU:104 now
where the time goes in v7:
time: 282 us; the launch traced here: 281 us
  waiting for transfers between devices  140 us (50%)
  Pallas kernels  48.9 us (17%)
  matrix products  25.7 us (9%)
  other arithmetic  24.3 us (9%)
  starting transfers between devices  15.1 us (5%)
  between operations  13.9 us (5%)
  local copies, waits for them, and re-layouts  13.4 us (5%)
    ppermute x6, waiting for transfers between devices, shift_x(): return lax.ppermute(value, 'x', [(i, (i + d) % n) for i in range(n)])  79.8 us
    pallas_call x1, Pallas kernels, span_attention(): pl.pallas_call(kernel, out_shape=jax.ShapeDtypeStruct((rows, q_cols), jnp...  48.9 us
    all_gather x1, waiting for transfers between devices, per_device(): gathered = lax.all_gather(kv_pair, CONTEXT, axis=1, tiled=True)  42.8 us
    dot_general x12, matrix products, project(): jnp.dot(r, w, preferred_element_type=jnp.float32)  21.2 us
    ppermute x1, waiting for transfers between devices, per_device(): received = lax.ppermute(for_partner, 'yh', [(0, 1), (1, 0)])  11.8 us
    ppermute x6, starting transfers between devices, shift_x(): return lax.ppermute(value, 'x', [(i, (i + d) % n) for i in range(n)])  9.52 us
    ppermute x1, waiting for transfers between devices, per_device(): partner_rows = lax.ppermute(other_rows, 'yh', [(0, 1), (1, 0)])  5.8 us
  transfers between devices with their start and end apart: 12, of which 7 were waited for; matrix products, arithmetic and copies ran while one was open for 9% of the time, Pallas kernels for 17%

profile of v7, /device:TPU:104, one launch (start us, length us, event | category | flops | bytes accessed | tf_op | source)
XLA Modules:
  0.0 281.5 jit_solution(9925876653137194894)
XLA Ops:
  6.5 5.0 %constant_dynamic-update-slice_fusion.2 = (bf16[4096,512]{1,0:T(8,128)(2,1)}, bf16[4096,256]{1,0:T(8,128)(2,1)}) fusion(bf16[4096,256]{1,0:T(8,128)(2,1)} %param.14, bf16[4096,128]{1,0:T(8,128)(2,1)} %param.16, bf16[4096,128]{1,0:T(8,128)(2,1)} %param.15, pred[]{:T(512)S(6)} %eq.111), kind=kLoop, calls=%fused_computation.109 | loop fusion | flops 5242879 | bytes 8388609
  13.7 2.8 %collective-permute-start = (bf16[128,4096]{1,0:T(8,128)(2,1)S(1)}, bf16[128,4096]{1,0:T(8,128)(2,1)}, u32[]{:S(2)}, u32[]{:S(2)}) collective-permute-start(bf16[128,4096]{1,0:T(8,128)(2,1)S(1)} %fusion.7), channel_id=1, source_target_pairs={{0,48},{16,0},{32,16},{48,32},{1,49},{17,1},{33,17},{49,33},{2,50}... | collective-permute-start | bytes 3145736 | tf_op jit(solution)/shard_map/ppermute | solution.py:140
  20.4 40.8 %collective-permute-done = bf16[128,4096]{1,0:T(8,128)(2,1)} collective-permute-done((bf16[128,4096]{1,0:T(8,128)(2,1)S(1)}, bf16[128,4096]{1,0:T(8,128)(2,1)}, u32[]{:S(2)}, u32[]{:S(2)}) %collective-permute-start) | collective-permute-done | bytes 1048608 | tf_op jit(solution)/shard_map/ppermute | solution.py:140
  61.2 3.8 %collective-permute-done.2 = bf16[128,4096]{1,0:T(8,128)(2,1)} collective-permute-done((bf16[128,4096]{1,0:T(8,128)(2,1)S(1)}, bf16[128,4096]{1,0:T(8,128)(2,1)}, u32[]{:S(2)}, u32[]{:S(2)}) %collective-permute-start.2) | collective-permute-done | bytes 1048608 | tf_op jit(solution)/shard_map/ppermute | solution.py:140
  65.0 2.4 constant_dynamic-update-slice_fusion.1
  74.8 2.4 gather_fusion.1
  77.2 2.0 convolution_bitcast_fusion.7
  79.2 2.4 convolution_bitcast_fusion.6
  81.6 2.4 convolution_bitcast_fusion.5
  84.0 2.4 convolution_bitcast_fusion.4
  92.5 1.9 convolution_bitcast_fusion.2
  94.4 1.9 convolution_bitcast_fusion.1
  96.4 1.9 convolution_bitcast_fusion
  103.8 11.8 %collective-permute-done.5 = bf16[512,512]{1,0:T(8,128)(2,1)S(1)} collective-permute-done((bf16[512,512]{1,0:T(8,128)(2,1)}, bf16[512,512]{1,0:T(8,128)(2,1)S(1)}, u32[]{:S(2)}, u32[]{:S(2)}) %collective-permute-start.5) | collective-permute-done | bytes 524320 | tf_op jit(solution)/shard_map/ppermute | solution.py:215
  123.4 42.8 %all-gather.2.cloned.1.call-done.k_ref.v_ref = bf16[2,16384,128]{2,1,0:T(8,128)(2,1)} async-done(((bf16[2,1024,128]{2,1,0:T(8,128)(2,1)}), bf16[2,16384,128]{2,1,0:T(8,128)(2,1)}) %all-gather.2.cloned.1.call-update) | async-done | bytes 8388624 | tf_op jit(solution)/shard_map/all_gather | solution.py:223
  166.2 48.9 %shard_map.82 = bf16[1024,256]{1,0:T(8,128)(2,1)} custom-call(s32[2,9]{1,0:T(2,128)} %copy.26.tbl_ref, s32[2,9]{1,0:T(2,128)} %copy-done.7, s32[2]{0:T(128)} %copy-done.8, bf16[1024,256]{1,0:T(8,128)(2,1)} %fusion.10.q_ref, s32[1024,1]{1,0:T(8,128)} %fusion.9.qpos_ref, s32[1024,1]{1,0:T(8,128)} %copy.27.qstart_ref, ...), custom_call_target="tpu_custom_call" | custom-call | flops 4831838208 | bytes 5767168 | tf_op jit(solution)/shard_map/pallas_call | solution.py:91
  216.1 2.2 collective-permute-start.6
  218.3 5.8 %collective-permute-done.6 = bf16[512,256]{1,0:T(8,128)(2,1)S(1)} collective-permute-done((bf16[512,256]{1,0:T(8,128)(2,1)S(1)}, bf16[512,256]{1,0:T(8,128)(2,1)S(1)}, u32[]{:S(2)}, u32[]{:S(2)}) %collective-permute-start.6) | collective-permute-done | bytes 262176 | tf_op jit(solution)/shard_map/ppermute | solution.py:241
  224.1 4.6 %convolution_convert_fusion = bf16[512,4096]{1,0:T(8,128)(2,1)S(1)} fusion(bf16[256,4096]{1,0:T(8,128)(2,1)} %collective-permute-done.7, bf16[256,4096]{1,0:T(8,128)(2,1)} %param.17, bf16[512,256]{1,0:T(8,128)(2,1)S(1)} %collective-permute-done.6, bf16[512,256]{1,0:T(8,128)(2,1)S(1)} %get-tuple-element.53), kind=kOutput, calls=%fused_computation.3 | convolution fusion | flops 2159017984 | bytes 8912896 | tf_op jit(solution)/shard_map/dot_general | solution.py:242
  230.6 2.7 collective-permute-start.10
  233.2 2.3 collective-permute-start.9
  235.6 31.7 %collective-permute-done.10 = bf16[128,4096]{1,0:T(8,128)(2,1)} collective-permute-done((bf16[128,4096]{1,0:T(8,128)(2,1)S(1)}, bf16[128,4096]{1,0:T(8,128)(2,1)}, u32[]{:S(2)}, u32[]{:S(2)}) %collective-permute-start.10) | collective-permute-done | bytes 1048608 | tf_op jit(solution)/shard_map/ppermute | solution.py:140
  267.3 3.5 %collective-permute-done.8 = bf16[128,4096]{1,0:T(8,128)(2,1)} collective-permute-done((bf16[128,4096]{1,0:T(8,128)(2,1)S(1)}, bf16[128,4096]{1,0:T(8,128)(2,1)}, u32[]{:S(2)}, u32[]{:S(2)}) %collective-permute-start.8) | collective-permute-done | bytes 1048608 | tf_op jit(solution)/shard_map/ppermute | solution.py:140
  270.8 3.8 %fusion.6 = bf16[1,128,4096]{2,1,0:T(8,128)(2,1)} fusion(bf16[128,4096]{1,0:T(8,128)(2,1)} %collective-permute-done.10, bf16[128,4096]{1,0:T(8,128)(2,1)} %collective-permute-done.9, bf16[128,4096]{1,0:T(8,128)(2,1)} %collective-permute-done.8, bf16[4,128,4096]{2,1,0:T(8,128)(2,1)} %bitcast.92, s32[]{:T(128)S(6)} %select_n.208, pred[]{:T(512)S(6)} %and.114), kind=kLoop, calls=%fused_computation.30 | loop fusion | flops 4718592 | bytes 5242885 | tf_op jit(solution)/shard_map/reshape | solution.py:248
  (112 shorter events, 35.4 us)
Async XLA Ops:
  6.5 159.6 %all-gather.2.cloned.1.call-start = ((), (), s32[]{:S(2)}) async-start(), calls=%async_computation | async-start | bytes 8912896 | tf_op jit(solution)/shard_map/all_gather | solution.py:223
  6.5 6.6 %copy-start.2 = (bf16[1,128,4096]{2,1,0:T(8,128)(2,1)S(1)}, bf16[1,128,4096]{2,1,0:T(8,128)(2,1)}, u32[]{:S(2)}) copy-start(bf16[1,128,4096]{2,1,0:T(8,128)(2,1)} %param.12) | copy-start | bytes 3145732
  6.5 6.9 %copy-start.6 = (f32[4096]{0:T(1024)S(1)}, f32[4096]{0:T(1024)}, u32[]{:S(2)}) copy-start(f32[4096]{0:T(1024)} %param.13) | copy-start | bytes 49156
  11.5 6.8 %copy-start.10 = (s32[32]{0:T(128)S(1)}, s32[32]{0:T(128)}, u32[]{:S(2)}) copy-start(s32[32]{0:T(128)} %param.19) | copy-start | bytes 388
  11.5 53.5 %collective-permute-start.3 = (bf16[4096,256]{1,0:T(8,128)(2,1)}, bf16[4096,256]{1,0:T(8,128)(2,1)S(1)}, u32[]{:S(2)}, u32[]{:S(2)}) collective-permute-start(bf16[4096,256]{1,0:T(8,128)(2,1)} %get-tuple-element.42), channel_id=1, source_target_pairs={{0,66},{66,0},{2,64},{64,2},{1,67},{67,1},{3,65},{65,3},{4,70},{70... | collective-permute-start | bytes 6291464 | tf_op jit(solution)/shard_map/ppermute | solution.py:187
  13.7 47.5 %collective-permute-start = (bf16[128,4096]{1,0:T(8,128)(2,1)S(1)}, bf16[128,4096]{1,0:T(8,128)(2,1)}, u32[]{:S(2)}, u32[]{:S(2)}) collective-permute-start(bf16[128,4096]{1,0:T(8,128)(2,1)S(1)} %fusion.7), channel_id=1, source_target_pairs={{0,48},{16,0},{32,16},{48,32},{1,49},{17,1},{33,17},{49,33},{2,50}... | collective-permute-start | bytes 3145736 | tf_op jit(solution)/shard_map/ppermute | solution.py:140
  16.6 44.6 %collective-permute-start.1 = (bf16[128,4096]{1,0:T(8,128)(2,1)S(1)}, bf16[128,4096]{1,0:T(8,128)(2,1)}, u32[]{:S(2)}, u32[]{:S(2)}) collective-permute-start(bf16[128,4096]{1,0:T(8,128)(2,1)S(1)} %fusion.7), channel_id=1, source_target_pairs={{0,32},{16,48},{32,0},{48,16},{1,33},{17,49},{33,1},{49,17},{2,34}... | collective-permute-start | bytes 3145736 | tf_op jit(solution)/shard_map/ppermute | solution.py:140
  17.4 47.6 %collective-permute-start.2 = (bf16[128,4096]{1,0:T(8,128)(2,1)S(1)}, bf16[128,4096]{1,0:T(8,128)(2,1)}, u32[]{:S(2)}, u32[]{:S(2)}) collective-permute-start(bf16[128,4096]{1,0:T(8,128)(2,1)S(1)} %fusion.7), channel_id=1, source_target_pairs={{0,16},{16,32},{32,48},{48,0},{1,17},{17,33},{33,49},{49,1},{2,18}... | collective-permute-start | bytes 3145736 | tf_op jit(solution)/shard_map/ppermute | solution.py:140
  18.4 48.9 %copy-start.1 = (bf16[4096,128]{1,0:T(8,128)(2,1)S(1)}, bf16[4096,128]{1,0:T(8,128)(2,1)}, u32[]{:S(2)}) copy-start(bf16[4096,128]{1,0:T(8,128)(2,1)} %param.16) | copy-start | bytes 3145732
  65.0 12.2 %collective-permute-start.4 = (bf16[4096,256]{1,0:T(8,128)(2,1)S(1)}, bf16[4096,256]{1,0:T(8,128)(2,1)}, u32[]{:S(2)}, u32[]{:S(2)}) collective-permute-start(bf16[4096,256]{1,0:T(8,128)(2,1)S(1)} %collective-permute-done.3), channel_id=1, source_target_pairs={{0,1},{1,0},{2,3},{3,2},{4,5},{5,4},{6,7},{7,6},{8,9},{9,8},{10,11... | collective-permute-start | bytes 6291464 | tf_op jit(solution)/shard_map/ppermute | solution.py:190
  84.0 3.1 %copy-start.5 = (f32[4,128,256]{2,1,0:T(8,128)S(1)}, f32[4,128,256]{2,1,0:T(8,128)}, u32[]{:S(2)}) copy-start(f32[4,128,256]{2,1,0:T(8,128)} %gather_fusion.1) | copy-start | bytes 1572868
  87.1 1.0 copy-start.4
  88.0 3.7 %copy-start = (bf16[4096,512]{1,0:T(8,128)(2,1)S(1)}, bf16[4096,512]{1,0:T(8,128)(2,1)}, u32[]{:S(2)}) copy-start(bf16[4096,512]{1,0:T(8,128)(2,1)} %constant_dynamic-update-slice_fusion) | copy-start | bytes 12582916
  99.3 16.3 %collective-permute-start.5 = (bf16[512,512]{1,0:T(8,128)(2,1)}, bf16[512,512]{1,0:T(8,128)(2,1)S(1)}, u32[]{:S(2)}, u32[]{:S(2)}) collective-permute-start(bf16[512,512]{1,0:T(8,128)(2,1)} %pad_maximum_fusion.3), channel_id=1, source_target_pairs={{0,64},{64,0},{1,65},{65,1},{2,66},{66,2},{3,67},{67,3},{4,68},{68... | collective-permute-start | bytes 1572872 | tf_op jit(solution)/shard_map/ppermute | solution.py:215
  115.9 1.8 copy-start.9
  116.8 101.5 %collective-permute-start.7 = (bf16[256,4096]{1,0:T(8,128)(2,1)}, bf16[256,4096]{1,0:T(8,128)(2,1)}, u32[]{:S(2)}, u32[]{:S(2)}) collective-permute-start(bf16[256,4096]{1,0:T(8,128)(2,1)} %param.17), channel_id=1, source_target_pairs={{0,66},{66,0},{2,64},{64,2},{1,67},{67,1},{3,65},{65,3},{4,70},{70... | collective-permute-start | bytes 6291464 | tf_op jit(solution)/shard_map/ppermute | solution.py:237
  118.8 47.4 %copy-start.8 = (s32[2]{0:T(128)}, s32[2]{0:T(128)S(1)}, u32[]{:S(2)}) copy-start(s32[2]{0:T(128)S(1)} %fusion.46.cnt_ref) | copy-start | bytes 28
  118.9 47.3 %copy-start.7 = (s32[2,9]{1,0:T(2,128)}, s32[2,9]{1,0:T(2,128)S(1)}, u32[]{:S(2)}) copy-start(s32[2,9]{1,0:T(2,128)S(1)} %add_minimum_fusion.seq_ref) | copy-start | bytes 220
  216.1 8.0 %collective-permute-start.6 = (bf16[512,256]{1,0:T(8,128)(2,1)S(1)}, bf16[512,256]{1,0:T(8,128)(2,1)S(1)}, u32[]{:S(2)}, u32[]{:S(2)}) collective-permute-start(bf16[512,256]{1,0:T(8,128)(2,1)S(1)} %get-tuple-element.54), channel_id=1, source_target_pairs={{0,64},{64,0},{1,65},{65,1},{2,66},{66,2},{3,67},{67,3},{4,68},{68... | collective-permute-start | bytes 786440 | tf_op jit(solution)/shard_map/ppermute | solution.py:241
  228.6 1.9 copy-start.3
  230.6 36.7 %collective-permute-start.10 = (bf16[128,4096]{1,0:T(8,128)(2,1)S(1)}, bf16[128,4096]{1,0:T(8,128)(2,1)}, u32[]{:S(2)}, u32[]{:S(2)}) collective-permute-start(bf16[128,4096]{1,0:T(8,128)(2,1)S(1)} %get-tuple-element.39), channel_id=1, source_target_pairs={{0,48},{16,0},{32,16},{48,32},{1,49},{17,1},{33,17},{49,33},{2,50}... | collective-permute-start | bytes 3145736 | tf_op jit(solution)/shard_map/ppermute | solution.py:140
  233.2 37.6 %collective-permute-start.8 = (bf16[128,4096]{1,0:T(8,128)(2,1)S(1)}, bf16[128,4096]{1,0:T(8,128)(2,1)}, u32[]{:S(2)}, u32[]{:S(2)}) collective-permute-start(bf16[128,4096]{1,0:T(8,128)(2,1)S(1)} %get-tuple-element.38), channel_id=1, source_target_pairs={{0,16},{16,32},{32,48},{48,0},{1,17},{17,33},{33,49},{49,1},{2,18}... | collective-permute-start | bytes 3145736 | tf_op jit(solution)/shard_map/ppermute | solution.py:140
  233.2 37.6 %collective-permute-start.9 = (bf16[128,4096]{1,0:T(8,128)(2,1)S(1)}, bf16[128,4096]{1,0:T(8,128)(2,1)}, u32[]{:S(2)}, u32[]{:S(2)}) collective-permute-start(bf16[128,4096]{1,0:T(8,128)(2,1)S(1)} %get-tuple-element.40), channel_id=1, source_target_pairs={{0,32},{16,48},{32,0},{48,16},{1,33},{17,49},{33,1},{49,17},{2,34}... | collective-permute-start | bytes 3145736 | tf_op jit(solution)/shard_map/ppermute | solution.py:140
Sparse Core Ops, SparseCore 0:
  116.9 49.2 all-gather.1

commit v8 on v6

--- a/solution.py
+++ b/solution.py
@@ -131,21 +131,13 @@
     count = jnp.sum(valid.astype(jnp.int32), axis=1)
     slot = jnp.arange(KEY_SLOTS, dtype=jnp.int32)
     seq = jnp.minimum(sq[:, None] - count[:, None] + 1 + slot[None, :], sq[:, None])
-    storage = jnp.sum(
-        jnp.where(seq[:, :, None] == span_ids[None, None, :], inverse[None, None, :], 0), axis=2)
-    return storage.astype(jnp.int32), seq.astype(jnp.int32), count.astype(jnp.int32)
+    tbl = jnp.sum(jnp.where(seq[:, :, None] == span_ids[None, None, :], inverse[None, None, :], 0),
+                  axis=2)
+    return tbl.astype(jnp.int32), seq.astype(jnp.int32), count.astype(jnp.int32)
 
 
 def shift_x(value, d, n):
     return lax.ppermute(value, "x", [(i, (i + d) % n) for i in range(n)])
-
-
-def gather_x(chunk):
-    n = lax.axis_size("x")
-    me = lax.axis_index("x")
-    from_right = jnp.stack([chunk] + [shift_x(chunk, n - e, n) for e in range(1, n)])
-    order = (jnp.arange(n, dtype=jnp.int32) - me) % n
-    return jnp.take(from_right, order, axis=0).reshape(n * chunk.shape[0], *chunk.shape[1:])
 
 
 def reduce_scatter_x(value):
@@ -180,7 +172,7 @@
     weights = jnp.concatenate([q_weight, k_weight, v_weight], axis=1)
     half_in = weights.shape[0] // 2
     sent_half = lax.dynamic_slice_in_dim(weights, core * half_in, half_in, 0)
-    plane_rows = gather_x(normed[0])[None]
+    plane_rows = lax.all_gather(normed, "x", axis=1, tiled=True)
     partner_half = lax.ppermute(sent_half, ("yh", "ylo"), NEIGHBOUR)
     plane_rows, partner_half = lax.optimization_barrier((plane_rows, partner_half))
     other_half = lax.ppermute(partner_half, "core", [(0, 1), (1, 0)])

time: 268 us -> 253 us (0.944)
  Pallas kernels: 30.5 us -> 44.3 us
  other arithmetic: 29.1 us -> 20.6 us
  local copies, waits for them, and re-layouts: 18.3 us -> 10 us
  waiting for transfers between devices: 140 us -> 133 us
  starting transfers between devices: 21.8 us -> 16.5 us
    ppermute x6 -> x3, waiting for transfers between devices: 82.7 us -> 29.5 us  [shift_x(): return lax.ppermute(value, 'x', [(i, (i + d) % n) for i in range(n)])]
    ppermute x1, waiting for transfers between devices: 0.01 us -> 45.6 us  [per_device(): partner_half = lax.ppermute(sent_half, ('yh', 'ylo'), NEIGHBOUR)]
    pallas_call x1, Pallas kernels: 30.5 us -> 44.3 us  [span_attention(): pl.pallas_call(kernel, out_shape=jax.ShapeDtypeStruct((rows, q_cols), jnp...]
    gather x1 -> x0, local copies, waits for them, and re-layouts: 4.97 us -> none  [gather_x(): jnp.take(from_right, order, axis=0)]
    select_n x2 -> x0, other arithmetic: 4.58 us -> none  [gather_x(): jnp.take(from_right, order, axis=0)]
    ppermute x6 -> x3, starting transfers between devices: 9.58 us -> 5.66 us  [shift_x(): return lax.ppermute(value, 'x', [(i, (i + d) % n) for i in range(n)])]
    another operation x7 -> x6, other arithmetic: 7.51 us -> 3.93 us
  transfers between devices with their start and end apart: 12 -> 10, of which waited for: 8 -> 7; matrix products, arithmetic and copies ran while one was open for 14% -> 7% of each run, Pallas kernels for 11% -> 18%
where the time goes in v8:
time: 253 us; the launch traced here: 252 us
  waiting for transfers between devices  133 us (53%)
  Pallas kernels  44.3 us (18%)
  other arithmetic  20.6 us (8%)
  starting transfers between devices  16.5 us (7%)
  matrix products  13.9 us (5%)
  between operations  13.8 us (5%)
  local copies, waits for them, and re-layouts  10 us (4%)
    ppermute x1, waiting for transfers between devices, per_device(): partner_half = lax.ppermute(sent_half, ('yh', 'ylo'), NEIGHBOUR)  45.6 us
    all_gather x1, waiting for transfers between devices, per_device(): gathered = lax.all_gather(kv_pair, CONTEXT, axis=1, tiled=True)  44.3 us
    pallas_call x1, Pallas kernels, span_attention(): pl.pallas_call(kernel, out_shape=jax.ShapeDtypeStruct((rows, q_cols), jnp...  44.3 us
    ppermute x3, waiting for transfers between devices, shift_x(): return lax.ppermute(value, 'x', [(i, (i + d) % n) for i in range(n)])  29.5 us
    unnamed x30, local copies, waits for them, and re-layouts  5.76 us
    ppermute x3, starting transfers between devices, shift_x(): return lax.ppermute(value, 'x', [(i, (i + d) % n) for i in range(n)])  5.66 us
    ppermute x1, waiting for transfers between devices, per_device(): received = lax.ppermute(for_partner, 'yh', [(0, 1), (1, 0)])  5.6 us
    ppermute x1, waiting for transfers between devices, per_device(): partner_rows = lax.ppermute(other_rows, 'yh', [(0, 1), (1, 0)])  5.09 us
  transfers between devices with their start and end apart: 10, of which 7 were waited for; matrix products, arithmetic and copies ran while one was open for 7% of the time, Pallas kernels for 18%

profile of v8, /device:TPU:96, one launch (start us, length us, event | category | flops | bytes accessed | tf_op | source)
XLA Modules:
  0.0 252.3 jit_solution(6098497171284466791)
XLA Ops:
  6.5 1.7 fusion.3
  8.2 2.5 %fusion.5 = bf16[1,128,4096]{2,1,0:T(8,128)(2,1)} fusion(bf16[1,128,4096]{2,1,0:T(8,128)(2,1)} %param.10, f32[4096]{0:T(1024)} %param.11, f32[128]{0:T(128)S(1)} %add_rsqrt_fusion), kind=kLoop, calls=%fused_computation.8 | loop fusion | flops 2097152 | bytes 2114048 | tf_op jit(solution)/shard_map/convert_element_type | solution.py:169
  12.8 1.8 copy-done.1
  14.6 3.0 %collective-permute-start = (bf16[2048,512]{1,0:T(8,128)(2,1)S(1)}, bf16[2048,512]{1,0:T(8,128)(2,1)S(1)}, u32[]{:S(2)}, u32[]{:S(2)}) collective-permute-start(bf16[2048,512]{1,0:T(8,128)(2,1)S(1)} %constant_dynamic-slice_fusion.2), channel_id=1, source_target_pairs={{0,66},{66,0},{2,64},{64,2},{1,67},{67,1},{3,65},{65,3},{4,70},{70... | collective-permute-start | bytes 6291464 | tf_op jit(solution)/shard_map/ppermute | solution.py:176
  17.6 45.6 %collective-permute-done = bf16[2048,512]{1,0:T(8,128)(2,1)S(1)} collective-permute-done((bf16[2048,512]{1,0:T(8,128)(2,1)S(1)}, bf16[2048,512]{1,0:T(8,128)(2,1)S(1)}, u32[]{:S(2)}, u32[]{:S(2)}) %collective-permute-start) | collective-permute-done | bytes 2097184 | tf_op jit(solution)/shard_map/ppermute | solution.py:176
  64.5 3.1 %collective-permute-done.1 = bf16[2048,512]{1,0:T(8,128)(2,1)} collective-permute-done((bf16[2048,512]{1,0:T(8,128)(2,1)S(1)}, bf16[2048,512]{1,0:T(8,128)(2,1)}, u32[]{:S(2)}, u32[]{:S(2)}) %collective-permute-start.1) | collective-permute-done | bytes 2097184 | tf_op jit(solution)/shard_map/ppermute | solution.py:178
  67.5 3.5 %fusion.6 = f32[512,512]{1,0:T(8,128)S(1)} fusion(bf16[2048,512]{1,0:T(8,128)(2,1)} %collective-permute-done.1, bf16[1,512,4096]{2,1,0:T(8,128)(2,1)} %all-gather.3.cloned.1.call-done, s32[]{:T(128)S(6)} %select_n.105), kind=kOutput, calls=%fused_computation.9 | convolution fusion | flops 1073741824 | bytes 5242884 | tf_op jit(solution)/shard_map/dot_general | solution.py:198
  71.0 1.3 fusion.12
  76.5 1.9 collective-permute-start.2
  78.4 4.6 %fusion.59 = f32[512,512]{0,1:T(8,128)S(1)} fusion(bf16[512,4096]{1,0:T(8,128)(2,1)} %bitcast.58, bf16[4096,512]{1,0:T(8,128)(2,1)S(1)} %copy-done.2), kind=kOutput, calls=%fused_computation.129 | convolution fusion | flops 2147483648 | bytes 9437184 | tf_op jit(solution)/shard_map/dot_general | solution.py:194
  86.5 5.6 %collective-permute-done.2 = bf16[512,512]{1,0:T(8,128)(2,1)S(1)} collective-permute-done((bf16[512,512]{1,0:T(8,128)(2,1)}, bf16[512,512]{1,0:T(8,128)(2,1)S(1)}, u32[]{:S(2)}, u32[]{:S(2)}) %collective-permute-start.2) | collective-permute-done | bytes 524320 | tf_op jit(solution)/shard_map/ppermute | solution.py:199
  93.3 3.0 %collective-permute-start.4 = (bf16[256,4096]{1,0:T(8,128)(2,1)}, bf16[256,4096]{1,0:T(8,128)(2,1)}, u32[]{:S(2)}, u32[]{:S(2)}) collective-permute-start(bf16[256,4096]{1,0:T(8,128)(2,1)} %param.15), channel_id=1, source_target_pairs={{0,66},{66,0},{2,64},{64,2},{1,67},{67,1},{3,65},{65,3},{4,70},{70... | collective-permute-start | bytes 6291464 | tf_op jit(solution)/shard_map/ppermute | solution.py:221
  102.4 44.3 %all-gather.5.cloned.1.call-done.k_ref.v_ref = bf16[2,16384,128]{2,1,0:T(8,128)(2,1)} async-done(((bf16[2,1024,128]{2,1,0:T(8,128)(2,1)}), bf16[2,16384,128]{2,1,0:T(8,128)(2,1)}) %all-gather.5.cloned.1.call-update) | async-done | bytes 8388624 | tf_op jit(solution)/shard_map/all_gather | solution.py:207
  146.7 44.3 %shard_map.82 = bf16[1024,256]{1,0:T(8,128)(2,1)} custom-call(s32[2,9]{1,0:T(2,128)} %copy.50.tbl_ref, s32[2,9]{1,0:T(2,128)} %copy-done.6, s32[2]{0:T(128)} %copy-done.7, bf16[1024,256]{1,0:T(8,128)(2,1)} %fusion.18.q_ref, s32[1024,1]{1,0:T(8,128)} %fusion.17.qpos_ref, s32[1024,1]{1,0:T(8,128)} %copy.51.qstart_ref, ...), custom_call_target="tpu_custom_call" | custom-call | flops 4831838208 | bytes 5767168 | tf_op jit(solution)/shard_map/pallas_call | solution.py:91
  192.0 2.9 %collective-permute-start.3 = (bf16[512,256]{1,0:T(8,128)(2,1)S(1)}, bf16[512,256]{1,0:T(8,128)(2,1)S(1)}, u32[]{:S(2)}, u32[]{:S(2)}) collective-permute-start(bf16[512,256]{1,0:T(8,128)(2,1)S(1)} %get-tuple-element.37), channel_id=1, source_target_pairs={{0,64},{64,0},{1,65},{65,1},{2,66},{66,2},{3,67},{67,3},{4,68},{68... | collective-permute-start | bytes 786440 | tf_op jit(solution)/shard_map/ppermute | solution.py:225
  194.9 5.1 %collective-permute-done.3 = bf16[512,256]{1,0:T(8,128)(2,1)S(1)} collective-permute-done((bf16[512,256]{1,0:T(8,128)(2,1)S(1)}, bf16[512,256]{1,0:T(8,128)(2,1)S(1)}, u32[]{:S(2)}, u32[]{:S(2)}) %collective-permute-start.3) | collective-permute-done | bytes 262176 | tf_op jit(solution)/shard_map/ppermute | solution.py:225
  200.0 4.6 %convolution_convert_fusion = bf16[512,4096]{1,0:T(8,128)(2,1)S(1)} fusion(bf16[256,4096]{1,0:T(8,128)(2,1)} %collective-permute-done.4, bf16[256,4096]{1,0:T(8,128)(2,1)} %param.15, bf16[512,256]{1,0:T(8,128)(2,1)S(1)} %collective-permute-done.3, bf16[512,256]{1,0:T(8,128)(2,1)S(1)} %get-tuple-element.36), kind=kOutput, calls=%fused_computation | convolution fusion | flops 2159017984 | bytes 8912896 | tf_op jit(solution)/shard_map/dot_general | solution.py:226
  204.9 1.6 copy-done
  206.5 1.5 collective-permute-start.5
  208.0 2.8 %collective-permute-start.6 = (bf16[128,4096]{1,0:T(8,128)(2,1)S(1)}, bf16[128,4096]{1,0:T(8,128)(2,1)}, u32[]{:S(2)}, u32[]{:S(2)}) collective-permute-start(bf16[128,4096]{1,0:T(8,128)(2,1)S(1)} %get-tuple-element.27), channel_id=1, source_target_pairs={{0,32},{16,48},{32,0},{48,16},{1,33},{17,49},{33,1},{49,17},{2,34}... | collective-permute-start | bytes 3145736 | tf_op jit(solution)/shard_map/ppermute | solution.py:140
  210.7 1.4 collective-permute-start.7
  212.1 18.2 %collective-permute-done.5 = bf16[128,4096]{1,0:T(8,128)(2,1)} collective-permute-done((bf16[128,4096]{1,0:T(8,128)(2,1)S(1)}, bf16[128,4096]{1,0:T(8,128)(2,1)}, u32[]{:S(2)}, u32[]{:S(2)}) %collective-permute-start.5) | collective-permute-done | bytes 1048608 | tf_op jit(solution)/shard_map/ppermute | solution.py:140
  230.4 11.2 %collective-permute-done.6 = bf16[128,4096]{1,0:T(8,128)(2,1)} collective-permute-done((bf16[128,4096]{1,0:T(8,128)(2,1)S(1)}, bf16[128,4096]{1,0:T(8,128)(2,1)}, u32[]{:S(2)}, u32[]{:S(2)}) %collective-permute-start.6) | collective-permute-done | bytes 1048608 | tf_op jit(solution)/shard_map/ppermute | solution.py:140
  241.6 3.8 %fusion.15 = bf16[1,128,4096]{2,1,0:T(8,128)(2,1)} fusion(bf16[128,4096]{1,0:T(8,128)(2,1)} %collective-permute-done.7, bf16[128,4096]{1,0:T(8,128)(2,1)} %collective-permute-done.6, bf16[128,4096]{1,0:T(8,128)(2,1)} %collective-permute-done.5, bf16[4,128,4096]{2,1,0:T(8,128)(2,1)} %bitcast.48, s32[]{:T(128)S(6)} %select_n.128, pred[]{:T(512)S(6)} %and.74), kind=kLoop, calls=%fused_computation.21 | loop fusion | flops 4718592 | bytes 5242885 | tf_op jit(solution)/shard_map/reshape | solution.py:232
  (92 shorter events, 19.3 us)
Async XLA Ops:
  6.5 4.3 %copy-start.3 = (bf16[4096,256]{1,0:T(8,128)(2,1)S(1)}, bf16[4096,256]{1,0:T(8,128)(2,1)}, u32[]{:S(2)}) copy-start(bf16[4096,256]{1,0:T(8,128)(2,1)} %param.12) | copy-start | bytes 6291460
  6.5 56.7 %all-gather.3.cloned.1.call-start = ((), (), s32[]{:S(2)}) async-start(), calls=%async_computation | async-start | bytes 5242880 | tf_op jit(solution)/shard_map/all_gather | solution.py:175
  10.8 135.9 %all-gather.5.cloned.1.call-start = ((), (), s32[]{:S(2)}) async-start(), calls=%async_computation.1 | async-start | bytes 8912896 | tf_op jit(solution)/shard_map/all_gather | solution.py:207
  10.8 1.2 copy-start.4
  10.8 1.5 copy-start.5
  12.6 2.0 copy-start.1
  12.6 50.6 %copy-start.9 = (s32[32]{0:T(128)S(1)}, s32[32]{0:T(128)}, u32[]{:S(2)}) copy-start(s32[32]{0:T(128)} %param.17) | copy-start | bytes 388
  14.6 48.6 %collective-permute-start = (bf16[2048,512]{1,0:T(8,128)(2,1)S(1)}, bf16[2048,512]{1,0:T(8,128)(2,1)S(1)}, u32[]{:S(2)}, u32[]{:S(2)}) collective-permute-start(bf16[2048,512]{1,0:T(8,128)(2,1)S(1)} %constant_dynamic-slice_fusion.2), channel_id=1, source_target_pairs={{0,66},{66,0},{2,64},{64,2},{1,67},{67,1},{3,65},{65,3},{4,70},{70... | collective-permute-start | bytes 6291464 | tf_op jit(solution)/shard_map/ppermute | solution.py:176
  63.2 4.3 %collective-permute-start.1 = (bf16[2048,512]{1,0:T(8,128)(2,1)S(1)}, bf16[2048,512]{1,0:T(8,128)(2,1)}, u32[]{:S(2)}, u32[]{:S(2)}) collective-permute-start(bf16[2048,512]{1,0:T(8,128)(2,1)S(1)} %collective-permute-done), channel_id=1, source_target_pairs={{0,1},{1,0},{2,3},{3,2},{4,5},{5,4},{6,7},{7,6},{8,9},{9,8},{10,11... | collective-permute-start | bytes 6291464 | tf_op jit(solution)/shard_map/ppermute | solution.py:178
  64.5 6.5 %copy-start.10 = (bf16[1,512,4096]{2,1,0:T(8,128)(2,1)S(1)}, bf16[1,512,4096]{2,1,0:T(8,128)(2,1)}, u32[]{:S(2)}) copy-start(bf16[1,512,4096]{2,1,0:T(8,128)(2,1)} %all-gather.3.cloned.1.call-done) | copy-start | bytes 12582916
  72.7 5.7 %copy-start.2 = (bf16[4096,512]{1,0:T(8,128)(2,1)S(1)}, bf16[4096,512]{1,0:T(8,128)(2,1)}, u32[]{:S(2)}) copy-start(bf16[4096,512]{1,0:T(8,128)(2,1)} %copy-done.1) | copy-start | bytes 12582916
  76.5 15.7 %collective-permute-start.2 = (bf16[512,512]{1,0:T(8,128)(2,1)}, bf16[512,512]{1,0:T(8,128)(2,1)S(1)}, u32[]{:S(2)}, u32[]{:S(2)}) collective-permute-start(bf16[512,512]{1,0:T(8,128)(2,1)} %pad_maximum_fusion), channel_id=1, source_target_pairs={{0,64},{64,0},{1,65},{65,1},{2,66},{66,2},{3,67},{67,3},{4,68},{68... | collective-permute-start | bytes 1572872 | tf_op jit(solution)/shard_map/ppermute | solution.py:199
  92.4 4.3 %copy-start.8 = (s32[16]{0:T(128)S(1)}, s32[16]{0:T(128)}, u32[]{:S(2)}) copy-start(s32[16]{0:T(128)} %param.16) | copy-start | bytes 196
  93.3 101.6 %collective-permute-start.4 = (bf16[256,4096]{1,0:T(8,128)(2,1)}, bf16[256,4096]{1,0:T(8,128)(2,1)}, u32[]{:S(2)}, u32[]{:S(2)}) collective-permute-start(bf16[256,4096]{1,0:T(8,128)(2,1)} %param.15), channel_id=1, source_target_pairs={{0,66},{66,0},{2,64},{64,2},{1,67},{67,1},{3,65},{65,3},{4,70},{70... | collective-permute-start | bytes 6291464 | tf_op jit(solution)/shard_map/ppermute | solution.py:221
  97.8 48.8 %copy-start.7 = (s32[2]{0:T(128)}, s32[2]{0:T(128)S(1)}, u32[]{:S(2)}) copy-start(s32[2]{0:T(128)S(1)} %fusion.56.cnt_ref) | copy-start | bytes 28
  97.9 48.8 %copy-start.6 = (s32[2,9]{1,0:T(2,128)}, s32[2,9]{1,0:T(2,128)S(1)}, u32[]{:S(2)}) copy-start(s32[2,9]{1,0:T(2,128)S(1)} %add_minimum_fusion.seq_ref) | copy-start | bytes 220
  192.0 8.0 %collective-permute-start.3 = (bf16[512,256]{1,0:T(8,128)(2,1)S(1)}, bf16[512,256]{1,0:T(8,128)(2,1)S(1)}, u32[]{:S(2)}, u32[]{:S(2)}) collective-permute-start(bf16[512,256]{1,0:T(8,128)(2,1)S(1)} %get-tuple-element.37), channel_id=1, source_target_pairs={{0,64},{64,0},{1,65},{65,1},{2,66},{66,2},{3,67},{67,3},{4,68},{68... | collective-permute-start | bytes 786440 | tf_op jit(solution)/shard_map/ppermute | solution.py:225
  204.6 1.9 copy-start
  206.5 23.9 %collective-permute-start.5 = (bf16[128,4096]{1,0:T(8,128)(2,1)S(1)}, bf16[128,4096]{1,0:T(8,128)(2,1)}, u32[]{:S(2)}, u32[]{:S(2)}) collective-permute-start(bf16[128,4096]{1,0:T(8,128)(2,1)S(1)} %get-tuple-element.25), channel_id=1, source_target_pairs={{0,16},{16,32},{32,48},{48,0},{1,17},{17,33},{33,49},{49,1},{2,18}... | collective-permute-start | bytes 3145736 | tf_op jit(solution)/shard_map/ppermute | solution.py:140
  208.0 33.7 %collective-permute-start.6 = (bf16[128,4096]{1,0:T(8,128)(2,1)S(1)}, bf16[128,4096]{1,0:T(8,128)(2,1)}, u32[]{:S(2)}, u32[]{:S(2)}) collective-permute-start(bf16[128,4096]{1,0:T(8,128)(2,1)S(1)} %get-tuple-element.27), channel_id=1, source_target_pairs={{0,32},{16,48},{32,0},{48,16},{1,33},{17,49},{33,1},{49,17},{2,34}... | collective-permute-start | bytes 3145736 | tf_op jit(solution)/shard_map/ppermute | solution.py:140
  210.7 30.9 %collective-permute-start.7 = (bf16[128,4096]{1,0:T(8,128)(2,1)S(1)}, bf16[128,4096]{1,0:T(8,128)(2,1)}, u32[]{:S(2)}, u32[]{:S(2)}) collective-permute-start(bf16[128,4096]{1,0:T(8,128)(2,1)S(1)} %get-tuple-element.26), channel_id=1, source_target_pairs={{0,48},{16,0},{32,16},{48,32},{1,49},{17,1},{33,17},{49,33},{2,50}... | collective-permute-start | bytes 3145736 | tf_op jit(solution)/shard_map/ppermute | solution.py:140
Sparse Core Ops, SparseCore 0:
  10.9 49.5 all-gather.2
  93.4 53.1 all-gather.4

commit v9 on v8

--- a/solution.py
+++ b/solution.py
@@ -39,7 +39,7 @@
     )
 
 
-def attention_kernel(heads, scale, tbl_ref, seq_ref, cnt_ref, q_ref, qpos_ref, qstart_ref,
+def attention_kernel(heads, scale, tbl_ref, seq_ref, cnt_ref, full_ref, q_ref, qpos_ref, qstart_ref,
                      k_ref, v_ref, o_ref, m_sc, l_sc, acc_sc):
     i = pl.program_id(0)
     j = pl.program_id(1)
@@ -50,34 +50,44 @@
         l_sc[...] = jnp.zeros_like(l_sc)
         acc_sc[...] = jnp.zeros_like(acc_sc)
 
-    @pl.when(j < cnt_ref[i])
-    def _():
+    def update(visible):
         k = k_ref[...]
         v = v_ref[...]
-        span = k.shape[0]
-        kpos = seq_ref[i, j] * span + lax.broadcasted_iota(jnp.int32, (1, span), 1)
-        visible = (kpos <= qpos_ref[...]) & (kpos >= qstart_ref[...])
         for h in range(heads):
             q = q_ref[:, h * HEAD_DIM:(h + 1) * HEAD_DIM]
             s = lax.dot_general(q, k, (((1,), (1,)), ((), ())),
                                 preferred_element_type=jnp.float32) * scale
+            if visible is not None:
+                s = jnp.where(visible, s, masked_score)
             m_old = m_sc[h]
-            m_new = jnp.maximum(
-                m_old, jnp.max(jnp.where(visible, s, masked_score), axis=-1, keepdims=True))
-            p = jnp.where(visible, jnp.exp(s - m_new), 0.0)
+            m_new = jnp.maximum(m_old, jnp.max(s, axis=-1, keepdims=True))
+            p = jnp.exp(s - m_new)
             alpha = jnp.exp(m_old - m_new)
             l_sc[h] = alpha * l_sc[h] + jnp.sum(p, axis=-1, keepdims=True)
             acc_sc[h] = alpha * acc_sc[h] + jnp.dot(
                 p.astype(jnp.bfloat16), v, preferred_element_type=jnp.float32)
             m_sc[h] = m_new
 
+    live = j < cnt_ref[i]
+    full = full_ref[i, j] == 1
+
+    @pl.when(live & full)
+    def _():
+        update(None)
+
+    @pl.when(live & jnp.logical_not(full))
+    def _():
+        span = k_ref.shape[0]
+        kpos = seq_ref[i, j] * span + lax.broadcasted_iota(jnp.int32, (1, span), 1)
+        update((kpos <= qpos_ref[...]) & (kpos >= qstart_ref[...]))
+
     @pl.when(j == pl.num_programs(1) - 1)
     def _():
         for h in range(heads):
             o_ref[:, h * HEAD_DIM:(h + 1) * HEAD_DIM] = (acc_sc[h] / l_sc[h]).astype(o_ref.dtype)
 
 
-def span_attention(tbl, seq, cnt, queries, qpos, qstart, kv):
+def span_attention(tbl, seq, cnt, full, queries, qpos, qstart, kv):
     rows, q_cols = queries.shape
     heads = q_cols // HEAD_DIM
     n_q = rows // SPAN
@@ -92,16 +102,16 @@
         kernel,
         out_shape=jax.ShapeDtypeStruct((rows, q_cols), jnp.bfloat16),
         grid_spec=pltpu.PrefetchScalarGridSpec(
-            num_scalar_prefetch=3,
+            num_scalar_prefetch=4,
             grid=(n_q, KEY_SLOTS),
             in_specs=[
-                pl.BlockSpec((SPAN, q_cols), lambda i, j, t, s, c: (i, 0)),
-                pl.BlockSpec((SPAN, 1), lambda i, j, t, s, c: (i, 0)),
-                pl.BlockSpec((SPAN, 1), lambda i, j, t, s, c: (i, 0)),
-                pl.BlockSpec((None, SPAN, HEAD_DIM), lambda i, j, t, s, c: (0, t[i, j], 0)),
-                pl.BlockSpec((None, SPAN, HEAD_DIM), lambda i, j, t, s, c: (1, t[i, j], 0)),
+                pl.BlockSpec((SPAN, q_cols), lambda i, j, t, s, c, f: (i, 0)),
+                pl.BlockSpec((SPAN, 1), lambda i, j, t, s, c, f: (i, 0)),
+                pl.BlockSpec((SPAN, 1), lambda i, j, t, s, c, f: (i, 0)),
+                pl.BlockSpec((None, SPAN, HEAD_DIM), lambda i, j, t, s, c, f: (0, t[i, j], 0)),
+                pl.BlockSpec((None, SPAN, HEAD_DIM), lambda i, j, t, s, c, f: (1, t[i, j], 0)),
             ],
-            out_specs=pl.BlockSpec((SPAN, q_cols), lambda i, j, t, s, c: (i, 0)),
+            out_specs=pl.BlockSpec((SPAN, q_cols), lambda i, j, t, s, c, f: (i, 0)),
             scratch_shapes=[
                 pltpu.VMEM((heads, SPAN, 1), jnp.float32),
                 pltpu.VMEM((heads, SPAN, 1), jnp.float32),
@@ -110,7 +120,7 @@
         ),
         compiler_params=pltpu.CompilerParams(dimension_semantics=("arbitrary", "arbitrary")),
         cost_estimate=cost,
-    )(tbl, seq, cnt, queries, qpos, qstart, kv, kv)
+    )(tbl, seq, cnt, full, queries, qpos, qstart, kv, kv)
 
 
 def key_tables(span_order, doc_ends, query_spans):
@@ -133,7 +143,11 @@
     seq = jnp.minimum(sq[:, None] - count[:, None] + 1 + slot[None, :], sq[:, None])
     tbl = jnp.sum(jnp.where(seq[:, :, None] == span_ids[None, None, :], inverse[None, None, :], 0),
                   axis=2)
-    return tbl.astype(jnp.int32), seq.astype(jnp.int32), count.astype(jnp.int32)
+    last_start = jnp.max(
+        jnp.where(doc_ends[None, :] <= (sq * SPAN + SPAN - 1)[:, None], doc_ends[None, :], 0), axis=1)
+    full = (seq < sq[:, None]) & (seq * SPAN >= last_start[:, None])
+    return (tbl.astype(jnp.int32), seq.astype(jnp.int32), count.astype(jnp.int32),
+            full.astype(jnp.int32))
 
 
 def shift_x(value, d, n):
@@ -212,9 +226,9 @@
     query_start = jnp.max(
         jnp.where(doc_ends[None, :] <= places[:, None], doc_ends[None, :], 0), axis=1)
     query_spans = lax.axis_index(CONTEXT) * 2 + jnp.arange(2, dtype=jnp.int32)
-    tbl, seq, cnt = key_tables(span_order, doc_ends, query_spans)
+    tbl, seq, cnt, full = key_tables(span_order, doc_ends, query_spans)
     attended = span_attention(
-        tbl, seq, cnt, query_rows,
+        tbl, seq, cnt, full, query_rows,
         places.astype(jnp.int32)[:, None], query_start.astype(jnp.int32)[:, None],
         gathered,
     )

time: 253 us -> 253 us (level)
  the two profiles are of different devices: /device:TPU:96 before, /device:TPU:8 now
where the time goes in v9:
time: 253 us
  waiting for transfers between devices  143 us (57%)
  Pallas kernels  36 us (14%)
  other arithmetic  21.4 us (8%)
  starting transfers between devices  14.5 us (6%)
  matrix products  13.9 us (5%)
  between operations  13.8 us (5%)
  local copies, waits for them, and re-layouts  10 us (4%)
    all_gather x1, waiting for transfers between devices, per_device(): gathered = lax.all_gather(kv_pair, CONTEXT, axis=1, tiled=True)  47.1 us
    ppermute x1, waiting for transfers between devices, per_device(): partner_half = lax.ppermute(sent_half, ('yh', 'ylo'), NEIGHBOUR)  45.8 us
    ppermute x3, waiting for transfers between devices, shift_x(): return lax.ppermute(value, 'x', [(i, (i + d) % n) for i in range(n)])  36.8 us
    pallas_call x1, Pallas kernels, span_attention(): pl.pallas_call(kernel, out_shape=jax.ShapeDtypeStruct((rows, q_cols), jnp...  36 us
    ppermute x1, waiting for transfers between devices, per_device(): partner_rows = lax.ppermute(other_rows, 'yh', [(0, 1), (1, 0)])  5.76 us
    unnamed x30, local copies, waits for them, and re-layouts  5.76 us
    ppermute x3, starting transfers between devices, shift_x(): return lax.ppermute(value, 'x', [(i, (i + d) % n) for i in range(n)])  5.61 us
  transfers between devices with their start and end apart: 10, of which 7 were waited for; matrix products, arithmetic and copies ran while one was open for 7% of the time, Pallas kernels for 14%

profile of v9, /device:TPU:8, one launch (start us, length us, event | category | flops | bytes accessed | tf_op | source)
XLA Modules:
  0.0 252.6 jit_solution(6485929289156388847)
XLA Ops:
  6.5 1.7 fusion.3
  8.2 2.5 %fusion.5 = bf16[1,128,4096]{2,1,0:T(8,128)(2,1)} fusion(bf16[1,128,4096]{2,1,0:T(8,128)(2,1)} %param.10, f32[4096]{0:T(1024)} %param.11, f32[128]{0:T(128)S(1)} %add_rsqrt_fusion), kind=kLoop, calls=%fused_computation.8 | loop fusion | flops 2097152 | bytes 2114048 | tf_op jit(solution)/shard_map/convert_element_type | solution.py:183
  12.8 1.8 copy-done.1
  14.6 1.6 collective-permute-start
  16.2 45.8 %collective-permute-done = bf16[2048,512]{1,0:T(8,128)(2,1)S(1)} collective-permute-done((bf16[2048,512]{1,0:T(8,128)(2,1)S(1)}, bf16[2048,512]{1,0:T(8,128)(2,1)S(1)}, u32[]{:S(2)}, u32[]{:S(2)}) %collective-permute-start) | collective-permute-done | bytes 2097184 | tf_op jit(solution)/shard_map/ppermute | solution.py:190
  63.2 3.1 %collective-permute-done.1 = bf16[2048,512]{1,0:T(8,128)(2,1)} collective-permute-done((bf16[2048,512]{1,0:T(8,128)(2,1)S(1)}, bf16[2048,512]{1,0:T(8,128)(2,1)}, u32[]{:S(2)}, u32[]{:S(2)}) %collective-permute-start.1) | collective-permute-done | bytes 2097184 | tf_op jit(solution)/shard_map/ppermute | solution.py:192
  66.3 3.5 %fusion.6 = f32[512,512]{1,0:T(8,128)S(1)} fusion(bf16[2048,512]{1,0:T(8,128)(2,1)} %collective-permute-done.1, bf16[1,512,4096]{2,1,0:T(8,128)(2,1)} %all-gather.3.cloned.1.call-done, s32[]{:T(128)S(6)} %select_n.110), kind=kOutput, calls=%fused_computation.9 | convolution fusion | flops 1073741824 | bytes 5242884 | tf_op jit(solution)/shard_map/dot_general | solution.py:212
  69.7 1.3 fusion.12
  75.2 3.5 %collective-permute-start.2 = (bf16[512,512]{1,0:T(8,128)(2,1)}, bf16[512,512]{1,0:T(8,128)(2,1)S(1)}, u32[]{:S(2)}, u32[]{:S(2)}) collective-permute-start(bf16[512,512]{1,0:T(8,128)(2,1)} %pad_maximum_fusion), channel_id=1, source_target_pairs={{0,64},{64,0},{1,65},{65,1},{2,66},{66,2},{3,67},{67,3},{4,68},{68... | collective-permute-start | bytes 1572872 | tf_op jit(solution)/shard_map/ppermute | solution.py:213
  78.7 4.6 %fusion.60 = f32[512,512]{0,1:T(8,128)S(1)} fusion(bf16[512,4096]{1,0:T(8,128)(2,1)} %bitcast.58, bf16[4096,512]{1,0:T(8,128)(2,1)S(1)} %copy-done.2), kind=kOutput, calls=%fused_computation.133 | convolution fusion | flops 2147483648 | bytes 9437184 | tf_op jit(solution)/shard_map/dot_general | solution.py:208
  86.9 4.3 %collective-permute-done.2 = bf16[512,512]{1,0:T(8,128)(2,1)S(1)} collective-permute-done((bf16[512,512]{1,0:T(8,128)(2,1)}, bf16[512,512]{1,0:T(8,128)(2,1)S(1)}, u32[]{:S(2)}, u32[]{:S(2)}) %collective-permute-start.2) | collective-permute-done | bytes 524320 | tf_op jit(solution)/shard_map/ppermute | solution.py:213
  92.3 1.4 collective-permute-start.4
  100.6 47.1 %all-gather.5.cloned.1.call-done.k_ref.v_ref = bf16[2,16384,128]{2,1,0:T(8,128)(2,1)} async-done(((bf16[2,1024,128]{2,1,0:T(8,128)(2,1)}), bf16[2,16384,128]{2,1,0:T(8,128)(2,1)}) %all-gather.5.cloned.1.call-update) | async-done | bytes 8388624 | tf_op jit(solution)/shard_map/all_gather | solution.py:221
  147.7 36.0 %shard_map.82 = bf16[1024,256]{1,0:T(8,128)(2,1)} custom-call(s32[2,9]{1,0:T(2,128)} %copy.50.tbl_ref, s32[2,9]{1,0:T(2,128)} %copy-done.6, s32[2]{0:T(128)} %copy-done.7, s32[2,9]{1,0:T(2,128)} %and_convert_fusion.full_ref, bf16[1024,256]{1,0:T(8,128)(2,1)} %fusion.18.q_ref, s32[1024,1]{1,0:T(8,128)} %fusion.17.qpos_ref, s32[1024,1]{1,0:T(8,128)} %copy.51.qstart_ref, ...), custom_call_target="tpu_custom_call" | custom-call | flops 4831838208 | bytes 5767168 | tf_op jit(solution)/shard_map/pallas_call | solution.py:101
  184.8 2.4 collective-permute-start.3
  187.2 5.8 %collective-permute-done.3 = bf16[512,256]{1,0:T(8,128)(2,1)S(1)} collective-permute-done((bf16[512,256]{1,0:T(8,128)(2,1)S(1)}, bf16[512,256]{1,0:T(8,128)(2,1)S(1)}, u32[]{:S(2)}, u32[]{:S(2)}) %collective-permute-start.3) | collective-permute-done | bytes 262176 | tf_op jit(solution)/shard_map/ppermute | solution.py:239
  193.0 4.6 %convolution_convert_fusion = bf16[512,4096]{1,0:T(8,128)(2,1)S(1)} fusion(bf16[256,4096]{1,0:T(8,128)(2,1)} %collective-permute-done.4, bf16[256,4096]{1,0:T(8,128)(2,1)} %param.15, bf16[512,256]{1,0:T(8,128)(2,1)S(1)} %collective-permute-done.3, bf16[512,256]{1,0:T(8,128)(2,1)S(1)} %get-tuple-element.36), kind=kOutput, calls=%fused_computation | convolution fusion | flops 2159017984 | bytes 8912896 | tf_op jit(solution)/shard_map/dot_general | solution.py:240
  197.8 1.6 copy-done
  199.5 1.5 collective-permute-start.5
  200.9 2.7 %collective-permute-start.6 = (bf16[128,4096]{1,0:T(8,128)(2,1)S(1)}, bf16[128,4096]{1,0:T(8,128)(2,1)}, u32[]{:S(2)}, u32[]{:S(2)}) collective-permute-start(bf16[128,4096]{1,0:T(8,128)(2,1)S(1)} %get-tuple-element.27), channel_id=1, source_target_pairs={{0,32},{16,48},{32,0},{48,16},{1,33},{17,49},{33,1},{49,17},{2,34}... | collective-permute-start | bytes 3145736 | tf_op jit(solution)/shard_map/ppermute | solution.py:154
  203.6 1.5 collective-permute-start.7
  205.1 20.9 %collective-permute-done.5 = bf16[128,4096]{1,0:T(8,128)(2,1)} collective-permute-done((bf16[128,4096]{1,0:T(8,128)(2,1)S(1)}, bf16[128,4096]{1,0:T(8,128)(2,1)}, u32[]{:S(2)}, u32[]{:S(2)}) %collective-permute-start.5) | collective-permute-done | bytes 1048608 | tf_op jit(solution)/shard_map/ppermute | solution.py:154
  226.0 15.9 %collective-permute-done.6 = bf16[128,4096]{1,0:T(8,128)(2,1)} collective-permute-done((bf16[128,4096]{1,0:T(8,128)(2,1)S(1)}, bf16[128,4096]{1,0:T(8,128)(2,1)}, u32[]{:S(2)}, u32[]{:S(2)}) %collective-permute-start.6) | collective-permute-done | bytes 1048608 | tf_op jit(solution)/shard_map/ppermute | solution.py:154
  241.9 3.8 %fusion.15 = bf16[1,128,4096]{2,1,0:T(8,128)(2,1)} fusion(bf16[128,4096]{1,0:T(8,128)(2,1)} %collective-permute-done.7, bf16[128,4096]{1,0:T(8,128)(2,1)} %collective-permute-done.6, bf16[128,4096]{1,0:T(8,128)(2,1)} %collective-permute-done.5, bf16[4,128,4096]{2,1,0:T(8,128)(2,1)} %bitcast.48, s32[]{:T(128)S(6)} %select_n.133, pred[]{:T(512)S(6)} %and.78), kind=kLoop, calls=%fused_computation.21 | loop fusion | flops 4718592 | bytes 5242885 | tf_op jit(solution)/shard_map/reshape | solution.py:246
  (94 shorter events, 20.1 us)
Async XLA Ops:
  6.5 4.3 %copy-start.3 = (bf16[4096,256]{1,0:T(8,128)(2,1)S(1)}, bf16[4096,256]{1,0:T(8,128)(2,1)}, u32[]{:S(2)}) copy-start(bf16[4096,256]{1,0:T(8,128)(2,1)} %param.12) | copy-start | bytes 6291460
  6.5 55.4 %all-gather.3.cloned.1.call-start = ((), (), s32[]{:S(2)}) async-start(), calls=%async_computation | async-start | bytes 5242880 | tf_op jit(solution)/shard_map/all_gather | solution.py:189
  10.8 136.9 %all-gather.5.cloned.1.call-start = ((), (), s32[]{:S(2)}) async-start(), calls=%async_computation.1 | async-start | bytes 8912896 | tf_op jit(solution)/shard_map/all_gather | solution.py:221
  10.8 1.2 copy-start.4
  10.8 1.5 copy-start.5
  12.6 2.0 copy-start.1
  12.6 49.4 %copy-start.9 = (s32[32]{0:T(128)S(1)}, s32[32]{0:T(128)}, u32[]{:S(2)}) copy-start(s32[32]{0:T(128)} %param.17) | copy-start | bytes 388
  14.6 47.4 %collective-permute-start = (bf16[2048,512]{1,0:T(8,128)(2,1)S(1)}, bf16[2048,512]{1,0:T(8,128)(2,1)S(1)}, u32[]{:S(2)}, u32[]{:S(2)}) collective-permute-start(bf16[2048,512]{1,0:T(8,128)(2,1)S(1)} %constant_dynamic-slice_fusion.2), channel_id=1, source_target_pairs={{0,66},{66,0},{2,64},{64,2},{1,67},{67,1},{3,65},{65,3},{4,70},{70... | collective-permute-start | bytes 6291464 | tf_op jit(solution)/shard_map/ppermute | solution.py:190
  62.0 4.3 %collective-permute-start.1 = (bf16[2048,512]{1,0:T(8,128)(2,1)S(1)}, bf16[2048,512]{1,0:T(8,128)(2,1)}, u32[]{:S(2)}, u32[]{:S(2)}) collective-permute-start(bf16[2048,512]{1,0:T(8,128)(2,1)S(1)} %collective-permute-done), channel_id=1, source_target_pairs={{0,1},{1,0},{2,3},{3,2},{4,5},{5,4},{6,7},{7,6},{8,9},{9,8},{10,11... | collective-permute-start | bytes 6291464 | tf_op jit(solution)/shard_map/ppermute | solution.py:192
  63.2 6.5 %copy-start.10 = (bf16[1,512,4096]{2,1,0:T(8,128)(2,1)S(1)}, bf16[1,512,4096]{2,1,0:T(8,128)(2,1)}, u32[]{:S(2)}) copy-start(bf16[1,512,4096]{2,1,0:T(8,128)(2,1)} %all-gather.3.cloned.1.call-done) | copy-start | bytes 12582916
  71.4 7.3 %copy-start.2 = (bf16[4096,512]{1,0:T(8,128)(2,1)S(1)}, bf16[4096,512]{1,0:T(8,128)(2,1)}, u32[]{:S(2)}) copy-start(bf16[4096,512]{1,0:T(8,128)(2,1)} %copy-done.1) | copy-start | bytes 12582916
  75.2 15.9 %collective-permute-start.2 = (bf16[512,512]{1,0:T(8,128)(2,1)}, bf16[512,512]{1,0:T(8,128)(2,1)S(1)}, u32[]{:S(2)}, u32[]{:S(2)}) collective-permute-start(bf16[512,512]{1,0:T(8,128)(2,1)} %pad_maximum_fusion), channel_id=1, source_target_pairs={{0,64},{64,0},{1,65},{65,1},{2,66},{66,2},{3,67},{67,3},{4,68},{68... | collective-permute-start | bytes 1572872 | tf_op jit(solution)/shard_map/ppermute | solution.py:213
  91.4 2.7 %copy-start.8 = (s32[16]{0:T(128)S(1)}, s32[16]{0:T(128)}, u32[]{:S(2)}) copy-start(s32[16]{0:T(128)} %param.16) | copy-start | bytes 196
  92.3 94.9 %collective-permute-start.4 = (bf16[256,4096]{1,0:T(8,128)(2,1)}, bf16[256,4096]{1,0:T(8,128)(2,1)}, u32[]{:S(2)}, u32[]{:S(2)}) collective-permute-start(bf16[256,4096]{1,0:T(8,128)(2,1)} %param.15), channel_id=1, source_target_pairs={{0,66},{66,0},{2,64},{64,2},{1,67},{67,1},{3,65},{65,3},{4,70},{70... | collective-permute-start | bytes 6291464 | tf_op jit(solution)/shard_map/ppermute | solution.py:235
  95.2 52.5 %copy-start.7 = (s32[2]{0:T(128)}, s32[2]{0:T(128)S(1)}, u32[]{:S(2)}) copy-start(s32[2]{0:T(128)S(1)} %fusion.56.cnt_ref) | copy-start | bytes 28
  95.3 52.4 %copy-start.6 = (s32[2,9]{1,0:T(2,128)}, s32[2,9]{1,0:T(2,128)S(1)}, u32[]{:S(2)}) copy-start(s32[2,9]{1,0:T(2,128)S(1)} %add_minimum_fusion.seq_ref) | copy-start | bytes 220
  184.8 8.2 %collective-permute-start.3 = (bf16[512,256]{1,0:T(8,128)(2,1)S(1)}, bf16[512,256]{1,0:T(8,128)(2,1)S(1)}, u32[]{:S(2)}, u32[]{:S(2)}) collective-permute-start(bf16[512,256]{1,0:T(8,128)(2,1)S(1)} %get-tuple-element.37), channel_id=1, source_target_pairs={{0,64},{64,0},{1,65},{65,1},{2,66},{66,2},{3,67},{67,3},{4,68},{68... | collective-permute-start | bytes 786440 | tf_op jit(solution)/shard_map/ppermute | solution.py:239
  197.5 1.9 copy-start
  199.5 26.5 %collective-permute-start.5 = (bf16[128,4096]{1,0:T(8,128)(2,1)S(1)}, bf16[128,4096]{1,0:T(8,128)(2,1)}, u32[]{:S(2)}, u32[]{:S(2)}) collective-permute-start(bf16[128,4096]{1,0:T(8,128)(2,1)S(1)} %get-tuple-element.25), channel_id=1, source_target_pairs={{0,16},{16,32},{32,48},{48,0},{1,17},{17,33},{33,49},{49,1},{2,18}... | collective-permute-start | bytes 3145736 | tf_op jit(solution)/shard_map/ppermute | solution.py:154
  200.9 41.0 %collective-permute-start.6 = (bf16[128,4096]{1,0:T(8,128)(2,1)S(1)}, bf16[128,4096]{1,0:T(8,128)(2,1)}, u32[]{:S(2)}, u32[]{:S(2)}) collective-permute-start(bf16[128,4096]{1,0:T(8,128)(2,1)S(1)} %get-tuple-element.27), channel_id=1, source_target_pairs={{0,32},{16,48},{32,0},{48,16},{1,33},{17,49},{33,1},{49,17},{2,34}... | collective-permute-start | bytes 3145736 | tf_op jit(solution)/shard_map/ppermute | solution.py:154
  203.6 38.3 %collective-permute-start.7 = (bf16[128,4096]{1,0:T(8,128)(2,1)S(1)}, bf16[128,4096]{1,0:T(8,128)(2,1)}, u32[]{:S(2)}, u32[]{:S(2)}) collective-permute-start(bf16[128,4096]{1,0:T(8,128)(2,1)S(1)} %get-tuple-element.26), channel_id=1, source_target_pairs={{0,48},{16,0},{32,16},{48,32},{1,49},{17,1},{33,17},{49,33},{2,50}... | collective-permute-start | bytes 3145736 | tf_op jit(solution)/shard_map/ppermute | solution.py:154
Sparse Core Ops, SparseCore 0:
  10.9 50.5 all-gather.2
  92.4 55.1 all-gather.4

commit v10 on v9

--- a/solution.py
+++ b/solution.py
@@ -39,7 +39,7 @@
     )
 
 
-def attention_kernel(heads, scale, tbl_ref, seq_ref, cnt_ref, full_ref, q_ref, qpos_ref, qstart_ref,
+def attention_kernel(heads, scale, which_ref, tbl_ref, seq_ref, cnt_ref, full_ref, q_ref, qpos_ref, qstart_ref,
                      k_ref, v_ref, o_ref, m_sc, l_sc, acc_sc):
     i = pl.program_id(0)
     j = pl.program_id(1)
@@ -87,31 +87,31 @@
             o_ref[:, h * HEAD_DIM:(h + 1) * HEAD_DIM] = (acc_sc[h] / l_sc[h]).astype(o_ref.dtype)
 
 
-def span_attention(tbl, seq, cnt, full, queries, qpos, qstart, kv):
+def span_attention(which, tbl, seq, cnt, full, queries, qpos, qstart, kv):
     rows, q_cols = queries.shape
     heads = q_cols // HEAD_DIM
-    n_q = rows // SPAN
+    n_q = 1
     kernel = functools.partial(attention_kernel, heads, 1.0 / math.sqrt(HEAD_DIM))
     steps = n_q * KEY_SLOTS
     cost = pl.CostEstimate(
         flops=4 * steps * heads * SPAN * SPAN * HEAD_DIM,
         transcendentals=steps * heads * SPAN * SPAN,
-        bytes_accessed=steps * 2 * SPAN * HEAD_DIM * 2 + 2 * rows * q_cols * 2,
+        bytes_accessed=steps * 2 * SPAN * HEAD_DIM * 2 + 2 * SPAN * q_cols * 2,
     )
     return pl.pallas_call(
         kernel,
-        out_shape=jax.ShapeDtypeStruct((rows, q_cols), jnp.bfloat16),
+        out_shape=jax.ShapeDtypeStruct((SPAN, q_cols), jnp.bfloat16),
         grid_spec=pltpu.PrefetchScalarGridSpec(
-            num_scalar_prefetch=4,
+            num_scalar_prefetch=5,
             grid=(n_q, KEY_SLOTS),
             in_specs=[
-                pl.BlockSpec((SPAN, q_cols), lambda i, j, t, s, c, f: (i, 0)),
-                pl.BlockSpec((SPAN, 1), lambda i, j, t, s, c, f: (i, 0)),
-                pl.BlockSpec((SPAN, 1), lambda i, j, t, s, c, f: (i, 0)),
-                pl.BlockSpec((None, SPAN, HEAD_DIM), lambda i, j, t, s, c, f: (0, t[i, j], 0)),
-                pl.BlockSpec((None, SPAN, HEAD_DIM), lambda i, j, t, s, c, f: (1, t[i, j], 0)),
+                pl.BlockSpec((SPAN, q_cols), lambda i, j, w, t, s, c, f: (w[0], 0)),
+                pl.BlockSpec((SPAN, 1), lambda i, j, w, t, s, c, f: (w[0], 0)),
+                pl.BlockSpec((SPAN, 1), lambda i, j, w, t, s, c, f: (w[0], 0)),
+                pl.BlockSpec((None, SPAN, HEAD_DIM), lambda i, j, w, t, s, c, f: (0, t[i, j], 0)),
+                pl.BlockSpec((None, SPAN, HEAD_DIM), lambda i, j, w, t, s, c, f: (1, t[i, j], 0)),
             ],
-            out_specs=pl.BlockSpec((SPAN, q_cols), lambda i, j, t, s, c, f: (i, 0)),
+            out_specs=pl.BlockSpec((SPAN, q_cols), lambda i, j, w, t, s, c, f: (0, 0)),
             scratch_shapes=[
                 pltpu.VMEM((heads, SPAN, 1), jnp.float32),
                 pltpu.VMEM((heads, SPAN, 1), jnp.float32),
@@ -120,7 +120,7 @@
         ),
         compiler_params=pltpu.CompilerParams(dimension_semantics=("arbitrary", "arbitrary")),
         cost_estimate=cost,
-    )(tbl, seq, cnt, full, queries, qpos, qstart, kv, kv)
+    )(which, tbl, seq, cnt, full, queries, qpos, qstart, kv, kv)
 
 
 def key_tables(span_order, doc_ends, query_spans):
@@ -227,16 +227,20 @@
         jnp.where(doc_ends[None, :] <= places[:, None], doc_ends[None, :], 0), axis=1)
     query_spans = lax.axis_index(CONTEXT) * 2 + jnp.arange(2, dtype=jnp.int32)
     tbl, seq, cnt, full = key_tables(span_order, doc_ends, query_spans)
-    attended = span_attention(
-        tbl, seq, cnt, full, query_rows,
-        places.astype(jnp.int32)[:, None], query_start.astype(jnp.int32)[:, None],
-        gathered,
-    )
+    plane_q = lax.axis_index("yh")
+    qpos_col = places.astype(jnp.int32)[:, None]
+    qstart_col = query_start.astype(jnp.int32)[:, None]
+
+    def attend(which):
+        pick = lambda a: lax.dynamic_slice_in_dim(a, which, 1, 0)
+        return span_attention(
+            jnp.reshape(which, (1,)).astype(jnp.int32), pick(tbl), pick(seq), pick(cnt), pick(full),
+            query_rows, qpos_col, qstart_col, gathered)
+
+    other_rows = attend(1 - plane_q)
     partner_o = lax.ppermute(o_weight, ("yh", "ylo"), NEIGHBOUR)
-    half = row_count // 2
-    own_rows = lax.dynamic_slice_in_dim(attended, plane * half, half, 0)
-    other_rows = lax.dynamic_slice_in_dim(attended, (1 - plane) * half, half, 0)
     partner_rows = lax.ppermute(other_rows, "yh", [(0, 1), (1, 0)])
+    own_rows = attend(plane_q)
     mixed = jnp.dot(
         jnp.concatenate([own_rows, partner_rows], axis=1),
         jnp.concatenate([o_weight, partner_o], axis=0),

time: 253 us -> 265 us (1.047)
  the two profiles are of different devices: /device:TPU:8 before, /device:TPU:1 now
where the time goes in v10:
time: 265 us; the launch traced here: 264 us
  waiting for transfers between devices  138 us (52%)
  Pallas kernels  34.3 us (13%)
  starting transfers between devices  31.5 us (12%)
  other arithmetic  20.8 us (8%)
  matrix products  14 us (5%)
  between operations  13.8 us (5%)
  local copies, waits for them, and re-layouts  11.4 us (4%)
    ppermute x1, waiting for transfers between devices, per_device(): partner_half = lax.ppermute(sent_half, ('yh', 'ylo'), NEIGHBOUR)  45.2 us
    all_gather x1, waiting for transfers between devices, per_device(): gathered = lax.all_gather(kv_pair, CONTEXT, axis=1, tiled=True)  44.5 us
    ppermute x3, waiting for transfers between devices, shift_x(): return lax.ppermute(value, 'x', [(i, (i + d) % n) for i in range(n)])  41 us
    pallas_call x2, Pallas kernels, span_attention(): pl.pallas_call(kernel, out_shape=jax.ShapeDtypeStruct((SPAN, q_cols), jnp...  34.3 us
    ppermute x1, starting transfers between devices, per_device(): partner_rows = lax.ppermute(other_rows, 'yh', [(0, 1), (1, 0)])  17.4 us
    unnamed x28, local copies, waits for them, and re-layouts  6.98 us
  transfers between devices with their start and end apart: 10, of which 6 were waited for; matrix products, arithmetic and copies ran while one was open for 7% of the time, Pallas kernels for 13%

profile of v10, /device:TPU:1, one launch (start us, length us, event | category | flops | bytes accessed | tf_op | source)
XLA Modules:
  0.0 264.3 jit_solution(8892964131089777926)
XLA Ops:
  6.5 1.7 fusion.3
  8.2 2.5 fusion.5
  12.8 1.8 copy-done.1
  14.6 3.6 %collective-permute-start = (bf16[2048,512]{1,0:T(8,128)(2,1)S(1)}, bf16[2048,512]{1,0:T(8,128)(2,1)S(1)}, u32[]{:S(2)}, u32[]{:S(2)}) collective-permute-start(bf16[2048,512]{1,0:T(8,128)(2,1)S(1)} %constant_dynamic-slice_fusion.3), channel_id=1, source_target_pairs={{0,66},{66,0},{2,64},{64,2},{1,67},{67,1},{3,65},{65,3},{4,70},{70... | collective-permute-start | bytes 6291464 | tf_op jit(solution)/shard_map/ppermute | solution.py:190
  18.2 45.2 %collective-permute-done = bf16[2048,512]{1,0:T(8,128)(2,1)S(1)} collective-permute-done((bf16[2048,512]{1,0:T(8,128)(2,1)S(1)}, bf16[2048,512]{1,0:T(8,128)(2,1)S(1)}, u32[]{:S(2)}, u32[]{:S(2)}) %collective-permute-start) | collective-permute-done | bytes 2097184 | tf_op jit(solution)/shard_map/ppermute | solution.py:190
  63.4 1.4 collective-permute-start.1
  66.0 2.7 %collective-permute-done.1 = bf16[2048,512]{1,0:T(8,128)(2,1)} collective-permute-done((bf16[2048,512]{1,0:T(8,128)(2,1)S(1)}, bf16[2048,512]{1,0:T(8,128)(2,1)}, u32[]{:S(2)}, u32[]{:S(2)}) %collective-permute-start.1) | collective-permute-done | bytes 2097184 | tf_op jit(solution)/shard_map/ppermute | solution.py:192
  68.7 3.5 %fusion.6 = f32[512,512]{1,0:T(8,128)S(1)} fusion(bf16[2048,512]{1,0:T(8,128)(2,1)} %collective-permute-done.1, bf16[1,512,4096]{2,1,0:T(8,128)(2,1)} %all-gather.3.cloned.1.call-done, s32[]{:T(128)S(6)} %select_n.119), kind=kOutput, calls=%fused_computation.9 | convolution fusion | flops 1073741824 | bytes 5242884 | tf_op jit(solution)/shard_map/dot_general | solution.py:212
  72.2 1.3 fusion.12
  77.6 1.6 collective-permute-start.2
  79.2 4.6 %fusion.61 = f32[512,512]{0,1:T(8,128)S(1)} fusion(bf16[512,4096]{1,0:T(8,128)(2,1)} %bitcast.60, bf16[4096,512]{1,0:T(8,128)(2,1)S(1)} %copy-done.2), kind=kOutput, calls=%fused_computation.138 | convolution fusion | flops 2147483648 | bytes 9437184 | tf_op jit(solution)/shard_map/dot_general | solution.py:208
  86.0 1.2 fusion.38
  87.4 5.1 %collective-permute-done.2 = bf16[512,512]{1,0:T(8,128)(2,1)S(1)} collective-permute-done((bf16[512,512]{1,0:T(8,128)(2,1)}, bf16[512,512]{1,0:T(8,128)(2,1)S(1)}, u32[]{:S(2)}, u32[]{:S(2)}) %collective-permute-start.2) | collective-permute-done | bytes 524320 | tf_op jit(solution)/shard_map/ppermute | solution.py:213
  93.6 2.7 %collective-permute-start.4 = (bf16[256,4096]{1,0:T(8,128)(2,1)}, bf16[256,4096]{1,0:T(8,128)(2,1)}, u32[]{:S(2)}, u32[]{:S(2)}) collective-permute-start(bf16[256,4096]{1,0:T(8,128)(2,1)} %param.15), channel_id=1, source_target_pairs={{0,66},{66,0},{2,64},{64,2},{1,67},{67,1},{3,65},{65,3},{4,70},{70... | collective-permute-start | bytes 6291464 | tf_op jit(solution)/shard_map/ppermute | solution.py:241
  104.5 44.5 %all-gather.5.cloned.1.call-done.k_ref.v_ref = bf16[2,16384,128]{2,1,0:T(8,128)(2,1)} async-done(((bf16[2,1024,128]{2,1,0:T(8,128)(2,1)}), bf16[2,16384,128]{2,1,0:T(8,128)(2,1)}) %all-gather.5.cloned.1.call-update) | async-done | bytes 8388624 | tf_op jit(solution)/shard_map/all_gather | solution.py:221
  149.1 9.9 %shard_map.83 = bf16[512,256]{1,0:T(8,128)(2,1)} custom-call(s32[1]{0:T(128)} %bitcast.14.which_ref, s32[1,9]{1,0:T(1,128)} %copy.62.tbl_ref, s32[1,9]{1,0:T(1,128)} %get-tuple-element.51.seq_ref, s32[1]{0:T(128)} %get-tuple-element.53.cnt_ref, s32[1,9]{1,0:T(1,128)} %get-tuple-element.49.full_ref, bf16[1024,256]{1,0:T(8,128)(2,1)} %fusion.18.q_ref, ...), custom_call_target="tpu_custom_call" | custom-call | flops 2415919104 | bytes 2883584 | tf_op jit(solution)/shard_map/pallas_call | solution.py:101
  158.9 17.4 %collective-permute-start.3 = (bf16[512,256]{1,0:T(8,128)(2,1)}, bf16[512,256]{1,0:T(8,128)(2,1)S(1)}, u32[]{:S(2)}, u32[]{:S(2)}) collective-permute-start(bf16[512,256]{1,0:T(8,128)(2,1)} %shard_map.83), channel_id=1, source_target_pairs={{0,64},{64,0},{1,65},{65,1},{2,66},{66,2},{3,67},{67,3},{4,68},{68... | collective-permute-start | bytes 786440 | tf_op jit(solution)/shard_map/ppermute | solution.py:242
  176.9 24.4 %shard_map.82 = bf16[512,256]{1,0:T(8,128)(2,1)} custom-call(s32[1]{0:T(128)} %bitcast.which_ref, s32[1,9]{1,0:T(1,128)} %copy.59.tbl_ref, s32[1,9]{1,0:T(1,128)} %get-tuple-element.50.seq_ref, s32[1]{0:T(128)} %get-tuple-element.52.cnt_ref, s32[1,9]{1,0:T(1,128)} %get-tuple-element.48.full_ref, bf16[1024,256]{1,0:T(8,128)(2,1)} %fusion.18.q_ref, ...), custom_call_target="tpu_custom_call" | custom-call | flops 2415919104 | bytes 2883584 | tf_op jit(solution)/shard_map/pallas_call | solution.py:101
  201.3 4.7 %convolution_convert_fusion = bf16[512,4096]{1,0:T(8,128)(2,1)S(1)} fusion(bf16[256,4096]{1,0:T(8,128)(2,1)} %collective-permute-done.4, bf16[256,4096]{1,0:T(8,128)(2,1)} %param.15, bf16[512,256]{1,0:T(8,128)(2,1)S(1)} %collective-permute-done.3, bf16[512,256]{1,0:T(8,128)(2,1)} %shard_map.82), kind=kOutput, calls=%fused_computation | convolution fusion | flops 2159017984 | bytes 8912896 | tf_op jit(solution)/shard_map/dot_general | solution.py:244
  206.3 1.6 copy-done
  209.1 2.4 collective-permute-start.6
  212.7 20.8 %collective-permute-done.5 = bf16[128,4096]{1,0:T(8,128)(2,1)} collective-permute-done((bf16[128,4096]{1,0:T(8,128)(2,1)S(1)}, bf16[128,4096]{1,0:T(8,128)(2,1)}, u32[]{:S(2)}, u32[]{:S(2)}) %collective-permute-start.5) | collective-permute-done | bytes 1048608 | tf_op jit(solution)/shard_map/ppermute | solution.py:154
  233.5 20.1 %collective-permute-done.6 = bf16[128,4096]{1,0:T(8,128)(2,1)} collective-permute-done((bf16[128,4096]{1,0:T(8,128)(2,1)S(1)}, bf16[128,4096]{1,0:T(8,128)(2,1)}, u32[]{:S(2)}, u32[]{:S(2)}) %collective-permute-start.6) | collective-permute-done | bytes 1048608 | tf_op jit(solution)/shard_map/ppermute | solution.py:154
  253.7 3.8 %fusion.15 = bf16[1,128,4096]{2,1,0:T(8,128)(2,1)} fusion(bf16[128,4096]{1,0:T(8,128)(2,1)} %collective-permute-done.7, bf16[128,4096]{1,0:T(8,128)(2,1)} %collective-permute-done.6, bf16[128,4096]{1,0:T(8,128)(2,1)} %collective-permute-done.5, bf16[4,128,4096]{2,1,0:T(8,128)(2,1)} %bitcast.50, s32[]{:T(128)S(6)} %select_n.142, pred[]{:T(512)S(6)} %and.78), kind=kLoop, calls=%fused_computation.21 | loop fusion | flops 4718592 | bytes 5242885 | tf_op jit(solution)/shard_map/reshape | solution.py:250
  (95 shorter events, 22.0 us)
Async XLA Ops:
  6.5 4.3 %copy-start.3 = (bf16[4096,256]{1,0:T(8,128)(2,1)S(1)}, bf16[4096,256]{1,0:T(8,128)(2,1)}, u32[]{:S(2)}) copy-start(bf16[4096,256]{1,0:T(8,128)(2,1)} %param.12) | copy-start | bytes 6291460
  6.5 56.8 %all-gather.3.cloned.1.call-start = ((), (), s32[]{:S(2)}) async-start(), calls=%async_computation | async-start | bytes 5242880 | tf_op jit(solution)/shard_map/all_gather | solution.py:189
  10.8 138.3 %all-gather.5.cloned.1.call-start = ((), (), s32[]{:S(2)}) async-start(), calls=%async_computation.1 | async-start | bytes 8912896 | tf_op jit(solution)/shard_map/all_gather | solution.py:221
  10.8 1.2 copy-start.4
  10.8 1.5 copy-start.5
  12.6 2.0 copy-start.1
  12.6 52.1 %copy-start.7 = (s32[32]{0:T(128)S(1)}, s32[32]{0:T(128)}, u32[]{:S(2)}) copy-start(s32[32]{0:T(128)} %param.17) | copy-start | bytes 388
  14.6 48.8 %collective-permute-start = (bf16[2048,512]{1,0:T(8,128)(2,1)S(1)}, bf16[2048,512]{1,0:T(8,128)(2,1)S(1)}, u32[]{:S(2)}, u32[]{:S(2)}) collective-permute-start(bf16[2048,512]{1,0:T(8,128)(2,1)S(1)} %constant_dynamic-slice_fusion.3), channel_id=1, source_target_pairs={{0,66},{66,0},{2,64},{64,2},{1,67},{67,1},{3,65},{65,3},{4,70},{70... | collective-permute-start | bytes 6291464 | tf_op jit(solution)/shard_map/ppermute | solution.py:190
  63.4 5.3 %collective-permute-start.1 = (bf16[2048,512]{1,0:T(8,128)(2,1)S(1)}, bf16[2048,512]{1,0:T(8,128)(2,1)}, u32[]{:S(2)}, u32[]{:S(2)}) collective-permute-start(bf16[2048,512]{1,0:T(8,128)(2,1)S(1)} %collective-permute-done), channel_id=1, source_target_pairs={{0,1},{1,0},{2,3},{3,2},{4,5},{5,4},{6,7},{7,6},{8,9},{9,8},{10,11... | collective-permute-start | bytes 6291464 | tf_op jit(solution)/shard_map/ppermute | solution.py:192
  66.0 6.2 %copy-start.8 = (bf16[1,512,4096]{2,1,0:T(8,128)(2,1)S(1)}, bf16[1,512,4096]{2,1,0:T(8,128)(2,1)}, u32[]{:S(2)}) copy-start(bf16[1,512,4096]{2,1,0:T(8,128)(2,1)} %all-gather.3.cloned.1.call-done) | copy-start | bytes 12582916
  73.8 5.4 %copy-start.2 = (bf16[4096,512]{1,0:T(8,128)(2,1)S(1)}, bf16[4096,512]{1,0:T(8,128)(2,1)}, u32[]{:S(2)}) copy-start(bf16[4096,512]{1,0:T(8,128)(2,1)} %copy-done.1) | copy-start | bytes 12582916
  77.6 14.9 %collective-permute-start.2 = (bf16[512,512]{1,0:T(8,128)(2,1)}, bf16[512,512]{1,0:T(8,128)(2,1)S(1)}, u32[]{:S(2)}, u32[]{:S(2)}) collective-permute-start(bf16[512,512]{1,0:T(8,128)(2,1)} %pad_maximum_fusion), channel_id=1, source_target_pairs={{0,64},{64,0},{1,65},{65,1},{2,66},{66,2},{3,67},{67,3},{4,68},{68... | collective-permute-start | bytes 1572872 | tf_op jit(solution)/shard_map/ppermute | solution.py:213
  92.7 4.0 %copy-start.6 = (s32[16]{0:T(128)S(1)}, s32[16]{0:T(128)}, u32[]{:S(2)}) copy-start(s32[16]{0:T(128)} %param.16) | copy-start | bytes 196
  93.6 107.7 %collective-permute-start.4 = (bf16[256,4096]{1,0:T(8,128)(2,1)}, bf16[256,4096]{1,0:T(8,128)(2,1)}, u32[]{:S(2)}, u32[]{:S(2)}) collective-permute-start(bf16[256,4096]{1,0:T(8,128)(2,1)} %param.15), channel_id=1, source_target_pairs={{0,66},{66,0},{2,64},{64,2},{1,67},{67,1},{3,65},{65,3},{4,70},{70... | collective-permute-start | bytes 6291464 | tf_op jit(solution)/shard_map/ppermute | solution.py:241
  158.9 42.4 %collective-permute-start.3 = (bf16[512,256]{1,0:T(8,128)(2,1)}, bf16[512,256]{1,0:T(8,128)(2,1)S(1)}, u32[]{:S(2)}, u32[]{:S(2)}) collective-permute-start(bf16[512,256]{1,0:T(8,128)(2,1)} %shard_map.83), channel_id=1, source_target_pairs={{0,64},{64,0},{1,65},{65,1},{2,66},{66,2},{3,67},{67,3},{4,68},{68... | collective-permute-start | bytes 786440 | tf_op jit(solution)/shard_map/ppermute | solution.py:242
  206.0 1.9 copy-start
  207.9 25.6 %collective-permute-start.5 = (bf16[128,4096]{1,0:T(8,128)(2,1)S(1)}, bf16[128,4096]{1,0:T(8,128)(2,1)}, u32[]{:S(2)}, u32[]{:S(2)}) collective-permute-start(bf16[128,4096]{1,0:T(8,128)(2,1)S(1)} %get-tuple-element.25), channel_id=1, source_target_pairs={{0,16},{16,32},{32,48},{48,0},{1,17},{17,33},{33,49},{49,1},{2,18}... | collective-permute-start | bytes 3145736 | tf_op jit(solution)/shard_map/ppermute | solution.py:154
  209.1 44.5 %collective-permute-start.6 = (bf16[128,4096]{1,0:T(8,128)(2,1)S(1)}, bf16[128,4096]{1,0:T(8,128)(2,1)}, u32[]{:S(2)}, u32[]{:S(2)}) collective-permute-start(bf16[128,4096]{1,0:T(8,128)(2,1)S(1)} %get-tuple-element.27), channel_id=1, source_target_pairs={{0,32},{16,48},{32,0},{48,16},{1,33},{17,49},{33,1},{49,17},{2,34}... | collective-permute-start | bytes 3145736 | tf_op jit(solution)/shard_map/ppermute | solution.py:154
  211.5 42.1 %collective-permute-start.7 = (bf16[128,4096]{1,0:T(8,128)(2,1)S(1)}, bf16[128,4096]{1,0:T(8,128)(2,1)}, u32[]{:S(2)}, u32[]{:S(2)}) collective-permute-start(bf16[128,4096]{1,0:T(8,128)(2,1)S(1)} %get-tuple-element.26), channel_id=1, source_target_pairs={{0,48},{16,0},{32,16},{48,32},{1,49},{17,1},{33,17},{49,33},{2,50}... | collective-permute-start | bytes 3145736 | tf_op jit(solution)/shard_map/ppermute | solution.py:154
Sparse Core Ops, SparseCore 0:
  10.9 51.4 all-gather.2
  93.7 55.2 all-gather.4

commit v11 on v9

--- a/solution.py
+++ b/solution.py
@@ -183,13 +183,13 @@
     ).astype(jnp.bfloat16)
     plane = lax.axis_index("yh")
     core = lax.axis_index("core")
-    weights = jnp.concatenate([q_weight, k_weight, v_weight], axis=1)
-    half_in = weights.shape[0] // 2
-    sent_half = lax.dynamic_slice_in_dim(weights, core * half_in, half_in, 0)
+    own_parts = (q_weight, k_weight, v_weight)
+    half_in = q_weight.shape[0] // 2
+    sent_parts = [lax.dynamic_slice_in_dim(w, core * half_in, half_in, 0) for w in own_parts]
     plane_rows = lax.all_gather(normed, "x", axis=1, tiled=True)
-    partner_half = lax.ppermute(sent_half, ("yh", "ylo"), NEIGHBOUR)
-    plane_rows, partner_half = lax.optimization_barrier((plane_rows, partner_half))
-    other_half = lax.ppermute(partner_half, "core", [(0, 1), (1, 0)])
+    partner_parts = [lax.ppermute(w, ("yh", "ylo"), NEIGHBOUR) for w in sent_parts]
+    plane_rows, partner_parts = lax.optimization_barrier((plane_rows, partner_parts))
+    other_parts = [lax.ppermute(w, "core", [(0, 1), (1, 0)]) for w in partner_parts]
     half = plane_rows.shape[1]
     flat_rows = plane_rows.reshape(half, model_width)
     all_places = positions(base_row + jnp.arange(tok_dev, dtype=jnp.int32), span_order, span_rows)
@@ -197,22 +197,19 @@
     rows_mine = lax.dynamic_slice_in_dim(flat_rows, core * half_in, half_in, 1)
     rows_other = lax.dynamic_slice_in_dim(flat_rows, (1 - core) * half_in, half_in, 1)
 
-    def finish(out):
-        q = rotary(out[:, :q_cols].reshape(half, q_heads, head_dim), places)
-        k = rotary(out[:, q_cols:q_cols + kv_cols].reshape(half, kv_local, head_dim), places)
+    def finish(q, k, v):
+        q = rotary(q.reshape(half, q_heads, head_dim), places)
+        k = rotary(k.reshape(half, kv_local, head_dim), places)
         return jnp.concatenate(
-            [q.reshape(half, q_cols), k.reshape(half, kv_cols), out[:, q_cols + kv_cols:]], axis=1
-        ).astype(jnp.bfloat16)
-
-    def project(w):
-        return finish(jnp.dot(flat_rows, w, preferred_element_type=jnp.float32))
-
-    for_partner = finish(
-        jnp.dot(rows_mine, partner_half, preferred_element_type=jnp.float32)
-        + jnp.dot(rows_other, other_half, preferred_element_type=jnp.float32))
+            [q.reshape(half, q_cols), k.reshape(half, kv_cols), v], axis=1).astype(jnp.bfloat16)
+
+    for_partner = finish(*[
+        jnp.dot(rows_mine, a, preferred_element_type=jnp.float32)
+        + jnp.dot(rows_other, b, preferred_element_type=jnp.float32)
+        for a, b in zip(partner_parts, other_parts)])
     received = lax.ppermute(for_partner, "yh", [(0, 1), (1, 0)])
     flat_rows, for_partner = lax.optimization_barrier((flat_rows, for_partner))
-    own = project(weights)
+    own = finish(*[jnp.dot(flat_rows, w, preferred_element_type=jnp.float32) for w in own_parts])
     first = jnp.where(plane == 0, own, received)
     second = jnp.where(plane == 0, received, own)
     projected = jnp.concatenate([first, second], axis=0)

time: 253 us -> 265 us (1.047)
  the two profiles are of different devices: /device:TPU:8 before, /device:TPU:65 now
where the time goes in v11:
time: 265 us; the launch traced here: 264 us
  waiting for transfers between devices  137 us (52%)
  Pallas kernels  29 us (11%)
  other arithmetic  28 us (11%)
  matrix products  21.1 us (8%)
  starting transfers between devices  19.4 us (7%)
  local copies, waits for them, and re-layouts  16.6 us (6%)
  between operations  13.7 us (5%)
    ppermute x3, waiting for transfers between devices, shift_x(): return lax.ppermute(value, 'x', [(i, (i + d) % n) for i in range(n)])  44.7 us
    all_gather x1, waiting for transfers between devices, per_device(): gathered = lax.all_gather(kv_pair, CONTEXT, axis=1, tiled=True)  42.6 us
    ppermute x3, waiting for transfers between devices, per_device(): lax.ppermute(w, ('yh', 'ylo'), NEIGHBOUR)  40.9 us
    pallas_call x1, Pallas kernels, span_attention(): pl.pallas_call(kernel, out_shape=jax.ShapeDtypeStruct((rows, q_cols), jnp...  29 us
    unnamed x36, local copies, waits for them, and re-layouts  7.95 us
    dot_general x3, matrix products, per_device(): jnp.dot(rows_mine, a, preferred_element_type=jnp.float32)  6.99 us
    another operation x6, other arithmetic  6.16 us
    dot_general x3, matrix products, per_device(): jnp.dot(flat_rows, w, preferred_element_type=jnp.float32)  5.77 us
  transfers between devices with their start and end apart: 14, of which 8 were waited for; matrix products, arithmetic and copies ran while one was open for 13% of the time, Pallas kernels for 11%

profile of v11, /device:TPU:65, one launch (start us, length us, event | category | flops | bytes accessed | tf_op | source)
XLA Modules:
  0.0 264.3 jit_solution(530676298335412303)
XLA Ops:
  8.2 2.5 fusion.5
  11.9 2.7 %collective-permute-start = (bf16[2048,256]{1,0:T(8,128)(2,1)}, bf16[2048,256]{1,0:T(8,128)(2,1)}, u32[]{:S(2)}, u32[]{:S(2)}) collective-permute-start(bf16[2048,256]{1,0:T(8,128)(2,1)} %constant_dynamic-slice_fusion.4), channel_id=1, source_target_pairs={{0,66},{66,0},{2,64},{64,2},{1,67},{67,1},{3,65},{65,3},{4,70},{70... | collective-permute-start | bytes 3145736 | tf_op jit(solution)/shard_map/ppermute | solution.py:190
  16.7 2.4 collective-permute-start.2
  19.2 29.7 %collective-permute-done.1 = bf16[2048,128]{1,0:T(8,128)(2,1)} collective-permute-done((bf16[2048,128]{1,0:T(8,128)(2,1)}, bf16[2048,128]{1,0:T(8,128)(2,1)}, u32[]{:S(2)}, u32[]{:S(2)}) %collective-permute-start.1) | collective-permute-done | bytes 524320 | tf_op jit(solution)/shard_map/ppermute | solution.py:190
  48.9 11.2 %collective-permute-done.2 = bf16[2048,128]{1,0:T(8,128)(2,1)} collective-permute-done((bf16[2048,128]{1,0:T(8,128)(2,1)}, bf16[2048,128]{1,0:T(8,128)(2,1)}, u32[]{:S(2)}, u32[]{:S(2)}) %collective-permute-start.2) | collective-permute-done | bytes 524320 | tf_op jit(solution)/shard_map/ppermute | solution.py:190
  63.9 2.3 fusion.8
  66.3 2.5 fusion.30
  70.9 2.5 fusion.36
  74.1 2.0 fusion.24
  85.7 2.0 convolution_bitcast_fusion
  87.7 2.6 collective-permute-start.6
  98.1 2.5 convolution_convert_fusion.1
  100.6 2.5 collective-permute-done.6
  105.3 2.8 %collective-permute-start.8 = (bf16[256,4096]{1,0:T(8,128)(2,1)}, bf16[256,4096]{1,0:T(8,128)(2,1)}, u32[]{:S(2)}, u32[]{:S(2)}) collective-permute-start(bf16[256,4096]{1,0:T(8,128)(2,1)} %param.15), channel_id=1, source_target_pairs={{0,66},{66,0},{2,64},{64,2},{1,67},{67,1},{3,65},{65,3},{4,70},{70... | collective-permute-start | bytes 6291464 | tf_op jit(solution)/shard_map/ppermute | solution.py:232
  113.8 2.1 fusion.41.qpos_ref
  116.8 42.6 %all-gather.5.cloned.1.call-done.k_ref.v_ref = bf16[2,16384,128]{2,1,0:T(8,128)(2,1)} async-done(((bf16[2,1024,128]{2,1,0:T(8,128)(2,1)}), bf16[2,16384,128]{2,1,0:T(8,128)(2,1)}) %all-gather.5.cloned.1.call-update) | async-done | bytes 8388624 | tf_op jit(solution)/shard_map/all_gather | solution.py:218
  159.4 29.0 %shard_map.82 = bf16[1024,256]{1,0:T(8,128)(2,1)} custom-call(s32[2,9]{1,0:T(2,128)} %copy.66.tbl_ref, s32[2,9]{1,0:T(2,128)} %copy-done.10, s32[2]{0:T(128)} %copy-done.11, s32[2,9]{1,0:T(2,128)} %and_convert_fusion.full_ref, bf16[1024,256]{1,0:T(8,128)(2,1)} %fusion.42.q_ref, s32[1024,1]{1,0:T(8,128)} %fusion.41.qpos_ref, s32[1024,1]{1,0:T(8,128)} %copy.67.qstart_ref, ...), custom_call_target="tpu_custom_call" | custom-call | flops 4831838208 | bytes 5767168 | tf_op jit(solution)/shard_map/pallas_call | solution.py:101
  189.5 3.1 %collective-permute-start.7 = (bf16[512,256]{1,0:T(8,128)(2,1)S(1)}, bf16[512,256]{1,0:T(8,128)(2,1)S(1)}, u32[]{:S(2)}, u32[]{:S(2)}) collective-permute-start(bf16[512,256]{1,0:T(8,128)(2,1)S(1)} %get-tuple-element.41), channel_id=1, source_target_pairs={{0,64},{64,0},{1,65},{65,1},{2,66},{66,2},{3,67},{67,3},{4,68},{68... | collective-permute-start | bytes 786440 | tf_op jit(solution)/shard_map/ppermute | solution.py:236
  192.5 5.1 %collective-permute-done.7 = bf16[512,256]{1,0:T(8,128)(2,1)S(1)} collective-permute-done((bf16[512,256]{1,0:T(8,128)(2,1)S(1)}, bf16[512,256]{1,0:T(8,128)(2,1)S(1)}, u32[]{:S(2)}, u32[]{:S(2)}) %collective-permute-start.7) | collective-permute-done | bytes 262176 | tf_op jit(solution)/shard_map/ppermute | solution.py:236
  197.6 4.6 %convolution_convert_fusion = bf16[512,4096]{1,0:T(8,128)(2,1)S(1)} fusion(bf16[256,4096]{1,0:T(8,128)(2,1)} %collective-permute-done.8, bf16[256,4096]{1,0:T(8,128)(2,1)} %param.15, bf16[512,256]{1,0:T(8,128)(2,1)S(1)} %collective-permute-done.7, bf16[512,256]{1,0:T(8,128)(2,1)S(1)} %get-tuple-element.40), kind=kOutput, calls=%fused_computation | convolution fusion | flops 2159017984 | bytes 8912896 | tf_op jit(solution)/shard_map/dot_general | solution.py:237
  204.8 2.7 %collective-permute-start.10 = (bf16[128,4096]{1,0:T(8,128)(2,1)}, bf16[128,4096]{1,0:T(8,128)(2,1)}, u32[]{:S(2)}, u32[]{:S(2)}) collective-permute-start(bf16[128,4096]{1,0:T(8,128)(2,1)} %get-tuple-element.31), channel_id=1, source_target_pairs={{0,32},{16,48},{32,0},{48,16},{1,33},{17,49},{33,1},{49,17},{2,34}... | collective-permute-start | bytes 3145736 | tf_op jit(solution)/shard_map/ppermute | solution.py:154
  209.0 22.5 %collective-permute-done.10 = bf16[128,4096]{1,0:T(8,128)(2,1)} collective-permute-done((bf16[128,4096]{1,0:T(8,128)(2,1)}, bf16[128,4096]{1,0:T(8,128)(2,1)}, u32[]{:S(2)}, u32[]{:S(2)}) %collective-permute-start.10) | collective-permute-done | bytes 1048608 | tf_op jit(solution)/shard_map/ppermute | solution.py:154
  231.5 22.1 %collective-permute-done.11 = bf16[128,4096]{1,0:T(8,128)(2,1)} collective-permute-done((bf16[128,4096]{1,0:T(8,128)(2,1)}, bf16[128,4096]{1,0:T(8,128)(2,1)}, u32[]{:S(2)}, u32[]{:S(2)}) %collective-permute-start.11) | collective-permute-done | bytes 1048608 | tf_op jit(solution)/shard_map/ppermute | solution.py:154
  253.7 3.8 %fusion.39 = bf16[1,128,4096]{2,1,0:T(8,128)(2,1)} fusion(bf16[128,4096]{1,0:T(8,128)(2,1)} %collective-permute-done.11, bf16[128,4096]{1,0:T(8,128)(2,1)} %collective-permute-done.10, bf16[128,4096]{1,0:T(8,128)(2,1)} %collective-permute-done.9, bf16[4,128,4096]{2,1,0:T(8,128)(2,1)} %bitcast.77, s32[]{:T(128)S(6)} %select_n.135, pred[]{:T(512)S(6)} %and.78), kind=kLoop, calls=%fused_computation.39 | loop fusion | flops 4718592 | bytes 5242885 | tf_op jit(solution)/shard_map/reshape | solution.py:243
  (109 shorter events, 42.7 us)
Async XLA Ops:
  6.5 4.3 %copy-start = (bf16[4096,256]{1,0:T(8,128)(2,1)S(1)}, bf16[4096,256]{1,0:T(8,128)(2,1)}, u32[]{:S(2)}) copy-start(bf16[4096,256]{1,0:T(8,128)(2,1)} %param.12) | copy-start | bytes 6291460
  6.5 54.3 %all-gather.3.cloned.1.call-start = ((), (), s32[]{:S(2)}) async-start(), calls=%async_computation | async-start | bytes 5242880 | tf_op jit(solution)/shard_map/all_gather | solution.py:189
  10.7 3.9 %copy-start.5 = (bf16[4096,128]{1,0:T(8,128)(2,1)S(1)}, bf16[4096,128]{1,0:T(8,128)(2,1)}, u32[]{:S(2)}) copy-start(bf16[4096,128]{1,0:T(8,128)(2,1)} %param.13) | copy-start | bytes 3145732
  10.8 148.6 %all-gather.5.cloned.1.call-start = ((), (), s32[]{:S(2)}) async-start(), calls=%async_computation.1 | async-start | bytes 8912896 | tf_op jit(solution)/shard_map/all_gather | solution.py:218
  10.8 4.9 %copy-start.9 = (bf16[4096,128]{1,0:T(8,128)(2,1)S(1)}, bf16[4096,128]{1,0:T(8,128)(2,1)}, u32[]{:S(2)}) copy-start(bf16[4096,128]{1,0:T(8,128)(2,1)} %param.14) | copy-start | bytes 3145732
  10.8 8.2 %copy-start.13 = (s32[32]{0:T(128)S(1)}, s32[32]{0:T(128)}, u32[]{:S(2)}) copy-start(s32[32]{0:T(128)} %param.17) | copy-start | bytes 388
  11.9 48.2 %collective-permute-start = (bf16[2048,256]{1,0:T(8,128)(2,1)}, bf16[2048,256]{1,0:T(8,128)(2,1)}, u32[]{:S(2)}, u32[]{:S(2)}) collective-permute-start(bf16[2048,256]{1,0:T(8,128)(2,1)} %constant_dynamic-slice_fusion.4), channel_id=1, source_target_pairs={{0,66},{66,0},{2,64},{64,2},{1,67},{67,1},{3,65},{65,3},{4,70},{70... | collective-permute-start | bytes 3145736 | tf_op jit(solution)/shard_map/ppermute | solution.py:190
  15.5 33.4 %collective-permute-start.1 = (bf16[2048,128]{1,0:T(8,128)(2,1)}, bf16[2048,128]{1,0:T(8,128)(2,1)}, u32[]{:S(2)}, u32[]{:S(2)}) collective-permute-start(bf16[2048,128]{1,0:T(8,128)(2,1)} %constant_dynamic-slice_fusion.3), channel_id=1, source_target_pairs={{0,66},{66,0},{2,64},{64,2},{1,67},{67,1},{3,65},{65,3},{4,70},{70... | collective-permute-start | bytes 1572872 | tf_op jit(solution)/shard_map/ppermute | solution.py:190
  16.7 43.4 %collective-permute-start.2 = (bf16[2048,128]{1,0:T(8,128)(2,1)}, bf16[2048,128]{1,0:T(8,128)(2,1)}, u32[]{:S(2)}, u32[]{:S(2)}) collective-permute-start(bf16[2048,128]{1,0:T(8,128)(2,1)} %constant_dynamic-slice_fusion.2), channel_id=1, source_target_pairs={{0,66},{66,0},{2,64},{64,2},{1,67},{67,1},{3,65},{65,3},{4,70},{70... | collective-permute-start | bytes 1572872 | tf_op jit(solution)/shard_map/ppermute | solution.py:190
  60.8 3.1 %collective-permute-start.4 = (bf16[2048,128]{1,0:T(8,128)(2,1)}, bf16[2048,128]{1,0:T(8,128)(2,1)S(1)}, u32[]{:S(2)}, u32[]{:S(2)}) collective-permute-start(bf16[2048,128]{1,0:T(8,128)(2,1)} %collective-permute-done.1), channel_id=1, source_target_pairs={{0,1},{1,0},{2,3},{3,2},{4,5},{5,4},{6,7},{7,6},{8,9},{9,8},{10,11... | collective-permute-start | bytes 1572872 | tf_op jit(solution)/shard_map/ppermute | solution.py:192
  63.4 9.9 %collective-permute-start.3 = (bf16[2048,256]{1,0:T(8,128)(2,1)}, bf16[2048,256]{1,0:T(8,128)(2,1)S(1)}, u32[]{:S(2)}, u32[]{:S(2)}) collective-permute-start(bf16[2048,256]{1,0:T(8,128)(2,1)} %collective-permute-done), channel_id=1, source_target_pairs={{0,1},{1,0},{2,3},{3,2},{4,5},{5,4},{6,7},{7,6},{8,9},{9,8},{10,11... | collective-permute-start | bytes 3145736 | tf_op jit(solution)/shard_map/ppermute | solution.py:192
  63.4 6.7 %collective-permute-start.5 = (bf16[2048,128]{1,0:T(8,128)(2,1)}, bf16[2048,128]{1,0:T(8,128)(2,1)S(1)}, u32[]{:S(2)}, u32[]{:S(2)}) collective-permute-start(bf16[2048,128]{1,0:T(8,128)(2,1)} %collective-permute-done.2), channel_id=1, source_target_pairs={{0,1},{1,0},{2,3},{3,2},{4,5},{5,4},{6,7},{7,6},{8,9},{9,8},{10,11... | collective-permute-start | bytes 1572872 | tf_op jit(solution)/shard_map/ppermute | solution.py:192
  66.2 3.9 %copy-start.1 = (bf16[1,512,4096]{2,1,0:T(8,128)(2,1)S(1)}, bf16[1,512,4096]{2,1,0:T(8,128)(2,1)}, u32[]{:S(2)}) copy-start(bf16[1,512,4096]{2,1,0:T(8,128)(2,1)} %all-gather.3.cloned.1.call-done) | copy-start | bytes 12582916
  87.7 6.7 %copy-start.7 = (f32[512,1,128]{2,0,1:T(8,128)S(1)}, f32[512,1,128]{2,0,1:T(8,128)}, u32[]{:S(2)}) copy-start(f32[512,1,128]{2,0,1:T(8,128)} %convolution_bitcast_fusion) | copy-start | bytes 786436
  87.7 7.9 %copy-start.6 = (f32[512,64]{1,0:T(8,128)S(1)}, f32[512,64]{1,0:T(8,128)}, u32[]{:S(2)}) copy-start(f32[512,64]{1,0:T(8,128)} %get-tuple-element.53) | copy-start | bytes 393220
  87.7 15.4 %collective-permute-start.6 = (bf16[512,512]{1,0:T(8,128)(2,1)}, bf16[512,512]{1,0:T(8,128)(2,1)}, u32[]{:S(2)}, u32[]{:S(2)}) collective-permute-start(bf16[512,512]{1,0:T(8,128)(2,1)} %pad_maximum_fusion), channel_id=1, source_target_pairs={{0,64},{64,0},{1,65},{65,1},{2,66},{66,2},{3,67},{67,3},{4,68},{68... | collective-permute-start | bytes 1572872 | tf_op jit(solution)/shard_map/ppermute | solution.py:210
  104.4 4.0 %copy-start.12 = (s32[16]{0:T(128)S(1)}, s32[16]{0:T(128)}, u32[]{:S(2)}) copy-start(s32[16]{0:T(128)} %param.16) | copy-start | bytes 196
  105.3 87.2 %collective-permute-start.8 = (bf16[256,4096]{1,0:T(8,128)(2,1)}, bf16[256,4096]{1,0:T(8,128)(2,1)}, u32[]{:S(2)}, u32[]{:S(2)}) collective-permute-start(bf16[256,4096]{1,0:T(8,128)(2,1)} %param.15), channel_id=1, source_target_pairs={{0,66},{66,0},{2,64},{64,2},{1,67},{67,1},{3,65},{65,3},{4,70},{70... | collective-permute-start | bytes 6291464 | tf_op jit(solution)/shard_map/ppermute | solution.py:232
  109.6 49.8 %copy-start.11 = (s32[2]{0:T(128)}, s32[2]{0:T(128)S(1)}, u32[]{:S(2)}) copy-start(s32[2]{0:T(128)S(1)} %fusion.84.cnt_ref) | copy-start | bytes 28
  109.7 49.7 %copy-start.10 = (s32[2,9]{1,0:T(2,128)}, s32[2,9]{1,0:T(2,128)S(1)}, u32[]{:S(2)}) copy-start(s32[2,9]{1,0:T(2,128)S(1)} %add_minimum_fusion.seq_ref) | copy-start | bytes 220
  189.5 8.2 %collective-permute-start.7 = (bf16[512,256]{1,0:T(8,128)(2,1)S(1)}, bf16[512,256]{1,0:T(8,128)(2,1)S(1)}, u32[]{:S(2)}, u32[]{:S(2)}) collective-permute-start(bf16[512,256]{1,0:T(8,128)(2,1)S(1)} %get-tuple-element.41), channel_id=1, source_target_pairs={{0,64},{64,0},{1,65},{65,1},{2,66},{66,2},{3,67},{67,3},{4,68},{68... | collective-permute-start | bytes 786440 | tf_op jit(solution)/shard_map/ppermute | solution.py:236
  204.8 26.7 %collective-permute-start.10 = (bf16[128,4096]{1,0:T(8,128)(2,1)}, bf16[128,4096]{1,0:T(8,128)(2,1)}, u32[]{:S(2)}, u32[]{:S(2)}) collective-permute-start(bf16[128,4096]{1,0:T(8,128)(2,1)} %get-tuple-element.31), channel_id=1, source_target_pairs={{0,32},{16,48},{32,0},{48,16},{1,33},{17,49},{33,1},{49,17},{2,34}... | collective-permute-start | bytes 3145736 | tf_op jit(solution)/shard_map/ppermute | solution.py:154
  207.5 46.1 %collective-permute-start.11 = (bf16[128,4096]{1,0:T(8,128)(2,1)}, bf16[128,4096]{1,0:T(8,128)(2,1)}, u32[]{:S(2)}, u32[]{:S(2)}) collective-permute-start(bf16[128,4096]{1,0:T(8,128)(2,1)} %get-tuple-element.30), channel_id=1, source_target_pairs={{0,48},{16,0},{32,16},{48,32},{1,49},{17,1},{33,17},{49,33},{2,50}... | collective-permute-start | bytes 3145736 | tf_op jit(solution)/shard_map/ppermute | solution.py:154
  208.4 45.2 %collective-permute-start.9 = (bf16[128,4096]{1,0:T(8,128)(2,1)S(1)}, bf16[128,4096]{1,0:T(8,128)(2,1)}, u32[]{:S(2)}, u32[]{:S(2)}) collective-permute-start(bf16[128,4096]{1,0:T(8,128)(2,1)S(1)} %get-tuple-element.29), channel_id=1, source_target_pairs={{0,16},{16,32},{32,48},{48,0},{1,17},{17,33},{33,49},{49,1},{2,18}... | collective-permute-start | bytes 3145736 | tf_op jit(solution)/shard_map/ppermute | solution.py:154
  (5 other events, 16.4 us)
Sparse Core Ops, SparseCore 0:
  10.9 49.8 all-gather.2
  105.5 53.8 all-gather.4

commit v12 on v8

--- a/solution.py
+++ b/solution.py
@@ -39,37 +39,53 @@
     )
 
 
+def online_update(heads, scale, q_ref, k_ref, v_ref, visible, m_sc, l_sc, acc_sc):
+    k = k_ref[...]
+    v = v_ref[...]
+    for h in range(heads):
+        q = q_ref[:, h * HEAD_DIM:(h + 1) * HEAD_DIM]
+        s = lax.dot_general(q, k, (((1,), (1,)), ((), ())),
+                            preferred_element_type=jnp.float32) * scale
+        m_old = m_sc[h]
+        m_new = jnp.maximum(
+            m_old, jnp.max(jnp.where(visible, s, masked_score), axis=-1, keepdims=True))
+        p = jnp.where(visible, jnp.exp(s - m_new), 0.0)
+        alpha = jnp.exp(m_old - m_new)
+        l_sc[h] = alpha * l_sc[h] + jnp.sum(p, axis=-1, keepdims=True)
+        acc_sc[h] = alpha * acc_sc[h] + jnp.dot(
+            p.astype(jnp.bfloat16), v, preferred_element_type=jnp.float32)
+        m_sc[h] = m_new
+
+
+def diagonal_kernel(heads, scale, sq_ref, q_ref, qpos_ref, qstart_ref, k_ref, v_ref,
+                    m_ref, l_ref, acc_ref):
+    i = pl.program_id(0)
+    m_ref[...] = jnp.full_like(m_ref, masked_score)
+    l_ref[...] = jnp.zeros_like(l_ref)
+    acc_ref[...] = jnp.zeros_like(acc_ref)
+    span = k_ref.shape[0]
+    kpos = sq_ref[i] * span + lax.broadcasted_iota(jnp.int32, (1, span), 1)
+    visible = (kpos <= qpos_ref[...]) & (kpos >= qstart_ref[...])
+    online_update(heads, scale, q_ref, k_ref, v_ref, visible, m_ref, l_ref, acc_ref)
+
+
 def attention_kernel(heads, scale, tbl_ref, seq_ref, cnt_ref, q_ref, qpos_ref, qstart_ref,
-                     k_ref, v_ref, o_ref, m_sc, l_sc, acc_sc):
+                     k_ref, v_ref, m_in, l_in, acc_in, o_ref, m_sc, l_sc, acc_sc):
     i = pl.program_id(0)
     j = pl.program_id(1)
 
     @pl.when(j == 0)
     def _():
-        m_sc[...] = jnp.full_like(m_sc, masked_score)
-        l_sc[...] = jnp.zeros_like(l_sc)
-        acc_sc[...] = jnp.zeros_like(acc_sc)
+        m_sc[...] = m_in[...]
+        l_sc[...] = l_in[...]
+        acc_sc[...] = acc_in[...]
 
     @pl.when(j < cnt_ref[i])
     def _():
-        k = k_ref[...]
-        v = v_ref[...]
-        span = k.shape[0]
+        span = k_ref.shape[0]
         kpos = seq_ref[i, j] * span + lax.broadcasted_iota(jnp.int32, (1, span), 1)
         visible = (kpos <= qpos_ref[...]) & (kpos >= qstart_ref[...])
-        for h in range(heads):
-            q = q_ref[:, h * HEAD_DIM:(h + 1) * HEAD_DIM]
-            s = lax.dot_general(q, k, (((1,), (1,)), ((), ())),
-                                preferred_element_type=jnp.float32) * scale
-            m_old = m_sc[h]
-            m_new = jnp.maximum(
-                m_old, jnp.max(jnp.where(visible, s, masked_score), axis=-1, keepdims=True))
-            p = jnp.where(visible, jnp.exp(s - m_new), 0.0)
-            alpha = jnp.exp(m_old - m_new)
-            l_sc[h] = alpha * l_sc[h] + jnp.sum(p, axis=-1, keepdims=True)
-            acc_sc[h] = alpha * acc_sc[h] + jnp.dot(
-                p.astype(jnp.bfloat16), v, preferred_element_type=jnp.float32)
-            m_sc[h] = m_new
+        online_update(heads, scale, q_ref, k_ref, v_ref, visible, m_sc, l_sc, acc_sc)
 
     @pl.when(j == pl.num_programs(1) - 1)
     def _():
@@ -77,12 +93,49 @@
             o_ref[:, h * HEAD_DIM:(h + 1) * HEAD_DIM] = (acc_sc[h] / l_sc[h]).astype(o_ref.dtype)
 
 
-def span_attention(tbl, seq, cnt, queries, qpos, qstart, kv):
+def diagonal_attention(sq, queries, qpos, qstart, local_kv):
     rows, q_cols = queries.shape
     heads = q_cols // HEAD_DIM
     n_q = rows // SPAN
+    kernel = functools.partial(diagonal_kernel, heads, 1.0 / math.sqrt(HEAD_DIM))
+    state = lambda w: pl.BlockSpec((None, heads, SPAN, w), lambda i, s: (i, 0, 0, 0))
+    cost = pl.CostEstimate(
+        flops=4 * n_q * heads * SPAN * SPAN * HEAD_DIM,
+        transcendentals=n_q * heads * SPAN * SPAN,
+        bytes_accessed=2 * rows * q_cols + 4 * rows * HEAD_DIM + 4 * n_q * heads * SPAN * 130,
+    )
+    return pl.pallas_call(
+        kernel,
+        out_shape=(
+            jax.ShapeDtypeStruct((n_q, heads, SPAN, 1), jnp.float32),
+            jax.ShapeDtypeStruct((n_q, heads, SPAN, 1), jnp.float32),
+            jax.ShapeDtypeStruct((n_q, heads, SPAN, HEAD_DIM), jnp.float32),
+        ),
+        grid_spec=pltpu.PrefetchScalarGridSpec(
+            num_scalar_prefetch=1,
+            grid=(n_q,),
+            in_specs=[
+                pl.BlockSpec((SPAN, q_cols), lambda i, s: (i, 0)),
+                pl.BlockSpec((SPAN, 1), lambda i, s: (i, 0)),
+                pl.BlockSpec((SPAN, 1), lambda i, s: (i, 0)),
+                pl.BlockSpec((None, SPAN, HEAD_DIM), lambda i, s: (0, i, 0)),
+                pl.BlockSpec((None, SPAN, HEAD_DIM), lambda i, s: (1, i, 0)),
+            ],
+            out_specs=[state(1), state(1), state(HEAD_DIM)],
+        ),
+        compiler_params=pltpu.CompilerParams(dimension_semantics=("arbitrary",)),
+        cost_estimate=cost,
+    )(sq, queries, qpos, qstart, local_kv, local_kv)
+
+
+def span_attention(tbl, seq, cnt, queries, qpos, qstart, kv, m0, l0, acc0):
+    rows, q_cols = queries.shape
+    heads = q_cols // HEAD_DIM
+    n_q = rows // SPAN
+    slots = tbl.shape[1]
     kernel = functools.partial(attention_kernel, heads, 1.0 / math.sqrt(HEAD_DIM))
-    steps = n_q * KEY_SLOTS
+    steps = n_q * slots
+    state = lambda w: pl.BlockSpec((None, heads, SPAN, w), lambda i, j, t, s, c: (i, 0, 0, 0))
     cost = pl.CostEstimate(
         flops=4 * steps * heads * SPAN * SPAN * HEAD_DIM,
         transcendentals=steps * heads * SPAN * SPAN,
@@ -93,13 +146,14 @@
         out_shape=jax.ShapeDtypeStruct((rows, q_cols), jnp.bfloat16),
         grid_spec=pltpu.PrefetchScalarGridSpec(
             num_scalar_prefetch=3,
-            grid=(n_q, KEY_SLOTS),
+            grid=(n_q, slots),
             in_specs=[
                 pl.BlockSpec((SPAN, q_cols), lambda i, j, t, s, c: (i, 0)),
                 pl.BlockSpec((SPAN, 1), lambda i, j, t, s, c: (i, 0)),
                 pl.BlockSpec((SPAN, 1), lambda i, j, t, s, c: (i, 0)),
                 pl.BlockSpec((None, SPAN, HEAD_DIM), lambda i, j, t, s, c: (0, t[i, j], 0)),
                 pl.BlockSpec((None, SPAN, HEAD_DIM), lambda i, j, t, s, c: (1, t[i, j], 0)),
+                state(1), state(1), state(HEAD_DIM),
             ],
             out_specs=pl.BlockSpec((SPAN, q_cols), lambda i, j, t, s, c: (i, 0)),
             scratch_shapes=[
@@ -110,7 +164,7 @@
         ),
         compiler_params=pltpu.CompilerParams(dimension_semantics=("arbitrary", "arbitrary")),
         cost_estimate=cost,
-    )(tbl, seq, cnt, queries, qpos, qstart, kv, kv)
+    )(tbl, seq, cnt, queries, qpos, qstart, kv, kv, m0, l0, acc0)
 
 
 def key_tables(span_order, doc_ends, query_spans):
@@ -129,11 +183,13 @@
         jnp.where(cand[:, :, None] == span_ids[None, None, :], last_doc[None, None, :], 0), axis=2)
     valid = (cand >= 0) & (cand_last >= q_first[:, None])
     count = jnp.sum(valid.astype(jnp.int32), axis=1)
-    slot = jnp.arange(KEY_SLOTS, dtype=jnp.int32)
-    seq = jnp.minimum(sq[:, None] - count[:, None] + 1 + slot[None, :], sq[:, None])
+    before = count - 1
+    slot = jnp.arange(KEY_SLOTS - 1, dtype=jnp.int32)
+    last = jnp.maximum(sq - 1, 0)
+    seq = jnp.clip(sq[:, None] - before[:, None] + slot[None, :], 0, last[:, None])
     tbl = jnp.sum(jnp.where(seq[:, :, None] == span_ids[None, None, :], inverse[None, None, :], 0),
                   axis=2)
-    return tbl.astype(jnp.int32), seq.astype(jnp.int32), count.astype(jnp.int32)
+    return tbl.astype(jnp.int32), seq.astype(jnp.int32), before.astype(jnp.int32), sq.astype(jnp.int32)
 
 
 def shift_x(value, d, n):
@@ -212,12 +268,12 @@
     query_start = jnp.max(
         jnp.where(doc_ends[None, :] <= places[:, None], doc_ends[None, :], 0), axis=1)
     query_spans = lax.axis_index(CONTEXT) * 2 + jnp.arange(2, dtype=jnp.int32)
-    tbl, seq, cnt = key_tables(span_order, doc_ends, query_spans)
+    tbl, seq, cnt, sq = key_tables(span_order, doc_ends, query_spans)
+    qpos_col = places.astype(jnp.int32)[:, None]
+    qstart_col = query_start.astype(jnp.int32)[:, None]
+    m0, l0, acc0 = diagonal_attention(sq, query_rows, qpos_col, qstart_col, kv_pair)
     attended = span_attention(
-        tbl, seq, cnt, query_rows,
-        places.astype(jnp.int32)[:, None], query_start.astype(jnp.int32)[:, None],
-        gathered,
-    )
+        tbl, seq, cnt, query_rows, qpos_col, qstart_col, gathered, m0, l0, acc0)
     partner_o = lax.ppermute(o_weight, ("yh", "ylo"), NEIGHBOUR)
     half = row_count // 2
     own_rows = lax.dynamic_slice_in_dim(attended, plane * half, half, 0)

time: 253 us -> 249 us (0.984)
  the two profiles are of different devices: /device:TPU:96 before, /device:TPU:8 now
where the time goes in v12:
time: 249 us; the launch traced here: 248 us
  waiting for transfers between devices  138 us (55%)
  Pallas kernels  37.5 us (15%)
  other arithmetic  21.6 us (9%)
  starting transfers between devices  14.5 us (6%)
  between operations  13.8 us (6%)
  matrix products  13.3 us (5%)
  local copies, waits for them, and re-layouts  9.27 us (4%)
    ppermute x1, waiting for transfers between devices, per_device(): partner_half = lax.ppermute(sent_half, ('yh', 'ylo'), NEIGHBOUR)  45.8 us
    ppermute x3, waiting for transfers between devices, shift_x(): return lax.ppermute(value, 'x', [(i, (i + d) % n) for i in range(n)])  40.5 us
    all_gather x1, waiting for transfers between devices, per_device(): gathered = lax.all_gather(kv_pair, CONTEXT, axis=1, tiled=True)  39 us
    pallas_call x1, Pallas kernels, span_attention(): pl.pallas_call(kernel, out_shape=jax.ShapeDtypeStruct((rows, q_cols), jnp...  28.9 us
    pallas_call x1, Pallas kernels, diagonal_attention(): pl.pallas_call(kernel, out_shape=(jax.ShapeDtypeStruct((n_q, heads, SPAN,...  8.62 us
    unnamed x32, local copies, waits for them, and re-layouts  5.78 us
    ppermute x1, waiting for transfers between devices, per_device(): partner_rows = lax.ppermute(other_rows, 'yh', [(0, 1), (1, 0)])  5.76 us
    ppermute x3, starting transfers between devices, shift_x(): return lax.ppermute(value, 'x', [(i, (i + d) % n) for i in range(n)])  5.61 us
  transfers between devices with their start and end apart: 10, of which 7 were waited for; matrix products, arithmetic and copies ran while one was open for 7% of the time, Pallas kernels for 15%

profile of v12, /device:TPU:8, one launch (start us, length us, event | category | flops | bytes accessed | tf_op | source)
XLA Modules:
  0.0 248.4 jit_solution(14642832512060361880)
XLA Ops:
  6.5 1.7 fusion.3
  8.2 2.5 %fusion.5 = bf16[1,128,4096]{2,1,0:T(8,128)(2,1)} fusion(bf16[1,128,4096]{2,1,0:T(8,128)(2,1)} %param.10, f32[4096]{0:T(1024)} %param.11, f32[128]{0:T(128)S(1)} %add_rsqrt_fusion), kind=kLoop, calls=%fused_computation.8 | loop fusion | flops 2097152 | bytes 2114048 | tf_op jit(solution)/shard_map/convert_element_type | solution.py:225
  12.8 1.8 copy-done.1
  14.6 1.6 collective-permute-start
  16.2 45.8 %collective-permute-done = bf16[2048,512]{1,0:T(8,128)(2,1)S(1)} collective-permute-done((bf16[2048,512]{1,0:T(8,128)(2,1)S(1)}, bf16[2048,512]{1,0:T(8,128)(2,1)S(1)}, u32[]{:S(2)}, u32[]{:S(2)}) %collective-permute-start) | collective-permute-done | bytes 2097184 | tf_op jit(solution)/shard_map/ppermute | solution.py:232
  63.2 3.1 %collective-permute-done.1 = bf16[2048,512]{1,0:T(8,128)(2,1)} collective-permute-done((bf16[2048,512]{1,0:T(8,128)(2,1)S(1)}, bf16[2048,512]{1,0:T(8,128)(2,1)}, u32[]{:S(2)}, u32[]{:S(2)}) %collective-permute-start.1) | collective-permute-done | bytes 2097184 | tf_op jit(solution)/shard_map/ppermute | solution.py:234
  66.3 3.5 %fusion.6 = f32[512,512]{1,0:T(8,128)S(1)} fusion(bf16[2048,512]{1,0:T(8,128)(2,1)} %collective-permute-done.1, bf16[1,512,4096]{2,1,0:T(8,128)(2,1)} %all-gather.3.cloned.1.call-done, s32[]{:T(128)S(6)} %select_n.106), kind=kOutput, calls=%fused_computation.9 | convolution fusion | flops 1073741824 | bytes 5242884 | tf_op jit(solution)/shard_map/dot_general | solution.py:254
  75.2 3.5 %collective-permute-start.2 = (bf16[512,512]{1,0:T(8,128)(2,1)}, bf16[512,512]{1,0:T(8,128)(2,1)S(1)}, u32[]{:S(2)}, u32[]{:S(2)}) collective-permute-start(bf16[512,512]{1,0:T(8,128)(2,1)} %pad_maximum_fusion), channel_id=1, source_target_pairs={{0,64},{64,0},{1,65},{65,1},{2,66},{66,2},{3,67},{67,3},{4,68},{68... | collective-permute-start | bytes 1572872 | tf_op jit(solution)/shard_map/ppermute | solution.py:255
  78.7 4.6 %fusion.59 = f32[512,512]{0,1:T(8,128)S(1)} fusion(bf16[512,4096]{1,0:T(8,128)(2,1)} %bitcast.58, bf16[4096,512]{1,0:T(8,128)(2,1)S(1)} %copy-done.2), kind=kOutput, calls=%fused_computation.131 | convolution fusion | flops 2147483648 | bytes 9437184 | tf_op jit(solution)/shard_map/dot_general | solution.py:250
  86.9 4.3 %collective-permute-done.2 = bf16[512,512]{1,0:T(8,128)(2,1)S(1)} collective-permute-done((bf16[512,512]{1,0:T(8,128)(2,1)}, bf16[512,512]{1,0:T(8,128)(2,1)S(1)}, u32[]{:S(2)}, u32[]{:S(2)}) %collective-permute-start.2) | collective-permute-done | bytes 524320 | tf_op jit(solution)/shard_map/ppermute | solution.py:255
  92.4 1.4 collective-permute-start.4
  100.1 8.6 %shard_map.82 = (f32[2,2,512,1]{3,2,1,0:T(8,128)}, f32[2,2,512,1]{3,2,1,0:T(8,128)}, f32[2,2,512,128]{3,2,1,0:T(8,128)}) custom-call(s32[2]{0:T(128)} %copy-done.7, bf16[1024,256]{1,0:T(8,128)(2,1)} %fusion.18.q_ref, s32[1024,1]{1,0:T(8,128)} %fusion.17.qpos_ref, s32[1024,1]{1,0:T(8,128)} %copy.49.qstart_ref, ...), custom_call_target="tpu_custom_call" | custom-call | flops 536870912 | bytes 2113536 | tf_op jit(solution)/shard_map/pallas_call | solution.py:107
  108.7 39.0 %all-gather.5.cloned.1.call-done.k_ref.v_ref = bf16[2,16384,128]{2,1,0:T(8,128)(2,1)} async-done(((bf16[2,1024,128]{2,1,0:T(8,128)(2,1)}), bf16[2,16384,128]{2,1,0:T(8,128)(2,1)}) %all-gather.5.cloned.1.call-update) | async-done | bytes 8388624 | tf_op jit(solution)/shard_map/all_gather | solution.py:263
  147.7 28.9 %shard_map.83 = bf16[1024,256]{1,0:T(8,128)(2,1)} custom-call(s32[2,8]{1,0:T(2,128)} %select_reduce_fusion.3.tbl_ref, s32[2,8]{1,0:T(2,128)} %copy-done.6, s32[2]{0:T(128)} %get-tuple-element.54.cnt_ref, bf16[1024,256]{1,0:T(8,128)(2,1)} %fusion.18.q_ref, s32[1024,1]{1,0:T(8,128)} %fusion.17.qpos_ref, s32[1024,1]{1,0:T(8,128)} %copy.49.qstart_ref, ...), custom_call_target="tpu_custom_call" | custom-call | flops 4294967296 | bytes 5242880 | tf_op jit(solution)/shard_map/pallas_call | solution.py:144
  177.6 2.4 collective-permute-start.3
  180.0 5.8 %collective-permute-done.3 = bf16[512,256]{1,0:T(8,128)(2,1)S(1)} collective-permute-done((bf16[512,256]{1,0:T(8,128)(2,1)S(1)}, bf16[512,256]{1,0:T(8,128)(2,1)S(1)}, u32[]{:S(2)}, u32[]{:S(2)}) %collective-permute-start.3) | collective-permute-done | bytes 262176 | tf_op jit(solution)/shard_map/ppermute | solution.py:281
  185.8 3.9 %convolution_convert_fusion = bf16[512,4096]{1,0:T(8,128)(2,1)S(1)} fusion(bf16[256,4096]{1,0:T(8,128)(2,1)} %collective-permute-done.4, bf16[256,4096]{1,0:T(8,128)(2,1)S(1)} %copy-done.11, bf16[512,256]{1,0:T(8,128)(2,1)S(1)} %collective-permute-done.3, bf16[512,256]{1,0:T(8,128)(2,1)S(1)} %get-tuple-element.42), kind=kOutput, calls=%fused_computation | convolution fusion | flops 2159017984 | bytes 8912896 | tf_op jit(solution)/shard_map/dot_general | solution.py:282
  190.0 1.6 copy-done
  191.7 1.5 collective-permute-start.5
  193.2 2.7 %collective-permute-start.6 = (bf16[128,4096]{1,0:T(8,128)(2,1)S(1)}, bf16[128,4096]{1,0:T(8,128)(2,1)}, u32[]{:S(2)}, u32[]{:S(2)}) collective-permute-start(bf16[128,4096]{1,0:T(8,128)(2,1)S(1)} %get-tuple-element.33), channel_id=1, source_target_pairs={{0,32},{16,48},{32,0},{48,16},{1,33},{17,49},{33,1},{49,17},{2,34}... | collective-permute-start | bytes 3145736 | tf_op jit(solution)/shard_map/ppermute | solution.py:196
  195.8 1.5 collective-permute-start.7
  197.3 20.9 %collective-permute-done.5 = bf16[128,4096]{1,0:T(8,128)(2,1)} collective-permute-done((bf16[128,4096]{1,0:T(8,128)(2,1)S(1)}, bf16[128,4096]{1,0:T(8,128)(2,1)}, u32[]{:S(2)}, u32[]{:S(2)}) %collective-permute-start.5) | collective-permute-done | bytes 1048608 | tf_op jit(solution)/shard_map/ppermute | solution.py:196
  218.2 19.6 %collective-permute-done.6 = bf16[128,4096]{1,0:T(8,128)(2,1)} collective-permute-done((bf16[128,4096]{1,0:T(8,128)(2,1)S(1)}, bf16[128,4096]{1,0:T(8,128)(2,1)}, u32[]{:S(2)}, u32[]{:S(2)}) %collective-permute-start.6) | collective-permute-done | bytes 1048608 | tf_op jit(solution)/shard_map/ppermute | solution.py:196
  237.8 3.8 %fusion.15 = bf16[1,128,4096]{2,1,0:T(8,128)(2,1)} fusion(bf16[128,4096]{1,0:T(8,128)(2,1)} %collective-permute-done.7, bf16[128,4096]{1,0:T(8,128)(2,1)} %collective-permute-done.6, bf16[128,4096]{1,0:T(8,128)(2,1)} %collective-permute-done.5, bf16[4,128,4096]{2,1,0:T(8,128)(2,1)} %bitcast.48, s32[]{:T(128)S(6)} %select_n.129, pred[]{:T(512)S(6)} %and.74), kind=kLoop, calls=%fused_computation.21 | loop fusion | flops 4718592 | bytes 5242885 | tf_op jit(solution)/shard_map/reshape | solution.py:288
  (93 shorter events, 20.8 us)
Async XLA Ops:
  6.5 4.3 %copy-start.3 = (bf16[4096,256]{1,0:T(8,128)(2,1)S(1)}, bf16[4096,256]{1,0:T(8,128)(2,1)}, u32[]{:S(2)}) copy-start(bf16[4096,256]{1,0:T(8,128)(2,1)} %param.12) | copy-start | bytes 6291460
  6.5 55.4 %all-gather.3.cloned.1.call-start = ((), (), s32[]{:S(2)}) async-start(), calls=%async_computation | async-start | bytes 5242880 | tf_op jit(solution)/shard_map/all_gather | solution.py:231
  10.8 136.9 %all-gather.5.cloned.1.call-start = ((), (), s32[]{:S(2)}) async-start(), calls=%async_computation.1 | async-start | bytes 8912896 | tf_op jit(solution)/shard_map/all_gather | solution.py:263
  10.8 1.2 copy-start.4
  10.8 1.5 copy-start.5
  12.6 2.0 copy-start.1
  12.6 49.4 %copy-start.9 = (s32[32]{0:T(128)S(1)}, s32[32]{0:T(128)}, u32[]{:S(2)}) copy-start(s32[32]{0:T(128)} %param.17) | copy-start | bytes 388
  14.6 47.4 %collective-permute-start = (bf16[2048,512]{1,0:T(8,128)(2,1)S(1)}, bf16[2048,512]{1,0:T(8,128)(2,1)S(1)}, u32[]{:S(2)}, u32[]{:S(2)}) collective-permute-start(bf16[2048,512]{1,0:T(8,128)(2,1)S(1)} %constant_dynamic-slice_fusion.2), channel_id=1, source_target_pairs={{0,66},{66,0},{2,64},{64,2},{1,67},{67,1},{3,65},{65,3},{4,70},{70... | collective-permute-start | bytes 6291464 | tf_op jit(solution)/shard_map/ppermute | solution.py:232
  62.0 4.3 %collective-permute-start.1 = (bf16[2048,512]{1,0:T(8,128)(2,1)S(1)}, bf16[2048,512]{1,0:T(8,128)(2,1)}, u32[]{:S(2)}, u32[]{:S(2)}) collective-permute-start(bf16[2048,512]{1,0:T(8,128)(2,1)S(1)} %collective-permute-done), channel_id=1, source_target_pairs={{0,1},{1,0},{2,3},{3,2},{4,5},{5,4},{6,7},{7,6},{8,9},{9,8},{10,11... | collective-permute-start | bytes 6291464 | tf_op jit(solution)/shard_map/ppermute | solution.py:234
  63.2 6.5 %copy-start.10 = (bf16[1,512,4096]{2,1,0:T(8,128)(2,1)S(1)}, bf16[1,512,4096]{2,1,0:T(8,128)(2,1)}, u32[]{:S(2)}) copy-start(bf16[1,512,4096]{2,1,0:T(8,128)(2,1)} %all-gather.3.cloned.1.call-done) | copy-start | bytes 12582916
  71.4 7.3 %copy-start.2 = (bf16[4096,512]{1,0:T(8,128)(2,1)S(1)}, bf16[4096,512]{1,0:T(8,128)(2,1)}, u32[]{:S(2)}) copy-start(bf16[4096,512]{1,0:T(8,128)(2,1)} %copy-done.1) | copy-start | bytes 12582916
  75.2 15.9 %collective-permute-start.2 = (bf16[512,512]{1,0:T(8,128)(2,1)}, bf16[512,512]{1,0:T(8,128)(2,1)S(1)}, u32[]{:S(2)}, u32[]{:S(2)}) collective-permute-start(bf16[512,512]{1,0:T(8,128)(2,1)} %pad_maximum_fusion), channel_id=1, source_target_pairs={{0,64},{64,0},{1,65},{65,1},{2,66},{66,2},{3,67},{67,3},{4,68},{68... | collective-permute-start | bytes 1572872 | tf_op jit(solution)/shard_map/ppermute | solution.py:255
  91.4 2.6 %copy-start.8 = (s32[16]{0:T(128)S(1)}, s32[16]{0:T(128)}, u32[]{:S(2)}) copy-start(s32[16]{0:T(128)} %param.16) | copy-start | bytes 196
  92.4 87.7 %collective-permute-start.4 = (bf16[256,4096]{1,0:T(8,128)(2,1)}, bf16[256,4096]{1,0:T(8,128)(2,1)}, u32[]{:S(2)}, u32[]{:S(2)}) collective-permute-start(bf16[256,4096]{1,0:T(8,128)(2,1)} %param.15), channel_id=1, source_target_pairs={{0,66},{66,0},{2,64},{64,2},{1,67},{67,1},{3,65},{65,3},{4,70},{70... | collective-permute-start | bytes 6291464 | tf_op jit(solution)/shard_map/ppermute | solution.py:277
  95.6 4.5 %copy-start.7 = (s32[2]{0:T(128)}, s32[2]{0:T(128)S(1)}, u32[]{:S(2)}) copy-start(s32[2]{0:T(128)S(1)} %fusion.53.sq_ref) | copy-start | bytes 28
  97.4 11.3 %copy-start.6 = (s32[2,8]{1,0:T(2,128)}, s32[2,8]{1,0:T(2,128)S(1)}, u32[]{:S(2)}) copy-start(s32[2,8]{1,0:T(2,128)S(1)} %maximum_minimum_fusion.seq_ref) | copy-start | bytes 196
  147.7 38.1 %copy-start.11 = (bf16[256,4096]{1,0:T(8,128)(2,1)S(1)}, bf16[256,4096]{1,0:T(8,128)(2,1)}, u32[]{:S(2)}) copy-start(bf16[256,4096]{1,0:T(8,128)(2,1)} %param.15) | copy-start | bytes 6291460
  177.6 8.2 %collective-permute-start.3 = (bf16[512,256]{1,0:T(8,128)(2,1)S(1)}, bf16[512,256]{1,0:T(8,128)(2,1)S(1)}, u32[]{:S(2)}, u32[]{:S(2)}) collective-permute-start(bf16[512,256]{1,0:T(8,128)(2,1)S(1)} %get-tuple-element.43), channel_id=1, source_target_pairs={{0,64},{64,0},{1,65},{65,1},{2,66},{66,2},{3,67},{67,3},{4,68},{68... | collective-permute-start | bytes 786440 | tf_op jit(solution)/shard_map/ppermute | solution.py:281
  189.7 1.9 copy-start
  191.7 26.5 %collective-permute-start.5 = (bf16[128,4096]{1,0:T(8,128)(2,1)S(1)}, bf16[128,4096]{1,0:T(8,128)(2,1)}, u32[]{:S(2)}, u32[]{:S(2)}) collective-permute-start(bf16[128,4096]{1,0:T(8,128)(2,1)S(1)} %get-tuple-element.31), channel_id=1, source_target_pairs={{0,16},{16,32},{32,48},{48,0},{1,17},{17,33},{33,49},{49,1},{2,18}... | collective-permute-start | bytes 3145736 | tf_op jit(solution)/shard_map/ppermute | solution.py:196
  193.2 44.6 %collective-permute-start.6 = (bf16[128,4096]{1,0:T(8,128)(2,1)S(1)}, bf16[128,4096]{1,0:T(8,128)(2,1)}, u32[]{:S(2)}, u32[]{:S(2)}) collective-permute-start(bf16[128,4096]{1,0:T(8,128)(2,1)S(1)} %get-tuple-element.33), channel_id=1, source_target_pairs={{0,32},{16,48},{32,0},{48,16},{1,33},{17,49},{33,1},{49,17},{2,34}... | collective-permute-start | bytes 3145736 | tf_op jit(solution)/shard_map/ppermute | solution.py:196
  195.8 42.0 %collective-permute-start.7 = (bf16[128,4096]{1,0:T(8,128)(2,1)S(1)}, bf16[128,4096]{1,0:T(8,128)(2,1)}, u32[]{:S(2)}, u32[]{:S(2)}) collective-permute-start(bf16[128,4096]{1,0:T(8,128)(2,1)S(1)} %get-tuple-element.32), channel_id=1, source_target_pairs={{0,48},{16,0},{32,16},{48,32},{1,49},{17,1},{33,17},{49,33},{2,50}... | collective-permute-start | bytes 3145736 | tf_op jit(solution)/shard_map/ppermute | solution.py:196
Sparse Core Ops, SparseCore 0:
  10.9 50.5 all-gather.2
  92.5 55.1 all-gather.4

commit v13 on v12

--- a/solution.py
+++ b/solution.py
@@ -47,9 +47,13 @@
         s = lax.dot_general(q, k, (((1,), (1,)), ((), ())),
                             preferred_element_type=jnp.float32) * scale
         m_old = m_sc[h]
-        m_new = jnp.maximum(
-            m_old, jnp.max(jnp.where(visible, s, masked_score), axis=-1, keepdims=True))
-        p = jnp.where(visible, jnp.exp(s - m_new), 0.0)
+        if visible is None:
+            m_new = jnp.maximum(m_old, jnp.max(s, axis=-1, keepdims=True))
+            p = jnp.exp(s - m_new)
+        else:
+            m_new = jnp.maximum(
+                m_old, jnp.max(jnp.where(visible, s, masked_score), axis=-1, keepdims=True))
+            p = jnp.where(visible, jnp.exp(s - m_new), 0.0)
         alpha = jnp.exp(m_old - m_new)
         l_sc[h] = alpha * l_sc[h] + jnp.sum(p, axis=-1, keepdims=True)
         acc_sc[h] = alpha * acc_sc[h] + jnp.dot(
@@ -69,7 +73,7 @@
     online_update(heads, scale, q_ref, k_ref, v_ref, visible, m_ref, l_ref, acc_ref)
 
 
-def attention_kernel(heads, scale, tbl_ref, seq_ref, cnt_ref, q_ref, qpos_ref, qstart_ref,
+def attention_kernel(heads, scale, tbl_ref, seq_ref, cnt_ref, full_ref, q_ref, qpos_ref, qstart_ref,
                      k_ref, v_ref, m_in, l_in, acc_in, o_ref, m_sc, l_sc, acc_sc):
     i = pl.program_id(0)
     j = pl.program_id(1)
@@ -80,7 +84,14 @@
         l_sc[...] = l_in[...]
         acc_sc[...] = acc_in[...]
 
-    @pl.when(j < cnt_ref[i])
+    live = j < cnt_ref[i]
+    full = full_ref[i, j] == 1
+
+    @pl.when(live & full)
+    def _():
+        online_update(heads, scale, q_ref, k_ref, v_ref, None, m_sc, l_sc, acc_sc)
+
+    @pl.when(live & jnp.logical_not(full))
     def _():
         span = k_ref.shape[0]
         kpos = seq_ref[i, j] * span + lax.broadcasted_iota(jnp.int32, (1, span), 1)
@@ -128,14 +139,14 @@
     )(sq, queries, qpos, qstart, local_kv, local_kv)
 
 
-def span_attention(tbl, seq, cnt, queries, qpos, qstart, kv, m0, l0, acc0):
+def span_attention(tbl, seq, cnt, full, queries, qpos, qstart, kv, m0, l0, acc0):
     rows, q_cols = queries.shape
     heads = q_cols // HEAD_DIM
     n_q = rows // SPAN
     slots = tbl.shape[1]
     kernel = functools.partial(attention_kernel, heads, 1.0 / math.sqrt(HEAD_DIM))
     steps = n_q * slots
-    state = lambda w: pl.BlockSpec((None, heads, SPAN, w), lambda i, j, t, s, c: (i, 0, 0, 0))
+    state = lambda w: pl.BlockSpec((None, heads, SPAN, w), lambda i, j, t, s, c, f: (i, 0, 0, 0))
     cost = pl.CostEstimate(
         flops=4 * steps * heads * SPAN * SPAN * HEAD_DIM,
         transcendentals=steps * heads * SPAN * SPAN,
@@ -145,17 +156,17 @@
         kernel,
         out_shape=jax.ShapeDtypeStruct((rows, q_cols), jnp.bfloat16),
         grid_spec=pltpu.PrefetchScalarGridSpec(
-            num_scalar_prefetch=3,
+            num_scalar_prefetch=4,
             grid=(n_q, slots),
             in_specs=[
-                pl.BlockSpec((SPAN, q_cols), lambda i, j, t, s, c: (i, 0)),
-                pl.BlockSpec((SPAN, 1), lambda i, j, t, s, c: (i, 0)),
-                pl.BlockSpec((SPAN, 1), lambda i, j, t, s, c: (i, 0)),
-                pl.BlockSpec((None, SPAN, HEAD_DIM), lambda i, j, t, s, c: (0, t[i, j], 0)),
-                pl.BlockSpec((None, SPAN, HEAD_DIM), lambda i, j, t, s, c: (1, t[i, j], 0)),
+                pl.BlockSpec((SPAN, q_cols), lambda i, j, t, s, c, f: (i, 0)),
+                pl.BlockSpec((SPAN, 1), lambda i, j, t, s, c, f: (i, 0)),
+                pl.BlockSpec((SPAN, 1), lambda i, j, t, s, c, f: (i, 0)),
+                pl.BlockSpec((None, SPAN, HEAD_DIM), lambda i, j, t, s, c, f: (0, t[i, j], 0)),
+                pl.BlockSpec((None, SPAN, HEAD_DIM), lambda i, j, t, s, c, f: (1, t[i, j], 0)),
                 state(1), state(1), state(HEAD_DIM),
             ],
-            out_specs=pl.BlockSpec((SPAN, q_cols), lambda i, j, t, s, c: (i, 0)),
+            out_specs=pl.BlockSpec((SPAN, q_cols), lambda i, j, t, s, c, f: (i, 0)),
             scratch_shapes=[
                 pltpu.VMEM((heads, SPAN, 1), jnp.float32),
                 pltpu.VMEM((heads, SPAN, 1), jnp.float32),
@@ -164,7 +175,7 @@
         ),
         compiler_params=pltpu.CompilerParams(dimension_semantics=("arbitrary", "arbitrary")),
         cost_estimate=cost,
-    )(tbl, seq, cnt, queries, qpos, qstart, kv, kv, m0, l0, acc0)
+    )(tbl, seq, cnt, full, queries, qpos, qstart, kv, kv, m0, l0, acc0)
 
 
 def key_tables(span_order, doc_ends, query_spans):
@@ -189,7 +200,11 @@
     seq = jnp.clip(sq[:, None] - before[:, None] + slot[None, :], 0, last[:, None])
     tbl = jnp.sum(jnp.where(seq[:, :, None] == span_ids[None, None, :], inverse[None, None, :], 0),
                   axis=2)
-    return tbl.astype(jnp.int32), seq.astype(jnp.int32), before.astype(jnp.int32), sq.astype(jnp.int32)
+    last_start = jnp.max(
+        jnp.where(doc_ends[None, :] <= (sq * SPAN + SPAN - 1)[:, None], doc_ends[None, :], 0), axis=1)
+    full = (seq < sq[:, None]) & (seq * SPAN >= last_start[:, None])
+    return (tbl.astype(jnp.int32), seq.astype(jnp.int32), before.astype(jnp.int32),
+            sq.astype(jnp.int32), full.astype(jnp.int32))
 
 
 def shift_x(value, d, n):
@@ -268,12 +283,12 @@
     query_start = jnp.max(
         jnp.where(doc_ends[None, :] <= places[:, None], doc_ends[None, :], 0), axis=1)
     query_spans = lax.axis_index(CONTEXT) * 2 + jnp.arange(2, dtype=jnp.int32)
-    tbl, seq, cnt, sq = key_tables(span_order, doc_ends, query_spans)
+    tbl, seq, cnt, sq, full = key_tables(span_order, doc_ends, query_spans)
     qpos_col = places.astype(jnp.int32)[:, None]
     qstart_col = query_start.astype(jnp.int32)[:, None]
     m0, l0, acc0 = diagonal_attention(sq, query_rows, qpos_col, qstart_col, kv_pair)
     attended = span_attention(
-        tbl, seq, cnt, query_rows, qpos_col, qstart_col, gathered, m0, l0, acc0)
+        tbl, seq, cnt, full, query_rows, qpos_col, qstart_col, gathered, m0, l0, acc0)
     partner_o = lax.ppermute(o_weight, ("yh", "ylo"), NEIGHBOUR)
     half = row_count // 2
     own_rows = lax.dynamic_slice_in_dim(attended, plane * half, half, 0)

time: 249 us -> 252 us (1.012); the launches traced: 248 us -> 247 us
  waiting for transfers between devices: 138 us -> 130 us
  Pallas kernels: 37.5 us -> 43.1 us
    ppermute x3, waiting for transfers between devices: 40.5 us -> 33.5 us  [shift_x(): return lax.ppermute(value, 'x', [(i, (i + d) % n) for i in range(n)])]
    pallas_call x1, Pallas kernels: 28.9 us -> 34.5 us  [span_attention(): pl.pallas_call(kernel, out_shape=jax.ShapeDtypeStruct((rows, q_cols), jnp...]
  transfers between devices with their start and end apart: 10 -> 10, of which waited for: 7 -> 7; matrix products, arithmetic and copies ran while one was open for 7% -> 7% of each run, Pallas kernels for 15% -> 17%
where the time goes in v13:
time: 252 us; the launch traced here: 247 us
  waiting for transfers between devices  130 us (52%)
  Pallas kernels  43.1 us (17%)
  other arithmetic  22.4 us (9%)
  starting transfers between devices  14.6 us (6%)
  between operations  13.8 us (5%)
  matrix products  13.3 us (5%)
  local copies, waits for them, and re-layouts  9.26 us (4%)
    ppermute x1, waiting for transfers between devices, per_device(): partner_half = lax.ppermute(sent_half, ('yh', 'ylo'), NEIGHBOUR)  45.8 us
    all_gather x1, waiting for transfers between devices, per_device(): gathered = lax.all_gather(kv_pair, CONTEXT, axis=1, tiled=True)  37.9 us
    pallas_call x1, Pallas kernels, span_attention(): pl.pallas_call(kernel, out_shape=jax.ShapeDtypeStruct((rows, q_cols), jnp...  34.5 us
    ppermute x3, waiting for transfers between devices, shift_x(): return lax.ppermute(value, 'x', [(i, (i + d) % n) for i in range(n)])  33.5 us
    pallas_call x1, Pallas kernels, diagonal_attention(): pl.pallas_call(kernel, out_shape=(jax.ShapeDtypeStruct((n_q, heads, SPAN,...  8.66 us
    unnamed x32, local copies, waits for them, and re-layouts  5.76 us
    ppermute x1, waiting for transfers between devices, per_device(): partner_rows = lax.ppermute(other_rows, 'yh', [(0, 1), (1, 0)])  5.75 us
    ppermute x3, starting transfers between devices, shift_x(): return lax.ppermute(value, 'x', [(i, (i + d) % n) for i in range(n)])  5.61 us
  transfers between devices with their start and end apart: 10, of which 7 were waited for; matrix products, arithmetic and copies ran while one was open for 7% of the time, Pallas kernels for 17%

profile of v13, /device:TPU:8, one launch (start us, length us, event | category | flops | bytes accessed | tf_op | source)
XLA Modules:
  0.0 246.8 jit_solution(6485914644700369848)
XLA Ops:
  6.5 1.7 fusion.3
  8.2 2.5 %fusion.5 = bf16[1,128,4096]{2,1,0:T(8,128)(2,1)} fusion(bf16[1,128,4096]{2,1,0:T(8,128)(2,1)} %param.10, f32[4096]{0:T(1024)} %param.11, f32[128]{0:T(128)S(1)} %add_rsqrt_fusion), kind=kLoop, calls=%fused_computation.8 | loop fusion | flops 2097152 | bytes 2114048 | tf_op jit(solution)/shard_map/convert_element_type | solution.py:240
  12.8 1.8 copy-done.1
  14.6 1.6 collective-permute-start
  16.2 45.8 %collective-permute-done = bf16[2048,512]{1,0:T(8,128)(2,1)S(1)} collective-permute-done((bf16[2048,512]{1,0:T(8,128)(2,1)S(1)}, bf16[2048,512]{1,0:T(8,128)(2,1)S(1)}, u32[]{:S(2)}, u32[]{:S(2)}) %collective-permute-start) | collective-permute-done | bytes 2097184 | tf_op jit(solution)/shard_map/ppermute | solution.py:247
  63.2 3.1 %collective-permute-done.1 = bf16[2048,512]{1,0:T(8,128)(2,1)} collective-permute-done((bf16[2048,512]{1,0:T(8,128)(2,1)S(1)}, bf16[2048,512]{1,0:T(8,128)(2,1)}, u32[]{:S(2)}, u32[]{:S(2)}) %collective-permute-start.1) | collective-permute-done | bytes 2097184 | tf_op jit(solution)/shard_map/ppermute | solution.py:249
  66.3 3.5 %fusion.6 = f32[512,512]{1,0:T(8,128)S(1)} fusion(bf16[2048,512]{1,0:T(8,128)(2,1)} %collective-permute-done.1, bf16[1,512,4096]{2,1,0:T(8,128)(2,1)} %all-gather.3.cloned.1.call-done, s32[]{:T(128)S(6)} %select_n.111), kind=kOutput, calls=%fused_computation.9 | convolution fusion | flops 1073741824 | bytes 5242884 | tf_op jit(solution)/shard_map/dot_general | solution.py:269
  75.2 3.5 %collective-permute-start.2 = (bf16[512,512]{1,0:T(8,128)(2,1)}, bf16[512,512]{1,0:T(8,128)(2,1)S(1)}, u32[]{:S(2)}, u32[]{:S(2)}) collective-permute-start(bf16[512,512]{1,0:T(8,128)(2,1)} %pad_maximum_fusion), channel_id=1, source_target_pairs={{0,64},{64,0},{1,65},{65,1},{2,66},{66,2},{3,67},{67,3},{4,68},{68... | collective-permute-start | bytes 1572872 | tf_op jit(solution)/shard_map/ppermute | solution.py:270
  78.7 4.6 %fusion.60 = f32[512,512]{0,1:T(8,128)S(1)} fusion(bf16[512,4096]{1,0:T(8,128)(2,1)} %bitcast.58, bf16[4096,512]{1,0:T(8,128)(2,1)S(1)} %copy-done.2), kind=kOutput, calls=%fused_computation.135 | convolution fusion | flops 2147483648 | bytes 9437184 | tf_op jit(solution)/shard_map/dot_general | solution.py:265
  86.9 4.3 %collective-permute-done.2 = bf16[512,512]{1,0:T(8,128)(2,1)S(1)} collective-permute-done((bf16[512,512]{1,0:T(8,128)(2,1)}, bf16[512,512]{1,0:T(8,128)(2,1)S(1)}, u32[]{:S(2)}, u32[]{:S(2)}) %collective-permute-start.2) | collective-permute-done | bytes 524320 | tf_op jit(solution)/shard_map/ppermute | solution.py:270
  92.4 1.6 collective-permute-start.4
  101.1 8.7 %shard_map.82 = (f32[2,2,512,1]{3,2,1,0:T(8,128)}, f32[2,2,512,1]{3,2,1,0:T(8,128)}, f32[2,2,512,128]{3,2,1,0:T(8,128)}) custom-call(s32[2]{0:T(128)} %copy-done.6, bf16[1024,256]{1,0:T(8,128)(2,1)} %fusion.18.q_ref, s32[1024,1]{1,0:T(8,128)} %fusion.17.qpos_ref, s32[1024,1]{1,0:T(8,128)} %copy.49.qstart_ref, ...), custom_call_target="tpu_custom_call" | custom-call | flops 536870912 | bytes 2113536 | tf_op jit(solution)/shard_map/pallas_call | solution.py:118
  109.7 37.9 %all-gather.5.cloned.1.call-done.k_ref.v_ref = bf16[2,16384,128]{2,1,0:T(8,128)(2,1)} async-done(((bf16[2,1024,128]{2,1,0:T(8,128)(2,1)}), bf16[2,16384,128]{2,1,0:T(8,128)(2,1)}) %all-gather.5.cloned.1.call-update) | async-done | bytes 8388624 | tf_op jit(solution)/shard_map/all_gather | solution.py:278
  147.7 34.5 %shard_map.83 = bf16[1024,256]{1,0:T(8,128)(2,1)} custom-call(s32[2,8]{1,0:T(2,128)} %select_reduce_fusion.3.tbl_ref, s32[2,8]{1,0:T(2,128)} %copy-done.7, s32[2]{0:T(128)} %get-tuple-element.56.cnt_ref, s32[2,8]{1,0:T(2,128)} %and_convert_fusion.full_ref, bf16[1024,256]{1,0:T(8,128)(2,1)} %fusion.18.q_ref, s32[1024,1]{1,0:T(8,128)} %fusion.17.qpos_ref, ...), custom_call_target="tpu_custom_call" | custom-call | flops 4294967296 | bytes 5242880 | tf_op jit(solution)/shard_map/pallas_call | solution.py:155
  183.2 2.2 collective-permute-start.3
  185.4 5.8 %collective-permute-done.3 = bf16[512,256]{1,0:T(8,128)(2,1)S(1)} collective-permute-done((bf16[512,256]{1,0:T(8,128)(2,1)S(1)}, bf16[512,256]{1,0:T(8,128)(2,1)S(1)}, u32[]{:S(2)}, u32[]{:S(2)}) %collective-permute-start.3) | collective-permute-done | bytes 262176 | tf_op jit(solution)/shard_map/ppermute | solution.py:296
  191.1 3.9 %convolution_convert_fusion = bf16[512,4096]{1,0:T(8,128)(2,1)S(1)} fusion(bf16[256,4096]{1,0:T(8,128)(2,1)} %collective-permute-done.4, bf16[256,4096]{1,0:T(8,128)(2,1)S(1)} %copy-done.11, bf16[512,256]{1,0:T(8,128)(2,1)S(1)} %collective-permute-done.3, bf16[512,256]{1,0:T(8,128)(2,1)S(1)} %get-tuple-element.42), kind=kOutput, calls=%fused_computation | convolution fusion | flops 2159017984 | bytes 8912896 | tf_op jit(solution)/shard_map/dot_general | solution.py:297
  195.4 1.6 copy-done
  197.0 1.4 collective-permute-start.5
  198.5 2.7 %collective-permute-start.6 = (bf16[128,4096]{1,0:T(8,128)(2,1)S(1)}, bf16[128,4096]{1,0:T(8,128)(2,1)}, u32[]{:S(2)}, u32[]{:S(2)}) collective-permute-start(bf16[128,4096]{1,0:T(8,128)(2,1)S(1)} %get-tuple-element.33), channel_id=1, source_target_pairs={{0,32},{16,48},{32,0},{48,16},{1,33},{17,49},{33,1},{49,17},{2,34}... | collective-permute-start | bytes 3145736 | tf_op jit(solution)/shard_map/ppermute | solution.py:211
  201.2 1.5 collective-permute-start.7
  202.6 21.7 %collective-permute-done.5 = bf16[128,4096]{1,0:T(8,128)(2,1)} collective-permute-done((bf16[128,4096]{1,0:T(8,128)(2,1)S(1)}, bf16[128,4096]{1,0:T(8,128)(2,1)}, u32[]{:S(2)}, u32[]{:S(2)}) %collective-permute-start.5) | collective-permute-done | bytes 1048608 | tf_op jit(solution)/shard_map/ppermute | solution.py:211
  224.3 11.8 %collective-permute-done.6 = bf16[128,4096]{1,0:T(8,128)(2,1)} collective-permute-done((bf16[128,4096]{1,0:T(8,128)(2,1)S(1)}, bf16[128,4096]{1,0:T(8,128)(2,1)}, u32[]{:S(2)}, u32[]{:S(2)}) %collective-permute-start.6) | collective-permute-done | bytes 1048608 | tf_op jit(solution)/shard_map/ppermute | solution.py:211
  236.1 3.8 %fusion.15 = bf16[1,128,4096]{2,1,0:T(8,128)(2,1)} fusion(bf16[128,4096]{1,0:T(8,128)(2,1)} %collective-permute-done.7, bf16[128,4096]{1,0:T(8,128)(2,1)} %collective-permute-done.6, bf16[128,4096]{1,0:T(8,128)(2,1)} %collective-permute-done.5, bf16[4,128,4096]{2,1,0:T(8,128)(2,1)} %bitcast.48, s32[]{:T(128)S(6)} %select_n.134, pred[]{:T(512)S(6)} %and.78), kind=kLoop, calls=%fused_computation.21 | loop fusion | flops 4718592 | bytes 5242885 | tf_op jit(solution)/shard_map/reshape | solution.py:303
  (95 shorter events, 21.6 us)
Async XLA Ops:
  6.5 4.3 %copy-start.3 = (bf16[4096,256]{1,0:T(8,128)(2,1)S(1)}, bf16[4096,256]{1,0:T(8,128)(2,1)}, u32[]{:S(2)}) copy-start(bf16[4096,256]{1,0:T(8,128)(2,1)} %param.12) | copy-start | bytes 6291460
  6.5 55.4 %all-gather.3.cloned.1.call-start = ((), (), s32[]{:S(2)}) async-start(), calls=%async_computation | async-start | bytes 5242880 | tf_op jit(solution)/shard_map/all_gather | solution.py:246
  10.8 136.9 %all-gather.5.cloned.1.call-start = ((), (), s32[]{:S(2)}) async-start(), calls=%async_computation.1 | async-start | bytes 8912896 | tf_op jit(solution)/shard_map/all_gather | solution.py:278
  10.8 1.2 copy-start.4
  10.8 1.5 copy-start.5
  12.6 2.0 copy-start.1
  12.6 49.4 %copy-start.9 = (s32[32]{0:T(128)S(1)}, s32[32]{0:T(128)}, u32[]{:S(2)}) copy-start(s32[32]{0:T(128)} %param.17) | copy-start | bytes 388
  14.6 47.4 %collective-permute-start = (bf16[2048,512]{1,0:T(8,128)(2,1)S(1)}, bf16[2048,512]{1,0:T(8,128)(2,1)S(1)}, u32[]{:S(2)}, u32[]{:S(2)}) collective-permute-start(bf16[2048,512]{1,0:T(8,128)(2,1)S(1)} %constant_dynamic-slice_fusion.2), channel_id=1, source_target_pairs={{0,66},{66,0},{2,64},{64,2},{1,67},{67,1},{3,65},{65,3},{4,70},{70... | collective-permute-start | bytes 6291464 | tf_op jit(solution)/shard_map/ppermute | solution.py:247
  62.0 4.3 %collective-permute-start.1 = (bf16[2048,512]{1,0:T(8,128)(2,1)S(1)}, bf16[2048,512]{1,0:T(8,128)(2,1)}, u32[]{:S(2)}, u32[]{:S(2)}) collective-permute-start(bf16[2048,512]{1,0:T(8,128)(2,1)S(1)} %collective-permute-done), channel_id=1, source_target_pairs={{0,1},{1,0},{2,3},{3,2},{4,5},{5,4},{6,7},{7,6},{8,9},{9,8},{10,11... | collective-permute-start | bytes 6291464 | tf_op jit(solution)/shard_map/ppermute | solution.py:249
  63.2 6.5 %copy-start.10 = (bf16[1,512,4096]{2,1,0:T(8,128)(2,1)S(1)}, bf16[1,512,4096]{2,1,0:T(8,128)(2,1)}, u32[]{:S(2)}) copy-start(bf16[1,512,4096]{2,1,0:T(8,128)(2,1)} %all-gather.3.cloned.1.call-done) | copy-start | bytes 12582916
  71.4 7.3 %copy-start.2 = (bf16[4096,512]{1,0:T(8,128)(2,1)S(1)}, bf16[4096,512]{1,0:T(8,128)(2,1)}, u32[]{:S(2)}) copy-start(bf16[4096,512]{1,0:T(8,128)(2,1)} %copy-done.1) | copy-start | bytes 12582916
  75.2 15.9 %collective-permute-start.2 = (bf16[512,512]{1,0:T(8,128)(2,1)}, bf16[512,512]{1,0:T(8,128)(2,1)S(1)}, u32[]{:S(2)}, u32[]{:S(2)}) collective-permute-start(bf16[512,512]{1,0:T(8,128)(2,1)} %pad_maximum_fusion), channel_id=1, source_target_pairs={{0,64},{64,0},{1,65},{65,1},{2,66},{66,2},{3,67},{67,3},{4,68},{68... | collective-permute-start | bytes 1572872 | tf_op jit(solution)/shard_map/ppermute | solution.py:270
  91.4 2.8 %copy-start.8 = (s32[16]{0:T(128)S(1)}, s32[16]{0:T(128)}, u32[]{:S(2)}) copy-start(s32[16]{0:T(128)} %param.16) | copy-start | bytes 196
  92.4 93.0 %collective-permute-start.4 = (bf16[256,4096]{1,0:T(8,128)(2,1)}, bf16[256,4096]{1,0:T(8,128)(2,1)}, u32[]{:S(2)}, u32[]{:S(2)}) collective-permute-start(bf16[256,4096]{1,0:T(8,128)(2,1)} %param.15), channel_id=1, source_target_pairs={{0,66},{66,0},{2,64},{64,2},{1,67},{67,1},{3,65},{65,3},{4,70},{70... | collective-permute-start | bytes 6291464 | tf_op jit(solution)/shard_map/ppermute | solution.py:292
  95.8 5.3 %copy-start.6 = (s32[2]{0:T(128)}, s32[2]{0:T(128)S(1)}, u32[]{:S(2)}) copy-start(s32[2]{0:T(128)S(1)} %fusion.53.sq_ref) | copy-start | bytes 28
  97.8 11.9 %copy-start.7 = (s32[2,8]{1,0:T(2,128)}, s32[2,8]{1,0:T(2,128)S(1)}, u32[]{:S(2)}) copy-start(s32[2,8]{1,0:T(2,128)S(1)} %maximum_minimum_fusion.seq_ref) | copy-start | bytes 196
  147.7 43.5 %copy-start.11 = (bf16[256,4096]{1,0:T(8,128)(2,1)S(1)}, bf16[256,4096]{1,0:T(8,128)(2,1)}, u32[]{:S(2)}) copy-start(bf16[256,4096]{1,0:T(8,128)(2,1)} %param.15) | copy-start | bytes 6291460
  183.2 8.0 %collective-permute-start.3 = (bf16[512,256]{1,0:T(8,128)(2,1)S(1)}, bf16[512,256]{1,0:T(8,128)(2,1)S(1)}, u32[]{:S(2)}, u32[]{:S(2)}) collective-permute-start(bf16[512,256]{1,0:T(8,128)(2,1)S(1)} %get-tuple-element.43), channel_id=1, source_target_pairs={{0,64},{64,0},{1,65},{65,1},{2,66},{66,2},{3,67},{67,3},{4,68},{68... | collective-permute-start | bytes 786440 | tf_op jit(solution)/shard_map/ppermute | solution.py:296
  195.1 1.9 copy-start
  197.0 27.3 %collective-permute-start.5 = (bf16[128,4096]{1,0:T(8,128)(2,1)S(1)}, bf16[128,4096]{1,0:T(8,128)(2,1)}, u32[]{:S(2)}, u32[]{:S(2)}) collective-permute-start(bf16[128,4096]{1,0:T(8,128)(2,1)S(1)} %get-tuple-element.31), channel_id=1, source_target_pairs={{0,16},{16,32},{32,48},{48,0},{1,17},{17,33},{33,49},{49,1},{2,18}... | collective-permute-start | bytes 3145736 | tf_op jit(solution)/shard_map/ppermute | solution.py:211
  198.5 37.7 %collective-permute-start.6 = (bf16[128,4096]{1,0:T(8,128)(2,1)S(1)}, bf16[128,4096]{1,0:T(8,128)(2,1)}, u32[]{:S(2)}, u32[]{:S(2)}) collective-permute-start(bf16[128,4096]{1,0:T(8,128)(2,1)S(1)} %get-tuple-element.33), channel_id=1, source_target_pairs={{0,32},{16,48},{32,0},{48,16},{1,33},{17,49},{33,1},{49,17},{2,34}... | collective-permute-start | bytes 3145736 | tf_op jit(solution)/shard_map/ppermute | solution.py:211
  201.2 35.0 %collective-permute-start.7 = (bf16[128,4096]{1,0:T(8,128)(2,1)S(1)}, bf16[128,4096]{1,0:T(8,128)(2,1)}, u32[]{:S(2)}, u32[]{:S(2)}) collective-permute-start(bf16[128,4096]{1,0:T(8,128)(2,1)S(1)} %get-tuple-element.32), channel_id=1, source_target_pairs={{0,48},{16,0},{32,16},{48,32},{1,49},{17,1},{33,17},{49,33},{2,50}... | collective-permute-start | bytes 3145736 | tf_op jit(solution)/shard_map/ppermute | solution.py:211
Sparse Core Ops, SparseCore 0:
  10.9 50.5 all-gather.2
  92.5 55.1 all-gather.4
